TPU v7x, 32 devices: a whole 2x2x4 slice. The times are simulated.
32 devices in a mesh: dp: 8 (over z, y), own: 4 (over x, core).
Axes of the slice: x: 2, y: 2, z: 4, core: 2. Of those that a mesh axis runs over, the one named last changes fastest.
Arguments:
- acts_kv: bfloat16 [1024, 2560], P('dp', 'own'), may hold values from -6 to 6
- grads_kv: bfloat16 [1024, 1024], P('dp', 'own'), may hold values from -6 to 6
- acts_up: bfloat16 [1024, 2560], P('dp', 'own'), may hold values from -6 to 6
- grads_up: bfloat16 [1024, 3072], P('dp', 'own'), may hold values from -6 to 6
- prev_a_kv: float32 [4, 640, 640], P('own'), as said below
- prev_g_kv: float32 [4, 256, 256], P('own'), as said below
- prev_a_up: float32 [4, 640, 640], P('own'), as said below
- prev_g_up: float32 [4, 768, 768], P('own'), as said below
- owners: int32 [2, 4], replicated, may hold values from 0 to 7, as said below
- damping: float32 [4], replicated, may hold values from 0.05 to 0.5
- init_scale: float32 [4, 4], replicated, may hold values from 0.4 to 0.8
- weights_kv: float32 [2560, 1024], P('own', 'dp'), may hold values from -0.75 to 0.75
- weights_up: float32 [2560, 3072], P('own', 'dp'), may hold values from -0.75 to 0.75
- step_size: float32 [], replicated, may hold values from 0.2 to 0.5
Outputs:
- new_kv: float32 [2560, 1024], P('own', 'dp')
- new_up: float32 [2560, 3072], P('own', 'dp')
Inputs may be any that keep to these rules, and one draw needn't show every extreme that they name: `owners`: row 0 names for each factor the dp index that inverts it: one index is named by two factors, the others by one, and 0 and 7 are always named. Row 1 refreshes both factors of one of the two linears and leaves at least one factor of the other unrefreshed. `prev_a_kv`: every block is symmetric and positive definite. `prev_g_kv`: every block is symmetric and positive definite. `prev_a_up`: every block is symmetric and positive definite. `prev_g_up`: every block is symmetric and positive definite.
All inputs are finite; a program needn't handle non-finite values.
Results may differ from a plain program's by a relative error of at most 0.0021.
Values may be sent and summed in bfloat16 or wider, within the bound.
No kernel may reach another device: no remote copies, remote signals or barrier semaphores. Data moves between devices by JAX's collectives and lax.ppermute only.
A program may use at most 128 MiB of HBM per device.

v0:
```python
import jax
import jax.numpy as jnp
from jax import lax
from jax.sharding import PartitionSpec as P

D = 2560
OUT_KV = 1024
OUT_UP = 3072
NF = 4
NS_STEPS = 2


def spread(value, axis, root):
    mine = lax.axis_index(axis) == root
    return lax.psum(jnp.where(mine, value, jnp.zeros_like(value)), axis)


def matrix_product(left_side, right_side):
    return jnp.dot(
        left_side, right_side, preferred_element_type=jnp.float32, precision=lax.Precision.HIGHEST
    )


def outer_sum(values):
    return lax.dot_general(
        values, values, (((0,), (0,)), ((), ())), preferred_element_type=jnp.float32
    )


def blend_factor(previous, summed, fresh, damping_value, identity):
    return jnp.where(fresh == 1, 0.5 * previous + 0.5 * summed, previous) + damping_value * identity


def newton_schulz(damped, scale_value):
    block_width = damped.shape[0]
    identity = jnp.eye(block_width, dtype=jnp.float32)
    frobenius = jnp.sqrt(jnp.sum(damped * damped))
    iterate = scale_value / frobenius * identity
    for repeat in range(NS_STEPS):
        iterate = 2.0 * iterate - matrix_product(matrix_product(damped, iterate), iterate)
    return iterate.astype(jnp.bfloat16)


def apply_output_inverse(grad_low, blocks):
    block_count, block_width, unused = blocks.shape
    shaped = grad_low.reshape(grad_low.shape[0], block_count, block_width)
    product = jnp.einsum("rjb,jbc->rjc", shaped, blocks, preferred_element_type=jnp.float32)
    return product.reshape(grad_low.shape).astype(jnp.bfloat16)


def shards(
    acts_kv,
    grads_kv,
    acts_up,
    grads_up,
    prev_a_kv,
    prev_g_kv,
    prev_a_up,
    prev_g_up,
    owners,
    damping,
    init_scale,
    weights_kv,
    weights_up,
    step_size,
):
    dp_count = lax.axis_size("dp")
    dp_index = lax.axis_index("dp")
    own_index = lax.axis_index("own")
    total_tokens = acts_kv.shape[0] * dp_count
    full_kv, full_up = (
        lax.all_gather(grads_kv, "own", axis=1, tiled=True),
        lax.all_gather(grads_up, "own", axis=1, tiled=True),
    )
    column_block = acts_kv
    gradient_kv = (
        lax.psum_scatter(
            lax.dot_general(
                column_block, full_kv, (((0,), (0,)), ((), ())), preferred_element_type=jnp.float32
            ),
            "dp",
            scatter_dimension=0,
            tiled=True,
        )
        / total_tokens
    )
    column_block = acts_up
    gradient_up = (
        lax.psum_scatter(
            lax.dot_general(
                column_block, full_up, (((0,), (0,)), ((), ())), preferred_element_type=jnp.float32
            ),
            "dp",
            scatter_dimension=0,
            tiled=True,
        )
        / total_tokens
    )
    partials = (outer_sum(acts_kv), outer_sum(grads_kv), outer_sum(acts_up), outer_sum(grads_up))
    previous = (prev_a_kv[0], prev_g_kv[0], prev_a_up[0], prev_g_up[0])
    scales = lax.dynamic_index_in_dim(init_scale, own_index, 1, keepdims=False)
    summed_rows = (
        lax.psum_scatter(partials[0], "dp", scatter_dimension=0, tiled=True),
        lax.psum_scatter(partials[1], "dp", scatter_dimension=0, tiled=True),
        lax.psum_scatter(partials[2], "dp", scatter_dimension=0, tiled=True),
        lax.psum_scatter(partials[3], "dp", scatter_dimension=0, tiled=True),
    )
    summed = (
        lax.all_gather(summed_rows[0], "dp", axis=0, tiled=True),
        lax.all_gather(summed_rows[1], "dp", axis=0, tiled=True),
        lax.all_gather(summed_rows[2], "dp", axis=0, tiled=True),
        lax.all_gather(summed_rows[3], "dp", axis=0, tiled=True),
    )
    inverses = []
    for factor in range(NF):
        owner_index = owners[0, factor]
        identity = jnp.eye(previous[factor].shape[0], dtype=jnp.float32)
        damped = blend_factor(
            previous[factor],
            summed[factor] / total_tokens,
            owners[1, factor],
            damping[factor],
            identity,
        )
        local_inverse = lax.cond(
            dp_index == owner_index,
            lambda matrix: newton_schulz(matrix, scales[factor]),
            lambda matrix: jnp.zeros(matrix.shape, jnp.bfloat16),
            damped,
        )
        inverses.append(spread(local_inverse, "dp", owner_index))
    blocks_kv, blocks_up = (
        lax.all_gather(inverses[1][None], "own", axis=0, tiled=True),
        lax.all_gather(inverses[3][None], "own", axis=0, tiled=True),
    )
    low_kv = gradient_kv.astype(jnp.bfloat16)
    low_up = gradient_up.astype(jnp.bfloat16)
    right_kv = apply_output_inverse(low_kv, blocks_kv)
    right_up = apply_output_inverse(low_up, blocks_up)
    arrived = (
        lax.all_to_all(right_kv, "dp", split_axis=1, concat_axis=0, tiled=True),
        lax.all_to_all(low_kv, "dp", split_axis=1, concat_axis=0, tiled=True),
        lax.all_to_all(right_up, "dp", split_axis=1, concat_axis=0, tiled=True),
        lax.all_to_all(low_up, "dp", split_axis=1, concat_axis=0, tiled=True),
    )
    precond_kv = jnp.dot(inverses[0], arrived[0], preferred_element_type=jnp.float32)
    precond_up = jnp.dot(inverses[2], arrived[2], preferred_element_type=jnp.float32)
    term_kv = jnp.sum(precond_kv * arrived[1].astype(jnp.float32))
    term_up = jnp.sum(precond_up * arrived[3].astype(jnp.float32))
    totals = lax.psum((term_kv, term_up), ("dp", "own"))
    new_kv = weights_kv - step_size * jnp.sqrt(D * OUT_KV / totals[0]) * precond_kv
    new_up = weights_up - step_size * jnp.sqrt(D * OUT_UP / totals[1]) * precond_up
    return (new_kv, new_up)


def solution(mesh):
    return jax.shard_map(
        shards,
        mesh=mesh,
        in_specs=(
            P("dp", "own"),
            P("dp", "own"),
            P("dp", "own"),
            P("dp", "own"),
            P("own", None, None),
            P("own", None, None),
            P("own", None, None),
            P("own", None, None),
            P(),
            P(),
            P(),
            P("own", "dp"),
            P("own", "dp"),
            P(),
        ),
        out_specs=(P("own", "dp"), P("own", "dp")),
        check_vma=False,
    )
```

profile of v0, /device:TPU:0, one launch (start us, length us, event | category | flops | bytes accessed | tf_op | source)
XLA Modules:
  0.0 931.1 jit_solution(16209690147066611134)
XLA Ops:
  7.2 2.6 fusion.74
  15.4 64.0 %reduce-scatter.7.cloned.1.call-done = f32[80,640]{1,0:T(8,128)} async-done(((f32[640,640]{1,0:T(8,128)}), f32[80,640]{1,0:T(8,128)}) %reduce-scatter.7.cloned.1.call-update) | async-done | bytes 204816 | tf_op jit(solution)/shard_map/reduce_scatter | solution.py:103
  79.5 68.1 %reduce-scatter.13.cloned.1.call-done = f32[80,640]{1,0:T(8,128)} async-done(((f32[640,640]{1,0:T(8,128)}), f32[80,640]{1,0:T(8,128)}) %reduce-scatter.13.cloned.1.call-update) | async-done | bytes 204816 | tf_op jit(solution)/shard_map/reduce_scatter | solution.py:105
  147.7 71.4 %reduce-scatter.15.cloned.1.call-done = f32[96,768]{1,0:T(8,128)} async-done(((f32[768,768]{1,0:T(8,128)}), f32[96,768]{1,0:T(8,128)}) %reduce-scatter.15.cloned.1.call-update) | async-done | bytes 294928 | tf_op jit(solution)/shard_map/reduce_scatter | solution.py:106
  223.3 59.8 %reduce-scatter.9.cloned.1.call-done = f32[32,256]{1,0:T(8,128)} async-done(((f32[256,256]{1,0:T(8,128)}), f32[32,256]{1,0:T(8,128)}) %reduce-scatter.9.cloned.1.call-update) | async-done | bytes 32784 | tf_op jit(solution)/shard_map/reduce_scatter | solution.py:104
  283.1 31.2 %all_gather.25 = f32[256,256]{1,0:T(8,128)S(1)} all-gather(f32[32,256]{1,0:T(8,128)} %reduce-scatter.9.cloned.1.call-done), channel_id=1, replica_groups=mesh['dp'=8,'own'=4] {'dp'}, dimensions={0}, use_global_device_ids=true | all-gather | bytes 294912 | tf_op jit(solution)/shard_map/all_gather | solution.py:110
  315.1 14.2 %all-gather.5.cloned.1.call-done = f32[640,640]{1,0:T(8,128)} async-done(((f32[80,640]{1,0:T(8,128)}), f32[640,640]{1,0:T(8,128)}) %all-gather.5.cloned.1.call-update) | async-done | bytes 1638416 | tf_op jit(solution)/shard_map/all_gather | solution.py:109
  332.0 29.4 %conditional.4 = (bf16[640,640]{1,0:T(8,128)(2,1)S(1)}) conditional(s32[]{:T(128)} %convert_element_type.80, () %tuple.44, (f32[4]{0:T(128)S(1)}, s32[2,4]{1,0:T(2,128)S(1)}, f32[1,640,640]{2,1,0:T(8,128)}, f32[640,640]{1,0:T(8,128)S(1)}, f32[640,640]{1,0:T(8,128)}, /*index=5*/f32[640,640]{1,0:T(8,128)}, f32[4]{0:T(128)S(1)}, ...), branch_computations={%region_1.0_spmd, %region_2.0_spmd} | conditional | flops 12590694400 | bytes 25804862 | solution.py:125
  333.7 4.2 multiply_reduce_fusion
  338.6 4.6 fusion.2
  343.2 4.7 fusion.4
  347.9 8.2 fusion.70
  356.2 5.0 subtract_convert_fusion
  361.5 13.5 %all-gather.7.cloned.1.call-done = f32[640,640]{1,0:T(8,128)} async-done(((f32[80,640]{1,0:T(8,128)}), f32[640,640]{1,0:T(8,128)}) %all-gather.7.cloned.1.call-update) | async-done | bytes 1638416 | tf_op jit(solution)/shard_map/all_gather | solution.py:111
  374.9 9.3 conditional.6
  386.7 41.4 %all-gather.9.cloned.1.call-done = f32[768,768]{1,0:T(8,128)} async-done(((f32[96,768]{1,0:T(8,128)}), f32[768,768]{1,0:T(8,128)}) %all-gather.9.cloned.1.call-update) | async-done | bytes 2359312 | tf_op jit(solution)/shard_map/all_gather | solution.py:112
  431.3 5.4 conditional.7
  438.0 5.8 all_gather.27
  446.7 8.7 all_gather.31
  455.4 4.3 fusion.79
  459.8 136.7 %all-reduce.4.cloned.1.call-done = (bf16[640,640]{1,0:T(8,128)(2,1)}, bf16[1,256,256]{2,1,0:T(8,128)(2,1)}, bf16[640,640]{1,0:T(8,128)(2,1)}, bf16[1,768,768]{2,1,0:T(8,128)(2,1)}) async-done(((bf16[640,640]{1,0:T(8,128)(2,1)}, bf16[1,256,256]{2,1,0:T(8,128)(2,1)}, bf16[640,640]{1,0:T(8,128)(2,1)}, bf16[1,768,768]{2,1,0:T(8,128)(2,1)}), (bf16[640,640]{1,0:T(8,128)(2,1)}, bf16[1,256,256]{2,1,0:T(8,128)(2,1)}, ...) | async-done | bytes 2949136 | tf_op jit(solution)/shard_map/psum | solution.py:15
  596.5 73.3 %reduce-scatter.11.cloned.1.call-done = f32[80,1024]{1,0:T(8,128)} async-done(((f32[640,1024]{1,0:T(8,128)}), f32[80,1024]{1,0:T(8,128)}) %reduce-scatter.11.cloned.1.call-update) | async-done | bytes 327696 | tf_op jit(solution)/shard_map/reduce_scatter | solution.py:77
  671.5 3.5 all-to-all-start.1
  676.0 7.1 all_gather.26
  684.2 6.0 all-to-all-start
  690.2 126.9 %reduce-scatter.17.cloned.1.call-done = f32[80,3072]{1,0:T(8,128)} async-done(((f32[640,3072]{1,0:T(8,128)}), f32[80,3072]{1,0:T(8,128)}) %reduce-scatter.17.cloned.1.call-update) | async-done | bytes 983056 | tf_op jit(solution)/shard_map/reduce_scatter | solution.py:89
  819.2 3.7 all-to-all-start.3
  822.9 32.4 %all-gather.11.cloned.1.call-done = bf16[4,768,768]{2,1,0:T(8,128)(2,1)} async-done(((bf16[1,768,768]{2,1,0:T(8,128)(2,1)}), bf16[4,768,768]{2,1,0:T(8,128)(2,1)}) %all-gather.11.cloned.1.call-update) | async-done | bytes 4718608 | tf_op jit(solution)/shard_map/all_gather | solution.py:134
  855.4 3.2 fusion.57
  859.9 5.5 all-to-all-start.2
  867.0 12.5 %all-to-all-done.2 = bf16[80,8,384]{2,0,1:T(8,128)(2,1)S(1)} async-done(((bf16[80,8,384]{2,0,1:T(8,128)(2,1)}), bf16[80,8,384]{2,0,1:T(8,128)(2,1)S(1)}, u32[]{:S(2)}, u32[]{:S(2)}) %all-to-all-start.2) | async-done | bytes 491552 | tf_op jit(solution)/shard_map/all_to_all | solution.py:143
  882.1 38.8 %all-reduce = (f32[]{:T(128)}, f32[]{:T(128)}) all-reduce(f32[]{:T(128)} %get-tuple-element.298, f32[]{:T(128)} %get-tuple-element.300), channel_id=1, replica_groups=mesh['dp'=8,'own'=4] {'dp','own'}, use_global_device_ids=true, to_apply=%region_12.13 | all-reduce | flops 2 | bytes 16 | tf_op jit(solution)/shard_map/psum | solution.py:150
  (94 shorter events, 33.8 us)
Async XLA Ops:
  7.2 2.8 copy-start
  7.2 72.2 %reduce-scatter.7.cloned.1.call-start = ((), (), s32[]{:S(2)}) async-start(), calls=%async_computation.10 | async-start | bytes 1843200 | tf_op jit(solution)/shard_map/reduce_scatter | solution.py:103
  9.9 1.7 copy-start.2
  9.9 137.7 %reduce-scatter.13.cloned.1.call-start = ((), (), s32[]{:S(2)}) async-start(), calls=%async_computation.14 | async-start | bytes 1843200 | tf_op jit(solution)/shard_map/reduce_scatter | solution.py:105
  11.6 207.5 %reduce-scatter.15.cloned.1.call-start = ((), (), s32[]{:S(2)}) async-start(), calls=%async_computation.16 | async-start | bytes 2654208 | tf_op jit(solution)/shard_map/reduce_scatter | solution.py:106
  13.5 0.8 copy-start.9
  13.5 205.6 %copy-start.13 = (s32[2,4]{1,0:T(2,128)S(1)}, s32[2,4]{1,0:T(2,128)}, u32[]{:S(2)}) copy-start(s32[2,4]{1,0:T(2,128)} %param.30) | copy-start | bytes 100
  13.5 208.7 %copy-start.14 = (f32[4,4]{1,0:T(4,128)S(1)}, f32[4,4]{1,0:T(4,128)}, u32[]{:S(2)}) copy-start(f32[4,4]{1,0:T(4,128)} %param.32) | copy-start | bytes 196
  13.6 300.8 %copy-start.11 = (f32[1,256,256]{2,1,0:T(8,128)S(1)}, f32[1,256,256]{2,1,0:T(8,128)}, u32[]{:S(2)}) copy-start(f32[1,256,256]{2,1,0:T(8,128)} %param.27) | copy-start | bytes 786436
  13.6 300.8 %copy-start.15 = (f32[4]{0:T(128)S(1)}, f32[4]{0:T(128)}, u32[]{:S(2)}) copy-start(f32[4]{0:T(128)} %param.31) | copy-start | bytes 52
  13.6 269.5 %reduce-scatter.9.cloned.1.call-start = ((), (), s32[]{:S(2)}) async-start(), calls=%async_computation.12 | async-start | bytes 294912 | tf_op jit(solution)/shard_map/reduce_scatter | solution.py:104
  15.3 313.9 %all-gather.5.cloned.1.call-start = ((), (), s32[]{:S(2)}) async-start(), calls=%async_computation.11 | async-start | bytes 1843200 | tf_op jit(solution)/shard_map/all_gather | solution.py:109
  79.4 295.5 %all-gather.7.cloned.1.call-start = ((), (), s32[]{:S(2)}) async-start(), calls=%async_computation.15 | async-start | bytes 1843200 | tf_op jit(solution)/shard_map/all_gather | solution.py:111
  147.6 280.5 %all-gather.9.cloned.1.call-start = ((), (), s32[]{:S(2)}) async-start(), calls=%async_computation.17 | async-start | bytes 2654208 | tf_op jit(solution)/shard_map/all_gather | solution.py:112
  219.1 377.3 %all-reduce.4.cloned.1.call-start = ((), (), s32[]{:S(2)}) async-start(), calls=%async_computation.20 | async-start | bytes 5898240 | tf_op jit(solution)/shard_map/psum | solution.py:15
  361.5 13.5 %copy-start.1 = (bf16[640,640]{1,0:T(8,128)(2,1)}, bf16[640,640]{1,0:T(8,128)(2,1)S(1)}, u32[]{:S(2)}) copy-start(bf16[640,640]{1,0:T(8,128)(2,1)S(1)} %get-tuple-element.308) | copy-start | bytes 2457604
  437.9 5.9 copy-start.4
  438.0 231.9 %reduce-scatter.11.cloned.1.call-start = ((), (), s32[]{:S(2)}) async-start(), calls=%async_computation.13 | async-start | bytes 2949120 | tf_op jit(solution)/shard_map/reduce_scatter | solution.py:77
  445.8 0.9 copy-start.3
  445.8 371.3 %reduce-scatter.17.cloned.1.call-start = ((), (), s32[]{:S(2)}) async-start(), calls=%async_computation.19 | async-start | bytes 8847360 | tf_op jit(solution)/shard_map/reduce_scatter | solution.py:89
  459.7 395.6 %all-gather.11.cloned.1.call-start = ((), (), s32[]{:S(2)}) async-start(), calls=%async_computation.18 | async-start | bytes 5898240 | tf_op jit(solution)/shard_map/all_gather | solution.py:134
  596.5 79.5 %copy-start.12 = (bf16[1,256,256]{2,1,0:T(8,128)(2,1)S(1)}, bf16[1,256,256]{2,1,0:T(8,128)(2,1)}, u32[]{:S(2)}) copy-start(bf16[1,256,256]{2,1,0:T(8,128)(2,1)} %get-tuple-element.283) | copy-start | bytes 393220
  671.5 12.7 %all-to-all-start.1 = ((bf16[80,8,128]{2,0,1:T(8,128)(2,1)}), bf16[80,8,128]{2,0,1:T(8,128)(2,1)S(1)}, u32[]{:S(2)}, u32[]{:S(2)}) async-start(bf16[80,8,128]{2,0,1:T(8,128)(2,1)} %copy_bitcast_fusion.1), calls=%async_computation.4 | async-start | bytes 327680 | tf_op jit(solution)/shard_map/all_to_all | solution.py:142
  684.2 135.0 %all-to-all-start = ((bf16[80,8,128]{2,0,1:T(8,128)(2,1)}), bf16[80,8,128]{2,0,1:T(8,128)(2,1)S(1)}, u32[]{:S(2)}, u32[]{:S(2)}) async-start(bf16[80,8,128]{2,0,1:T(8,128)(2,1)} %copy.34), calls=%async_computation.3 | async-start | bytes 327680 | tf_op jit(solution)/shard_map/all_to_all | solution.py:141
  819.2 39.4 %copy-start.7 = (bf16[80,8,128]{2,0,1:T(8,128)(2,1)}, bf16[80,8,128]{2,0,1:T(8,128)(2,1)S(1)}, u32[]{:S(2)}) copy-start(bf16[80,8,128]{2,0,1:T(8,128)(2,1)S(1)} %all-to-all-done) | copy-start | bytes 491524
  819.2 40.6 %all-to-all-start.3 = ((bf16[80,8,384]{2,0,1:T(8,128)(2,1)}), bf16[80,8,384]{2,0,1:T(8,128)(2,1)S(1)}, u32[]{:S(2)}, u32[]{:S(2)}) async-start(bf16[80,8,384]{2,0,1:T(8,128)(2,1)} %bitcast.140), calls=%async_computation.9 | async-start | bytes 983040 | tf_op jit(solution)/shard_map/all_to_all | solution.py:144
  858.9 7.2 copy-start.6
  859.0 7.0 copy-start.8
  859.9 19.7 %all-to-all-start.2 = ((bf16[80,8,384]{2,0,1:T(8,128)(2,1)}), bf16[80,8,384]{2,0,1:T(8,128)(2,1)S(1)}, u32[]{:S(2)}, u32[]{:S(2)}) async-start(bf16[80,8,384]{2,0,1:T(8,128)(2,1)} %copy.38), calls=%async_computation.8 | async-start | bytes 983040 | tf_op jit(solution)/shard_map/all_to_all | solution.py:143
  867.0 55.3 %copy-start.5 = (f32[640,384]{1,0:T(8,128)S(1)}, f32[640,384]{1,0:T(8,128)}, u32[]{:S(2)}) copy-start(f32[640,384]{1,0:T(8,128)} %param.34) | copy-start | bytes 2949124
  882.1 41.3 %copy-start.10 = (f32[640,128]{1,0:T(8,128)S(1)}, f32[640,128]{1,0:T(8,128)}, u32[]{:S(2)}) copy-start(f32[640,128]{1,0:T(8,128)} %param.33) | copy-start | bytes 983044
Sparse Core Ops, SparseCore 0:
  11.5 67.9 reduce-scatter.6
  83.2 64.3 reduce-scatter.12
  151.1 67.9 reduce-scatter.14
  222.9 60.2 reduce-scatter.8
  285.2 44.0 all-gather.4
  331.3 43.5 all-gather.6
  377.1 50.9 all-gather.8
  438.1 158.3 all-reduce.3
  600.4 69.3 reduce-scatter.10
  673.8 143.3 reduce-scatter.16
  818.8 36.5 all-gather.10
where the time goes:
time: 936 us; the launch traced here: 931 us
  waiting for transfers between devices  714 us (76%)
  blocking collectives  91.5 us (10%)
  matrix products  42.8 us (5%)
  starting transfers between devices  19.2 us (2%)
  between operations  19.1 us (2%)
  loops' own time  16.7 us (2%)
  other arithmetic  15.2 us (2%)
  local copies, waits for them, and re-layouts  12 us (1%)
    psum x1, waiting for transfers between devices, spread(): return lax.psum(jnp.where(mine, value, jnp.zeros_like(value)), axis)  137 us
    reduce_scatter x1, waiting for transfers between devices, shards(): lax.psum_scatter(lax.dot_general(column_block, full_up, (((0,), (0,)), ((...  127 us
    reduce_scatter x1, waiting for transfers between devices, shards(): lax.psum_scatter(lax.dot_general(column_block, full_kv, (((0,), (0,)), ((...  73.3 us
    reduce_scatter x1, waiting for transfers between devices, shards(): lax.psum_scatter(partials[3], 'dp', scatter_dimension=0, tiled=True)  71.4 us
    reduce_scatter x1, waiting for transfers between devices, shards(): lax.psum_scatter(partials[2], 'dp', scatter_dimension=0, tiled=True)  68.1 us
    reduce_scatter x1, waiting for transfers between devices, shards(): lax.psum_scatter(partials[0], 'dp', scatter_dimension=0, tiled=True)  64 us
    reduce_scatter x1, waiting for transfers between devices, shards(): lax.psum_scatter(partials[1], 'dp', scatter_dimension=0, tiled=True)  59.8 us
    all_gather x1, waiting for transfers between devices, shards(): lax.all_gather(summed_rows[3], 'dp', axis=0, tiled=True)  41.4 us
  transfers between devices with their start and end apart: 15, of which 12 were waited for; matrix products, arithmetic and copies ran while one was open for 6% of the time, Pallas kernels for 0%

commit v1 on v0

v1 whole, which is shorter than its diff:
```python
import jax
import jax.numpy as jnp
from jax import lax
from jax.sharding import PartitionSpec as P

BF = jnp.bfloat16
F32 = jnp.float32


def mm(a, b, dims=((1,), (0,))):
    return lax.dot_general(a, b, (dims, ((), ())), preferred_element_type=F32)


def damp(previous, stat, fresh, lam):
    n = previous.shape[0]
    eye = (lax.broadcasted_iota(jnp.int32, (n, n), 0) == lax.broadcasted_iota(jnp.int32, (n, n), 1))
    mixed = jnp.where(fresh == 1, 0.5 * previous + 0.5 * stat, previous)
    return mixed + jnp.where(eye, lam, 0.0)


def normalised(damped, scale):
    coef = scale / jnp.sqrt(jnp.sum(damped * damped))
    return coef, coef * damped


def inverse_columns(damped, scale, start, width):
    n = damped.shape[0]
    coef, y_full = normalised(damped, scale)
    y_low = y_full.astype(BF)
    y_cols = lax.dynamic_slice_in_dim(y_full, start, width, 1)
    square = mm(y_low, y_cols.astype(BF))
    cubic = mm(y_low, (4.0 * y_cols - square).astype(BF))
    rows = lax.broadcasted_iota(jnp.int32, (n, width), 0)
    cols = lax.broadcasted_iota(jnp.int32, (n, width), 1) + start
    out = coef * (jnp.where(rows == cols, 4.0, 0.0) - 6.0 * y_cols + cubic)
    return out.astype(BF)


def apply_inverse(damped, scale, right):
    coef, y_full = normalised(damped, scale)
    y_low = y_full.astype(BF)
    wide = right.astype(F32)
    inner = 4.0 * wide - mm(y_low, right)
    inner = 6.0 * wide - mm(y_low, inner.astype(BF))
    return coef * (4.0 * wide - mm(y_low, inner.astype(BF)))


def gather_fast(acts, grads, prev_low):
    dp, own = lax.axis_index("dp"), lax.axis_index("own")
    z, x = dp // 2, own // 2
    rows = acts.shape[0]
    half = rows // 2
    z_swap = lambda k: [(d, d ^ (2 * k)) for d in range(8)]
    y_swap = [(d, d ^ 1) for d in range(8)]
    x_swap = [(o, o ^ 2) for o in range(4)]
    both = ("dp", "own")
    at = lambda d, o: d * 4 + o

    keep = lax.dynamic_slice_in_dim(grads, half * x, half, 0)
    give = lax.dynamic_slice_in_dim(grads, half * (1 - x), half, 0)
    take = lax.ppermute(give, "own", x_swap)
    mine = jnp.concatenate(
        [lax.dynamic_slice_in_dim(acts, half * x, half, 0), lax.dynamic_slice_in_dim(acts, half * (1 - x), half, 0)], 0
    )
    a = [mine] + [lax.ppermute(mine, "dp", z_swap(k)) for k in (1, 2, 3)]
    pieces = []
    for k in range(4):
        target = jnp.bitwise_xor(z, k)
        piece = jnp.where(target // 2 == x, keep, take)
        if k:
            pairs = [
                (at(d, o), at(d ^ (2 * k), o))
                for d in range(8)
                for o in range(4)
                if (o & 1) == (((d // 2) ^ k) & 1)
            ]
            piece = lax.ppermute(piece, both, pairs)
        pieces.append(piece)
    sender = [(d, o) for d in range(8) for o in range(4) if (o & 1) == ((d // 2) & 1)]
    near = jnp.concatenate(pieces, 0)
    far = lax.ppermute(near, both, [(at(d, o), at(d ^ 1, o)) for d, o in sender])
    row = jnp.concatenate([near, far], 0)
    across = lax.ppermute(row, both, [(at(d, o), at(d, o ^ 2)) for d, o in sender])
    block = jnp.concatenate([row, across], 0)
    copy = lax.ppermute(block, both, [(at(d, o), at(d, o ^ 1)) for d, o in sender])
    is_sender = (own & 1) == (z & 1)
    block = jnp.where(is_sender, block, copy)
    a = a + [lax.ppermute(v, "dp", y_swap) for v in a]
    acts_all = jnp.concatenate([v[:half] for v in a] + [v[half:] for v in a], 0)

    prevs = []
    for p in prev_low:
        q = lax.ppermute(p, both, [(at(d, d // 2), at(d, (d // 2) ^ 2)) for d in range(8)])
        p = jnp.where(own == z, p, q)
        q = lax.ppermute(
            p, both, [(at(d, o), at(d, o ^ 1)) for d in range(8) for o in range(4) if (o & 1) == ((d // 2) & 1)]
        )
        prevs.append(jnp.where(is_sender, p, q))
    return acts_all, block, prevs


def gather_any(acts, grads, prev_low, block_index, dp_count, own_count):
    rows, cols = grads.shape
    acts_all = lax.all_gather(acts, "dp", axis=0, tiled=True)
    split = lax.all_to_all(grads.reshape(own_count, rows // own_count, cols), "own", 0, 0, tiled=True)
    wanted = jnp.repeat(split, dp_count // own_count, axis=0)
    pieces = lax.all_to_all(wanted, "dp", 0, 0, tiled=True)
    block = lax.all_gather(pieces, "own", axis=1, tiled=True).reshape(rows * dp_count, cols)
    prevs = [
        lax.dynamic_index_in_dim(lax.all_gather(p[None], "own", axis=0, tiled=True), block_index, 0, keepdims=False)
        for p in prev_low
    ]
    return acts_all, block, prevs


def shards(acts_kv, grads_kv, acts_up, grads_up, prev_a_kv, prev_g_kv, prev_a_up, prev_g_up, owners, damping,
           init_scale, weights_kv, weights_up, step_size):
    dp_count, own_count = lax.axis_size("dp"), lax.axis_size("own")
    dp, own = lax.axis_index("dp"), lax.axis_index("own")
    block_index = dp * own_count // dp_count
    total = acts_kv.shape[0] * dp_count
    in_width = acts_kv.shape[1]
    kv_width, up_width = grads_kv.shape[1], grads_up.shape[1]
    kv_cols, up_cols = weights_kv.shape[1], weights_up.shape[1]
    slot = dp % (dp_count // own_count)

    acts = jnp.concatenate([acts_kv, acts_up], 1)
    grads = jnp.concatenate([grads_kv, grads_up], 1)
    prev_low = [prev_g_kv[0].astype(BF), prev_g_up[0].astype(BF)]
    if (dp_count, own_count) == (8, 4):
        acts_all, block, prevs = gather_fast(acts, grads, prev_low)
    else:
        acts_all, block, prevs = gather_any(acts, grads, prev_low, block_index, dp_count, own_count)

    tokens = ((0,), (0,))
    outs, terms = [], []
    for linear, (a_prev, cols, start, width) in enumerate(
        ((prev_a_kv, kv_cols, 0, kv_width), (prev_a_up, up_cols, kv_width, up_width))
    ):
        fa, fg = 2 * linear, 2 * linear + 1
        a_l = acts_all[:, linear * in_width:(linear + 1) * in_width]
        g_l = block[:, start:start + width]
        g_damped = damp(prevs[linear].astype(F32), mm(g_l, g_l, tokens) / total, owners[1, fg], damping[fg])
        g_inv = inverse_columns(g_damped, init_scale[fg, block_index], slot * cols, cols)
        low = (mm(a_l, g_l, tokens) / total).astype(BF)
        right = mm(low, g_inv).astype(BF)
        a_damped = damp(a_prev[0], mm(a_l, a_l, tokens) / total, owners[1, fa], damping[fa])
        precond = apply_inverse(a_damped, init_scale[fa, own], right)
        term = jnp.sum(precond * lax.dynamic_slice_in_dim(low, slot * cols, cols, 1).astype(F32))
        outs.append(precond)
        terms.append(term)
    lane = lax.broadcasted_iota(jnp.int32, (dp_count * own_count, 128), 1)
    packed = jnp.where(lane == 0, terms[0], jnp.where(lane == 1, terms[1], 0.0))
    totals = jnp.sum(lax.all_to_all(packed, ("dp", "own"), 0, 0, tiled=True), axis=0)
    new = []
    for linear, w in enumerate((weights_kv, weights_up)):
        entries = w.shape[0] * w.shape[1] * dp_count * own_count
        new.append(w - step_size * jnp.sqrt(entries / totals[linear]) * outs[linear])
    return tuple(new)


def solution(mesh):
    tok, fac, rep = P("dp", "own"), P("own", None, None), P()
    return jax.shard_map(
        shards,
        mesh=mesh,
        in_specs=(tok, tok, tok, tok, fac, fac, fac, fac, rep, rep, rep, P("own", "dp"), P("own", "dp"), rep),
        out_specs=(P("own", "dp"), P("own", "dp")),
        check_vma=False,
    )
```

time: 936 us -> 179 us (0.19)
  waiting for transfers between devices: 714 us -> 51.1 us
  blocking collectives: 91.5 us -> 0 us
  starting transfers between devices: 19.2 us -> 40.3 us
  loops' own time: 16.7 us -> 0 us
    reduce_scatter x6 -> x0, waiting for transfers between devices: 464 us -> none  [the longest x1 127 us: shards(): lax.psum_scatter(lax.dot_general(column_block, full_up, (((0,), (0,)), ((...]
    psum x1 -> x0, waiting for transfers between devices: 137 us -> none  [spread(): return lax.psum(jnp.where(mine, value, jnp.zeros_like(value)), axis)]
    all_gather x4 -> x0, waiting for transfers between devices: 101 us -> none  [the longest x1 41.4 us: shards(): lax.all_gather(summed_rows[3], 'dp', axis=0, tiled=True)]
    all_gather x4 -> x0, blocking collectives: 52.8 us -> none  [the longest x1 31.2 us: shards(): lax.all_gather(summed_rows[1], 'dp', axis=0, tiled=True)]
    ppermute x0 -> x18, waiting for transfers between devices: none -> 44.7 us  [the longest x4 17.3 us: gather_fast(): a = a + [lax.ppermute(v, 'dp', y_swap) for v in a]]
    psum x1 -> x0, blocking collectives: 38.8 us -> none  [shards(): totals = lax.psum((term_kv, term_up), ('dp', 'own'))]
    ppermute x0 -> x18, starting transfers between devices: none -> 36.9 us  [the longest x2 6.72 us: gather_fast(): lax.ppermute(p, both, [(at(d, d // 2), at(d, d // 2 ^ 2)) for d in range(...]
    another operation x4 -> x0, loops' own time: 16.7 us -> none  [shards(): lax.cond(dp_index == owner_index, lambda matrix: newton_schulz(matrix, sc...]
  transfers between devices with their start and end apart: 15 -> 19, of which waited for: 12 -> 7; matrix products, arithmetic and copies ran while one was open for 6% -> 25% of each run, Pallas kernels for 0% -> 0%
where the time goes in v1:
time: 179 us; the launch traced here: 178 us
  waiting for transfers between devices  51.1 us (29%)
  starting transfers between devices  40.3 us (23%)
  matrix products  39.1 us (22%)
  other arithmetic  19.1 us (11%)
  local copies, waits for them, and re-layouts  17 us (9%)
  between operations  11 us (6%)
    dot_general x14, matrix products, mm(): return lax.dot_general(a, b, (dims, ((), ())), preferred_element_type=F32)  39.1 us
    ppermute x4, waiting for transfers between devices, gather_fast(): a = a + [lax.ppermute(v, 'dp', y_swap) for v in a]  17.3 us
    ppermute x3, waiting for transfers between devices, gather_fast(): piece = lax.ppermute(piece, both, pairs)  14.1 us
    ppermute x1, waiting for transfers between devices, gather_fast(): lax.ppermute(row, both, [(at(d, o), at(d, o ^ 2)) for d, o in sender])  13.2 us
    unnamed x51, local copies, waits for them, and re-layouts  9.87 us
    ppermute x2, starting transfers between devices, gather_fast(): lax.ppermute(p, both, [(at(d, d // 2), at(d, d // 2 ^ 2)) for d in range(...  6.72 us
    all_to_all x1, waiting for transfers between devices, shards(): lax.all_to_all(packed, ('dp', 'own'), 0, 0, tiled=True)  6.43 us
    ppermute x3, starting transfers between devices, gather_fast(): a = [mine] + [lax.ppermute(mine, 'dp', z_swap(k)) for k in (1, 2, 3)]  5.62 us
  transfers between devices with their start and end apart: 19, of which 7 were waited for; matrix products, arithmetic and copies ran while one was open for 25% of the time, Pallas kernels for 0%

profile of v1, /device:TPU:0, one launch (start us, length us, event | category | flops | bytes accessed | tf_op | source)
XLA Modules:
  0.0 177.7 jit_solution(12226562276012777822)
XLA Ops:
  4.2 3.0 %collective-permute-start = (bf16[128,1280]{1,0:T(8,128)(2,1)}, bf16[128,1280]{1,0:T(8,128)(2,1)}, u32[]{:S(2)}, u32[]{:S(2)}) collective-permute-start(bf16[128,1280]{1,0:T(8,128)(2,1)} %pad_maximum_fusion.1), channel_id=1, source_target_pairs={{0,8},{4,12},{8,0},{12,4},{16,24},{20,28},{24,16},{28,20},{1,9},{5... | collective-permute-start | bytes 983048 | tf_op jit(solution)/shard_map/ppermute | solution.py:65
  7.2 2.6 %collective-permute-start.1 = (bf16[128,1280]{1,0:T(8,128)(2,1)}, bf16[128,1280]{1,0:T(8,128)(2,1)}, u32[]{:S(2)}, u32[]{:S(2)}) collective-permute-start(bf16[128,1280]{1,0:T(8,128)(2,1)} %pad_maximum_fusion.1), channel_id=1, source_target_pairs={{0,16},{4,20},{8,24},{12,28},{16,0},{20,4},{24,8},{28,12},{1,17},{... | collective-permute-start | bytes 983048 | tf_op jit(solution)/shard_map/ppermute | solution.py:65
  13.8 2.2 %collective-permute-start.14 = (bf16[256,256]{1,0:T(8,128)(2,1)}, bf16[256,256]{1,0:T(8,128)(2,1)S(1)}, u32[]{:S(2)}, u32[]{:S(2)}) collective-permute-start(bf16[256,256]{1,0:T(8,128)(2,1)} %convert_bitcast_fusion.1), channel_id=1, source_target_pairs={{0,2},{4,6},{9,11},{13,15},{18,16},{22,20},{27,25},{31,29}} | collective-permute-start | bytes 393224 | tf_op jit(solution)/shard_map/ppermute | solution.py:93
  24.1 2.7 %collective-permute-start.9 = (bf16[64,1024]{1,0:T(8,128)(2,1)S(1)}, bf16[64,1024]{1,0:T(8,128)(2,1)S(1)}, u32[]{:S(2)}, u32[]{:S(2)}) collective-permute-start(bf16[64,1024]{1,0:T(8,128)(2,1)S(1)} %get-tuple-element.9), channel_id=1, source_target_pairs={{0,16},{2,18},{4,20},{6,22},{9,25},{11,27},{13,29},{15,31},{16,0},... | collective-permute-start | bytes 393224 | tf_op jit(solution)/shard_map/ppermute | solution.py:77
  28.2 4.8 %collective-permute-done.8 = bf16[64,1024]{1,0:T(8,128)(2,1)S(1)} collective-permute-done((bf16[64,1024]{1,0:T(8,128)(2,1)S(1)}, bf16[64,1024]{1,0:T(8,128)(2,1)S(1)}, u32[]{:S(2)}, u32[]{:S(2)}) %collective-permute-start.8) | collective-permute-done | bytes 131104 | tf_op jit(solution)/shard_map/ppermute | solution.py:77
  34.9 9.4 %collective-permute-done.9 = bf16[64,1024]{1,0:T(8,128)(2,1)S(1)} collective-permute-done((bf16[64,1024]{1,0:T(8,128)(2,1)S(1)}, bf16[64,1024]{1,0:T(8,128)(2,1)S(1)}, u32[]{:S(2)}, u32[]{:S(2)}) %collective-permute-start.9) | collective-permute-done | bytes 131104 | tf_op jit(solution)/shard_map/ppermute | solution.py:77
  46.5 4.5 %collective-permute-start.16 = (bf16[768,768]{1,0:T(8,128)(2,1)}, bf16[768,768]{1,0:T(8,128)(2,1)}, u32[]{:S(2)}, u32[]{:S(2)}) collective-permute-start(bf16[768,768]{1,0:T(8,128)(2,1)} %convert_bitcast_fusion), channel_id=1, source_target_pairs={{0,2},{4,6},{9,11},{13,15},{18,16},{22,20},{27,25},{31,29}} | collective-permute-start | bytes 3538952 | tf_op jit(solution)/shard_map/ppermute | solution.py:93
  54.0 2.4 %collective-permute-start.11 = (bf16[256,1024]{1,0:T(8,128)(2,1)S(1)}, bf16[256,1024]{1,0:T(8,128)(2,1)S(1)}, u32[]{:S(2)}, u32[]{:S(2)}) collective-permute-start(bf16[256,1024]{1,0:T(8,128)(2,1)S(1)} %pad_maximum_fusion), channel_id=1, source_target_pairs={{0,4},{2,6},{4,0},{6,2},{9,13},{11,15},{13,9},{15,11},{16,20},{18,... | collective-permute-start | bytes 1572872 | tf_op jit(solution)/shard_map/ppermute | solution.py:81
  59.6 11.7 %collective-permute-done.4 = bf16[128,1280]{1,0:T(8,128)(2,1)S(1)} collective-permute-done((bf16[128,1280]{1,0:T(8,128)(2,1)}, bf16[128,1280]{1,0:T(8,128)(2,1)S(1)}, u32[]{:S(2)}, u32[]{:S(2)}) %collective-permute-start.4) | collective-permute-done | bytes 327712 | tf_op jit(solution)/shard_map/ppermute | solution.py:88
  72.7 2.1 %collective-permute-done.5 = bf16[128,1280]{1,0:T(8,128)(2,1)S(1)} collective-permute-done((bf16[128,1280]{1,0:T(8,128)(2,1)}, bf16[128,1280]{1,0:T(8,128)(2,1)S(1)}, u32[]{:S(2)}, u32[]{:S(2)}) %collective-permute-start.5) | collective-permute-done | bytes 327712 | tf_op jit(solution)/shard_map/ppermute | solution.py:88
  74.8 3.5 %collective-permute-done.6 = bf16[128,1280]{1,0:T(8,128)(2,1)S(1)} collective-permute-done((bf16[128,1280]{1,0:T(8,128)(2,1)S(1)}, bf16[128,1280]{1,0:T(8,128)(2,1)S(1)}, u32[]{:S(2)}, u32[]{:S(2)}) %collective-permute-start.6) | collective-permute-done | bytes 327712 | tf_op jit(solution)/shard_map/ppermute | solution.py:88
  81.1 3.5 %collective-permute-start.12 = (bf16[512,1024]{1,0:T(8,128)(2,1)S(1)}, bf16[512,1024]{1,0:T(8,128)(2,1)S(1)}, u32[]{:S(2)}, u32[]{:S(2)}) collective-permute-start(bf16[512,1024]{1,0:T(8,128)(2,1)S(1)} %get-tuple-element.6), channel_id=1, source_target_pairs={{0,2},{2,0},{4,6},{6,4},{9,11},{11,9},{13,15},{15,13},{16,18},{18,... | collective-permute-start | bytes 3145736 | tf_op jit(solution)/shard_map/ppermute | solution.py:83
  84.7 13.2 %collective-permute-done.12 = bf16[512,1024]{1,0:T(8,128)(2,1)S(1)} collective-permute-done((bf16[512,1024]{1,0:T(8,128)(2,1)S(1)}, bf16[512,1024]{1,0:T(8,128)(2,1)S(1)}, u32[]{:S(2)}, u32[]{:S(2)}) %collective-permute-start.12) | collective-permute-done | bytes 1048608 | tf_op jit(solution)/shard_map/ppermute | solution.py:83
  99.0 2.7 %collective-permute-start.13 = (bf16[1024,1024]{1,0:T(8,128)(2,1)}, bf16[1024,1024]{1,0:T(8,128)(2,1)}, u32[]{:S(2)}, u32[]{:S(2)}) collective-permute-start(bf16[1024,1024]{1,0:T(8,128)(2,1)} %constant_dynamic-update-slice_fusion.11), channel_id=1, source_target_pairs={{0,1},{2,3},{4,5},{6,7},{9,8},{11,10},{13,12},{15,14},{16,17},{18,... | collective-permute-start | bytes 6291464 | tf_op jit(solution)/shard_map/ppermute | solution.py:85
  101.7 2.8 %multiply_reduce_fusion.2 = (f32[]{:T(128)}, f32[640,640]{1,0:T(8,128)S(1)}) fusion(f32[]{:T(128)} %bitcast.3, bf16[1024,1280]{1,0:T(8,128)(2,1)S(1)} %slice_dynamic-update-slice_fusion, f32[1,640,640]{2,1,0:T(8,128)S(1)} %copy-done.14, pred[]{:T(512)} %bitcast.1), kind=kOutput, calls=%fused_computation.19 | convolution fusion | flops 842547200 | bytes 4587529 | tf_op jit(solution)/shard_map/dot_general | solution.py:11
  105.2 4.8 %multiply_reduce_fusion.1 = (f32[]{:T(128)}, f32[640,640]{1,0:T(8,128)S(1)}) fusion(f32[]{:T(128)} %bitcast.11, bf16[1024,1280]{1,0:T(8,128)(2,1)} %copy-done.9, f32[1,640,640]{2,1,0:T(8,128)} %param.20, pred[]{:T(512)} %bitcast.9), kind=kOutput, calls=%fused_computation.17 | convolution fusion | flops 842547200 | bytes 4588548 | tf_op jit(solution)/shard_map/dot_general | solution.py:11
  112.0 2.9 %broadcast_select_fusion.1 = bf16[768,768]{1,0:T(8,128)(2,1)} fusion(bf16[768,768]{1,0:T(8,128)(2,1)} %collective-permute-done.16, pred[]{:T(512)S(6)} %eq.89, f32[1,768,768]{2,1,0:T(8,128)} %param.21), kind=kLoop, calls=%fused_computation.46 | loop fusion | flops 1179648 | bytes 4718593 | tf_op jit(solution)/shard_map/jit(_where)/select_n | solution.py:94
  114.9 2.7 %collective-permute-start.17 = (bf16[768,768]{1,0:T(8,128)(2,1)}, bf16[768,768]{1,0:T(8,128)(2,1)}, u32[]{:S(2)}, u32[]{:S(2)}) collective-permute-start(bf16[768,768]{1,0:T(8,128)(2,1)} %broadcast_select_fusion.1), channel_id=1, source_target_pairs={{0,1},{2,3},{4,5},{6,7},{9,8},{11,10},{13,12},{15,14},{16,17},{18,... | collective-permute-start | bytes 3538952 | tf_op jit(solution)/shard_map/ppermute | solution.py:95
  117.5 1.8 %broadcast_select_fusion = bf16[1024,1024]{1,0:T(8,128)(2,1)S(1)} fusion(bf16[1024,1024]{1,0:T(8,128)(2,1)} %constant_dynamic-update-slice_fusion.11, bf16[1024,1024]{1,0:T(8,128)(2,1)} %collective-permute-done.13, pred[]{:T(512)S(6)} %eq.82), kind=kLoop, calls=%fused_computation.6 | loop fusion | flops 1048576 | bytes 6291457 | tf_op jit(solution)/shard_map/jit(_where)/select_n | solution.py:87
  120.8 3.2 %multiply_reduce_fusion.5 = (f32[]{:T(128)}, f32[256,256]{1,0:T(8,128)}) fusion(f32[]{:T(128)} %bitcast.7, bf16[1024,1024]{1,0:T(8,128)(2,1)S(1)} %broadcast_select_fusion, bf16[256,256]{1,0:T(8,128)(2,1)} %broadcast_select_fusion.2, bf16[256,256]{1,0:T(8,128)(2,1)S(1)} %collective-permute-done.15, pred[]{:T(512)S(6)} %eq.82, pred[]{:T(512)} %bitcast.5), kind=kOutput, calls=%fused_computation.85 | convolution fusion | flops 134938624 | bytes 1048586 | tf_op jit(solution)/shard_map/dot_general | solution.py:11
  127.1 2.1 %convolution_convert_fusion.1 = bf16[640,128]{1,0:T(8,128)(2,1)} fusion(bf16[640,256]{1,0:T(8,128)(2,1)} %fusion.14, bf16[256,128]{1,0:T(8,128)(2,1)} %fusion.24, f32[256,256]{1,0:T(8,128)S(1)} %broadcast_multiply_fusion.1, s32[]{:T(128)S(6)} %select_n.217, s32[128]{0:T(128)S(1)} %iota_add_fusion.1, f32[]{:T(128)S(6)} %div.112), kind=kOutput, calls=%fused_computation.48 | convolution fusion | flops 59097088 | bytes 950792 | tf_op jit(solution)/shard_map/dot_general | solution.py:11
  130.5 3.3 %multiply_reduce_fusion.4 = (f32[]{:T(128)}, f32[640,128]{1,0:T(8,128)}) fusion(bf16[640,256]{1,0:T(8,128)(2,1)} %fusion.14, s32[]{:T(128)S(6)} %select_n.217, bf16[640,128]{1,0:T(8,128)(2,1)S(1)} %fusion.16, bf16[640,128]{1,0:T(8,128)(2,1)} %convolution_convert_fusion.1, f32[640,640]{1,0:T(8,128)S(1)} %get-tuple-element.37, f32[]{:T(128)S(6)} %div.91), kind=kOutput, calls=%fused_computation.82 | convolution fusion | flops 212254720 | bytes 4261892 | tf_op jit(solution)/shard_map/dot_general | solution.py:11
  133.8 3.2 %multiply_convert_fusion = bf16[640,768]{1,0:T(8,128)(2,1)S(1)} fusion(bf16[1024,1024]{1,0:T(8,128)(2,1)} %copy-done.2, bf16[1024,1280]{1,0:T(8,128)(2,1)} %copy-done.9), kind=kOutput, calls=%fused_computation.7 | convolution fusion | flops 1007616000 | bytes 3866624 | tf_op jit(solution)/shard_map/dot_general | solution.py:11
  137.1 5.7 %multiply_reduce_fusion = (f32[]{:T(128)}, f32[768,768]{1,0:T(8,128)}) fusion(f32[]{:T(128)} %bitcast.15, bf16[768,768]{1,0:T(8,128)(2,1)} %broadcast_select_fusion.1, bf16[768,768]{1,0:T(8,128)(2,1)} %collective-permute-done.17, pred[]{:T(512)S(6)} %eq.82, pred[]{:T(512)} %bitcast.13, bf16[1024,1024]{1,0:T(8,128)(2,1)S(1)} %copy-done.3), kind=kOutput, calls=%fused_computation.4 | convolution fusion | flops 1214447616 | bytes 6291466 | tf_op jit(solution)/shard_map/dot_general | solution.py:11
  144.0 3.3 %broadcast_multiply_fusion = f32[768,768]{1,0:T(8,128)S(1)} fusion(f32[]{:T(128)S(6)} %div.116, f32[]{:T(128)} %bitcast.15, f32[768,768]{1,0:T(8,128)} %get-tuple-element.39, bf16[768,768]{1,0:T(8,128)(2,1)} %broadcast_select_fusion.1, bf16[768,768]{1,0:T(8,128)(2,1)} %collective-permute-done.17, pred[]{:T(512)S(6)} %eq.82, pred[]{:T(512)} %bitcast.13), kind=kLoop, calls=%fused_computation.43 | loop fusion | flops 5898240 | bytes 7077898 | tf_op jit(solution)/shard_map/mul | solution.py:23
  148.7 1.8 %fusion.26 = f32[768,384]{1,0:T(8,128)} fusion(f32[768,768]{1,0:T(8,128)S(1)} %broadcast_multiply_fusion, s32[]{:T(128)S(6)} %select_n.229), kind=kOutput, calls=%fused_computation.64 | convolution fusion | flops 453574656 | bytes 4128772 | tf_op jit(solution)/shard_map/dot_general | solution.py:11
  150.5 4.2 %convolution_convert_fusion = bf16[640,384]{1,0:T(8,128)(2,1)S(1)} fusion(bf16[640,768]{1,0:T(8,128)(2,1)S(1)} %multiply_convert_fusion, f32[768,768]{1,0:T(8,128)} %copy-done.1, s32[]{:T(128)S(6)} %select_n.229, f32[768,384]{1,0:T(8,128)} %fusion.26, s32[384]{0:T(512)S(1)} %iota_add_fusion, f32[]{:T(128)S(6)} %div.116), kind=kOutput, calls=%fused_computation.31 | convolution fusion | flops 834256896 | bytes 7375872 | tf_op jit(solution)/shard_map/dot_general | solution.py:11
  156.1 3.1 %multiply_reduce_fusion.3 = (f32[]{:T(128)}, f32[640,384]{1,0:T(8,128)S(1)}) fusion(bf16[640,768]{1,0:T(8,128)(2,1)} %copy-done.6, s32[]{:T(128)S(6)} %select_n.229, bf16[640,384]{1,0:T(8,128)(2,1)} %fusion.12, bf16[640,384]{1,0:T(8,128)(2,1)S(1)} %convolution_convert_fusion, f32[640,640]{1,0:T(8,128)S(1)} %get-tuple-element.41, f32[]{:T(128)S(6)} %div.113), kind=kOutput, calls=%fused_computation.63 | convolution fusion | flops 633487360 | bytes 6227972 | tf_op jit(solution)/shard_map/dot_general | solution.py:11
  161.2 3.4 %all-to-all-start = ((f32[32,1,128]{2,1,0:T(1,128)}), f32[32,1,128]{2,1,0:T(1,128)S(1)}, u32[]{:S(2)}, u32[]{:S(2)}) async-start(f32[32,1,128]{2,1,0:T(1,128)} %broadcast_select_fusion.7), calls=%async_computation | async-start | bytes 32768 | tf_op jit(solution)/shard_map/all_to_all | solution.py:154
  165.3 6.4 %all-to-all-done = f32[32,1,128]{2,1,0:T(1,128)S(1)} async-done(((f32[32,1,128]{2,1,0:T(1,128)}), f32[32,1,128]{2,1,0:T(1,128)S(1)}, u32[]{:S(2)}, u32[]{:S(2)}) %all-to-all-start) | async-done | bytes 16416 | tf_op jit(solution)/shard_map/all_to_all | solution.py:154
  173.8 1.7 multiply_subtract_fusion.1
  175.5 2.2 %multiply_subtract_fusion = f32[640,384]{1,0:T(8,128)} fusion(f32[640,384]{1,0:T(8,128)} %param.26, f32[640,384]{1,0:T(8,128)S(1)} %get-tuple-element.43, f32[]{:T(128)S(6)} %mul.226), kind=kLoop, calls=%fused_computation.62 | loop fusion | flops 491520 | bytes 2949124 | tf_op jit(solution)/shard_map/sub | solution.py:158
  (99 shorter events, 39.9 us)
Async XLA Ops:
  0.6 9.2 %copy-start.7 = (bf16[128,256]{1,0:T(8,128)(2,1)S(1)}, bf16[128,256]{1,0:T(8,128)(2,1)}, u32[]{:S(2)}) copy-start(bf16[128,256]{1,0:T(8,128)(2,1)} %param.15) | copy-start | bytes 196612
  0.6 12.5 %copy-start.5 = (f32[1,256,256]{2,1,0:T(8,128)S(1)}, f32[1,256,256]{2,1,0:T(8,128)}, u32[]{:S(2)}) copy-start(f32[1,256,256]{2,1,0:T(8,128)} %param.19) | copy-start | bytes 786436
  0.7 15.4 %copy-start.12 = (s32[2,4]{1,0:T(2,128)S(1)}, s32[2,4]{1,0:T(2,128)}, u32[]{:S(2)}) copy-start(s32[2,4]{1,0:T(2,128)} %param.22) | copy-start | bytes 100
  0.7 16.1 %copy-start = (f32[1,768,768]{2,1,0:T(8,128)S(1)}, f32[1,768,768]{2,1,0:T(8,128)}, u32[]{:S(2)}) copy-start(f32[1,768,768]{2,1,0:T(8,128)} %param.21) | copy-start | bytes 7077892
  4.2 47.6 %collective-permute-start = (bf16[128,1280]{1,0:T(8,128)(2,1)}, bf16[128,1280]{1,0:T(8,128)(2,1)}, u32[]{:S(2)}, u32[]{:S(2)}) collective-permute-start(bf16[128,1280]{1,0:T(8,128)(2,1)} %pad_maximum_fusion.1), channel_id=1, source_target_pairs={{0,8},{4,12},{8,0},{12,4},{16,24},{20,28},{24,16},{28,20},{1,9},{5... | collective-permute-start | bytes 983048 | tf_op jit(solution)/shard_map/ppermute | solution.py:65
  7.2 46.8 %collective-permute-start.1 = (bf16[128,1280]{1,0:T(8,128)(2,1)}, bf16[128,1280]{1,0:T(8,128)(2,1)}, u32[]{:S(2)}, u32[]{:S(2)}) collective-permute-start(bf16[128,1280]{1,0:T(8,128)(2,1)} %pad_maximum_fusion.1), channel_id=1, source_target_pairs={{0,16},{4,20},{8,24},{12,28},{16,0},{20,4},{24,8},{28,12},{1,17},{... | collective-permute-start | bytes 983048 | tf_op jit(solution)/shard_map/ppermute | solution.py:65
  9.8 47.6 %collective-permute-start.2 = (bf16[128,1280]{1,0:T(8,128)(2,1)}, bf16[128,1280]{1,0:T(8,128)(2,1)S(1)}, u32[]{:S(2)}, u32[]{:S(2)}) collective-permute-start(bf16[128,1280]{1,0:T(8,128)(2,1)} %pad_maximum_fusion.1), channel_id=1, source_target_pairs={{0,24},{4,28},{8,16},{12,20},{16,8},{20,12},{24,0},{28,4},{1,25},{... | collective-permute-start | bytes 983048 | tf_op jit(solution)/shard_map/ppermute | solution.py:65
  11.4 9.0 %copy-start.13 = (f32[4,4]{1,0:T(4,128)S(1)}, f32[4,4]{1,0:T(4,128)}, u32[]{:S(2)}) copy-start(f32[4,4]{1,0:T(4,128)} %param.24) | copy-start | bytes 196
  11.4 9.7 %copy-start.11 = (f32[4]{0:T(128)S(1)}, f32[4]{0:T(128)}, u32[]{:S(2)}) copy-start(f32[4]{0:T(128)} %param.23) | copy-start | bytes 52
  11.4 10.4 %collective-permute-start.7 = (bf16[64,1024]{1,0:T(8,128)(2,1)}, bf16[64,1024]{1,0:T(8,128)(2,1)}, u32[]{:S(2)}, u32[]{:S(2)}) collective-permute-start(bf16[64,1024]{1,0:T(8,128)(2,1)} %constant_dynamic-slice_fusion), channel_id=1, source_target_pairs={{0,2},{1,3},{2,0},{3,1},{4,6},{5,7},{6,4},{7,5},{8,10},{9,11},{10,... | collective-permute-start | bytes 393224 | tf_op jit(solution)/shard_map/ppermute | solution.py:61
  13.8 10.3 %collective-permute-start.14 = (bf16[256,256]{1,0:T(8,128)(2,1)}, bf16[256,256]{1,0:T(8,128)(2,1)S(1)}, u32[]{:S(2)}, u32[]{:S(2)}) collective-permute-start(bf16[256,256]{1,0:T(8,128)(2,1)} %convert_bitcast_fusion.1), channel_id=1, source_target_pairs={{0,2},{4,6},{9,11},{13,15},{18,16},{22,20},{27,25},{31,29}} | collective-permute-start | bytes 393224 | tf_op jit(solution)/shard_map/ppermute | solution.py:93
  20.5 32.6 %copy-start.8 = (bf16[1024,1280]{1,0:T(8,128)(2,1)S(1)}, bf16[1024,1280]{1,0:T(8,128)(2,1)}, u32[]{:S(2)}) copy-start(bf16[1024,1280]{1,0:T(8,128)(2,1)} %get-tuple-element.4) | copy-start | bytes 7864324
  22.8 10.1 %collective-permute-start.8 = (bf16[64,1024]{1,0:T(8,128)(2,1)S(1)}, bf16[64,1024]{1,0:T(8,128)(2,1)S(1)}, u32[]{:S(2)}, u32[]{:S(2)}) collective-permute-start(bf16[64,1024]{1,0:T(8,128)(2,1)S(1)} %get-tuple-element.10), channel_id=1, source_target_pairs={{1,9},{3,11},{5,13},{7,15},{8,0},{10,2},{12,4},{14,6},{17,25},{19,... | collective-permute-start | bytes 393224 | tf_op jit(solution)/shard_map/ppermute | solution.py:77
  24.1 20.1 %collective-permute-start.9 = (bf16[64,1024]{1,0:T(8,128)(2,1)S(1)}, bf16[64,1024]{1,0:T(8,128)(2,1)S(1)}, u32[]{:S(2)}, u32[]{:S(2)}) collective-permute-start(bf16[64,1024]{1,0:T(8,128)(2,1)S(1)} %get-tuple-element.9), channel_id=1, source_target_pairs={{0,16},{2,18},{4,20},{6,22},{9,25},{11,27},{13,29},{15,31},{16,0},... | collective-permute-start | bytes 393224 | tf_op jit(solution)/shard_map/ppermute | solution.py:77
  32.9 13.6 %collective-permute-start.10 = (bf16[64,1024]{1,0:T(8,128)(2,1)S(1)}, bf16[64,1024]{1,0:T(8,128)(2,1)S(1)}, u32[]{:S(2)}, u32[]{:S(2)}) collective-permute-start(bf16[64,1024]{1,0:T(8,128)(2,1)S(1)} %get-tuple-element.8), channel_id=1, source_target_pairs={{1,25},{3,27},{5,29},{7,31},{8,16},{10,18},{12,20},{14,22},{17,9},... | collective-permute-start | bytes 393224 | tf_op jit(solution)/shard_map/ppermute | solution.py:77
  44.3 14.7 %collective-permute-start.3 = (bf16[128,1280]{1,0:T(8,128)(2,1)}, bf16[128,1280]{1,0:T(8,128)(2,1)S(1)}, u32[]{:S(2)}, u32[]{:S(2)}) collective-permute-start(bf16[128,1280]{1,0:T(8,128)(2,1)} %pad_maximum_fusion.1), channel_id=1, source_target_pairs={{0,4},{4,0},{8,12},{12,8},{16,20},{20,16},{24,28},{28,24},{1,5},{5... | collective-permute-start | bytes 983048 | tf_op jit(solution)/shard_map/ppermute | solution.py:88
  46.5 65.5 %collective-permute-start.16 = (bf16[768,768]{1,0:T(8,128)(2,1)}, bf16[768,768]{1,0:T(8,128)(2,1)}, u32[]{:S(2)}, u32[]{:S(2)}) collective-permute-start(bf16[768,768]{1,0:T(8,128)(2,1)} %convert_bitcast_fusion), channel_id=1, source_target_pairs={{0,2},{4,6},{9,11},{13,15},{18,16},{22,20},{27,25},{31,29}} | collective-permute-start | bytes 3538952 | tf_op jit(solution)/shard_map/ppermute | solution.py:93
  51.8 69.0 %collective-permute-start.15 = (bf16[256,256]{1,0:T(8,128)(2,1)}, bf16[256,256]{1,0:T(8,128)(2,1)S(1)}, u32[]{:S(2)}, u32[]{:S(2)}) collective-permute-start(bf16[256,256]{1,0:T(8,128)(2,1)} %broadcast_select_fusion.2), channel_id=1, source_target_pairs={{0,1},{2,3},{4,5},{6,7},{9,8},{11,10},{13,12},{15,14},{16,17},{18,... | collective-permute-start | bytes 393224 | tf_op jit(solution)/shard_map/ppermute | solution.py:95
  54.0 26.2 %collective-permute-start.11 = (bf16[256,1024]{1,0:T(8,128)(2,1)S(1)}, bf16[256,1024]{1,0:T(8,128)(2,1)S(1)}, u32[]{:S(2)}, u32[]{:S(2)}) collective-permute-start(bf16[256,1024]{1,0:T(8,128)(2,1)S(1)} %pad_maximum_fusion), channel_id=1, source_target_pairs={{0,4},{2,6},{4,0},{6,2},{9,13},{11,15},{13,9},{15,11},{16,20},{18,... | collective-permute-start | bytes 1572872 | tf_op jit(solution)/shard_map/ppermute | solution.py:81
  57.4 13.9 %collective-permute-start.4 = (bf16[128,1280]{1,0:T(8,128)(2,1)}, bf16[128,1280]{1,0:T(8,128)(2,1)S(1)}, u32[]{:S(2)}, u32[]{:S(2)}) collective-permute-start(bf16[128,1280]{1,0:T(8,128)(2,1)} %collective-permute-done), channel_id=1, source_target_pairs={{0,4},{4,0},{8,12},{12,8},{16,20},{20,16},{24,28},{28,24},{1,5},{5... | collective-permute-start | bytes 983048 | tf_op jit(solution)/shard_map/ppermute | solution.py:88
  59.0 15.8 %collective-permute-start.5 = (bf16[128,1280]{1,0:T(8,128)(2,1)}, bf16[128,1280]{1,0:T(8,128)(2,1)S(1)}, u32[]{:S(2)}, u32[]{:S(2)}) collective-permute-start(bf16[128,1280]{1,0:T(8,128)(2,1)} %collective-permute-done.1), channel_id=1, source_target_pairs={{0,4},{4,0},{8,12},{12,8},{16,20},{20,16},{24,28},{28,24},{1,5},{5... | collective-permute-start | bytes 983048 | tf_op jit(solution)/shard_map/ppermute | solution.py:88
  71.2 7.1 %collective-permute-start.6 = (bf16[128,1280]{1,0:T(8,128)(2,1)S(1)}, bf16[128,1280]{1,0:T(8,128)(2,1)S(1)}, u32[]{:S(2)}, u32[]{:S(2)}) collective-permute-start(bf16[128,1280]{1,0:T(8,128)(2,1)S(1)} %collective-permute-done.2), channel_id=1, source_target_pairs={{0,4},{4,0},{8,12},{12,8},{16,20},{20,16},{24,28},{28,24},{1,5},{5... | collective-permute-start | bytes 983048 | tf_op jit(solution)/shard_map/ppermute | solution.py:88
  81.1 20.6 %copy-start.14 = (f32[1,640,640]{2,1,0:T(8,128)S(1)}, f32[1,640,640]{2,1,0:T(8,128)}, u32[]{:S(2)}) copy-start(f32[1,640,640]{2,1,0:T(8,128)} %param.18) | copy-start | bytes 4915204
  81.1 16.8 %collective-permute-start.12 = (bf16[512,1024]{1,0:T(8,128)(2,1)S(1)}, bf16[512,1024]{1,0:T(8,128)(2,1)S(1)}, u32[]{:S(2)}, u32[]{:S(2)}) collective-permute-start(bf16[512,1024]{1,0:T(8,128)(2,1)S(1)} %get-tuple-element.6), channel_id=1, source_target_pairs={{0,2},{2,0},{4,6},{6,4},{9,11},{11,9},{13,15},{15,13},{16,18},{18,... | collective-permute-start | bytes 3145736 | tf_op jit(solution)/shard_map/ppermute | solution.py:83
  99.0 18.5 %collective-permute-start.13 = (bf16[1024,1024]{1,0:T(8,128)(2,1)}, bf16[1024,1024]{1,0:T(8,128)(2,1)}, u32[]{:S(2)}, u32[]{:S(2)}) collective-permute-start(bf16[1024,1024]{1,0:T(8,128)(2,1)} %constant_dynamic-update-slice_fusion.11), channel_id=1, source_target_pairs={{0,1},{2,3},{4,5},{6,7},{9,8},{11,10},{13,12},{15,14},{16,17},{18,... | collective-permute-start | bytes 6291464 | tf_op jit(solution)/shard_map/ppermute | solution.py:85
  114.9 4.5 %copy-start.10 = (bf16[1024,1280]{1,0:T(8,128)(2,1)S(1)}, bf16[1024,1280]{1,0:T(8,128)(2,1)}, u32[]{:S(2)}) copy-start(bf16[1024,1280]{1,0:T(8,128)(2,1)} %copy-done.9) | copy-start | bytes 7864324
  114.9 22.2 %collective-permute-start.17 = (bf16[768,768]{1,0:T(8,128)(2,1)}, bf16[768,768]{1,0:T(8,128)(2,1)}, u32[]{:S(2)}, u32[]{:S(2)}) collective-permute-start(bf16[768,768]{1,0:T(8,128)(2,1)} %broadcast_select_fusion.1), channel_id=1, source_target_pairs={{0,1},{2,3},{4,5},{6,7},{9,8},{11,10},{13,12},{15,14},{16,17},{18,... | collective-permute-start | bytes 3538952 | tf_op jit(solution)/shard_map/ppermute | solution.py:95
  119.3 4.6 %copy-start.2 = (bf16[1024,1024]{1,0:T(8,128)(2,1)}, bf16[1024,1024]{1,0:T(8,128)(2,1)S(1)}, u32[]{:S(2)}) copy-start(bf16[1024,1024]{1,0:T(8,128)(2,1)S(1)} %broadcast_select_fusion) | copy-start | bytes 6291460
  133.8 3.2 %copy-start.3 = (bf16[1024,1024]{1,0:T(8,128)(2,1)S(1)}, bf16[1024,1024]{1,0:T(8,128)(2,1)}, u32[]{:S(2)}) copy-start(bf16[1024,1024]{1,0:T(8,128)(2,1)} %copy-done.2) | copy-start | bytes 6291460
  137.0 13.4 %copy-start.6 = (bf16[640,768]{1,0:T(8,128)(2,1)}, bf16[640,768]{1,0:T(8,128)(2,1)S(1)}, u32[]{:S(2)}) copy-start(bf16[640,768]{1,0:T(8,128)(2,1)S(1)} %multiply_convert_fusion) | copy-start | bytes 2949124
  156.1 17.6 %copy-start.4 = (f32[640,128]{1,0:T(8,128)S(1)}, f32[640,128]{1,0:T(8,128)}, u32[]{:S(2)}) copy-start(f32[640,128]{1,0:T(8,128)} %get-tuple-element.45) | copy-start | bytes 983044
  161.2 10.5 %all-to-all-start = ((f32[32,1,128]{2,1,0:T(1,128)}), f32[32,1,128]{2,1,0:T(1,128)S(1)}, u32[]{:S(2)}, u32[]{:S(2)}) async-start(f32[32,1,128]{2,1,0:T(1,128)} %broadcast_select_fusion.7), calls=%async_computation | async-start | bytes 32768 | tf_op jit(solution)/shard_map/all_to_all | solution.py:154
  (2 other events, 4.2 us)

commit v2 on v1

v2 whole, which is shorter than its diff:
```python
import functools

import jax
import jax.numpy as jnp
from jax import lax
from jax.experimental import pallas as pl
from jax.experimental.pallas import tpu as pltpu
from jax.sharding import PartitionSpec as P

BF = jnp.bfloat16
F32 = jnp.float32


def contract(a, b, ad, bd):
    return lax.dot_general(a, b, (((ad,), (bd,)), ((), ())), preferred_element_type=F32)


def tiles(n, step=256):
    return [(s, min(step, n - s)) for s in range(0, n, step)]


def damped_into(m_ref, product, prev_ref, keep, mix, lam):
    n = m_ref.shape[0]
    total = jnp.zeros((1, 1), F32)
    for s, w in tiles(n):
        m = keep * prev_ref[:, s:s + w].astype(F32) + mix * product(s, w)
        rows = lax.broadcasted_iota(jnp.int32, (n, w), 0)
        cols = lax.broadcasted_iota(jnp.int32, (n, w), 1) + s
        m = jnp.where(rows == cols, m + lam, m)
        m_ref[:, s:s + w] = m
        total = total + jnp.sum(m * m, keepdims=True)
    return total


def scaled_into(y_ref, m_ref, coef):
    for s, w in tiles(m_ref.shape[0]):
        y_ref[:, s:s + w] = (coef * m_ref[:, s:s + w]).astype(BF)


def tile_kernel(count, quarters, in_width, widths, sc, where_ref, *refs):
    parts, blocks = refs[:count], refs[count:count + quarters]
    pa_kv, pa_up, pg_kv, pg_up, o_kv, o_up, t_ref = refs[count + quarters:count + quarters + 7]
    at, g, m_a, y_a, low, rt = refs[count + quarters + 7:count + quarters + 13]
    factor_refs = refs[count + quarters + 13:]
    dp, slot = where_ref[0], where_ref[1]
    chunk = parts[0].shape[1]
    piece = chunk // quarters
    for m in range(count):
        at[:, chunk * m:chunk * (m + 1)] = parts[m][...]
        source = pl.multiple_of(jnp.bitwise_xor(dp, m) * piece, piece)
        for q in range(quarters):
            g[chunk * m + piece * q:chunk * m + piece * (q + 1), :] = blocks[q][pl.ds(source, piece), :]
    begin = 0
    for linear, (pa, pg, out) in enumerate(((pa_kv, pg_kv, o_kv), (pa_up, pg_up, o_up))):
        width, cols = widths[linear], out.shape[1]
        m_g, y_g, i_g = factor_refs[3 * linear:3 * linear + 3]
        fa, fg = 2 * linear, 2 * linear + 1
        part = lambda s, w, begin=begin: g[:, begin + s:begin + s + w]
        squares = damped_into(
            m_g, lambda s, w: contract(part(0, width), part(s, w), 0, 0), pg, sc[0, fg], sc[1, fg], sc[2, fg]
        )
        coef = sc[3, fg] * lax.rsqrt(squares)
        scaled_into(y_g, m_g, coef)
        first = pl.multiple_of(slot * cols, 128)
        for s, w in tiles(cols):
            yc = coef * m_g[:, pl.ds(pl.multiple_of(first + s, 128), w)]
            square = contract(y_g[...], yc.astype(BF), 1, 0)
            cubic = contract(y_g[...], (4.0 * yc - square).astype(BF), 1, 0)
            rows = lax.broadcasted_iota(jnp.int32, (width, w), 0)
            lanes = lax.broadcasted_iota(jnp.int32, (width, w), 1) + (first + s)
            i_g[:, s:s + w] = (coef * (jnp.where(rows == lanes, 4.0, 0.0) - 6.0 * yc + cubic)).astype(BF)
        al = at.at[in_width * linear:in_width * (linear + 1), :]
        for s, w in tiles(width):
            low[:, s:s + w] = (contract(al[...], part(s, w), 1, 0) * sc[4, 0]).astype(BF)
        for s, w in tiles(cols):
            rt[:, s:s + w] = contract(low[:, :width], i_g[:, s:s + w], 1, 0).astype(BF)
        squares = damped_into(
            m_a, lambda s, w: contract(al[...], al[s:s + w, :], 1, 1), pa, sc[0, fa], sc[1, fa], sc[2, fa]
        )
        coef = sc[3, fa] * lax.rsqrt(squares)
        scaled_into(y_a, m_a, coef)
        total = jnp.zeros((1, 1), F32)
        for s, w in tiles(cols):
            right = rt[:, s:s + w]
            wide = right.astype(F32)
            inner = 4.0 * wide - contract(y_a[...], right, 1, 0)
            inner = 6.0 * wide - contract(y_a[...], inner.astype(BF), 1, 0)
            pre = coef * (4.0 * wide - contract(y_a[...], inner.astype(BF), 1, 0))
            out[:, s:s + w] = pre
            own_low = low[:, pl.ds(pl.multiple_of(first + s, 128), w)].astype(F32)
            total = total + jnp.sum(pre * own_low, keepdims=True)
        t_ref[linear:linear + 1, :] = jnp.broadcast_to(total, (1, 128))
        begin += width


def tile(sc, where, parts, blocks, pa_kv, pa_up, pg_kv, pg_up, cols):
    count, quarters = len(parts), len(blocks)
    in_width, widths = pa_kv.shape[0], (pg_kv.shape[0], pg_up.shape[0])
    tokens = parts[0].shape[1] * count
    vmem, smem = pl.BlockSpec(memory_space=pltpu.VMEM), pl.BlockSpec(memory_space=pltpu.SMEM)
    factors = []
    for w, c in zip(widths, cols):
        factors += [pltpu.VMEM((w, w), F32), pltpu.VMEM((w, w), BF), pltpu.VMEM((w, c), BF)]
    return pl.pallas_call(
        functools.partial(tile_kernel, count, quarters, in_width, widths),
        out_shape=(
            jax.ShapeDtypeStruct((in_width, cols[0]), F32),
            jax.ShapeDtypeStruct((in_width, cols[1]), F32),
            jax.ShapeDtypeStruct((2, 128), F32),
        ),
        in_specs=[smem, smem] + [vmem] * (count + quarters + 4),
        out_specs=(vmem, vmem, vmem),
        scratch_shapes=[
            pltpu.VMEM((2 * in_width, tokens), BF),
            pltpu.VMEM((tokens, sum(widths)), BF),
            pltpu.VMEM((in_width, in_width), F32),
            pltpu.VMEM((in_width, in_width), BF),
            pltpu.VMEM((in_width, max(widths)), BF),
            pltpu.VMEM((in_width, max(cols)), BF),
        ]
        + factors,
        compiler_params=pltpu.CompilerParams(vmem_limit_bytes=44 * 2**20),
        name="tile",
    )(sc, where, *parts, *blocks, pa_kv, pa_up, pg_kv, pg_up)


def update_kernel(entries, step_ref, sums_ref, p_kv, p_up, w_kv, w_up, n_kv, n_up):
    totals = jnp.sum(sums_ref[...], axis=0, keepdims=True)
    for linear, (p, w, n) in enumerate(((p_kv, w_kv, n_kv), (p_up, w_up, n_up))):
        total = totals[:, 128 * linear:128 * (linear + 1)]
        factor = step_ref[0] * jnp.sqrt(entries[linear] / total)
        for s, width in tiles(p.shape[1], 128):
            n[:, s:s + width] = w[:, s:s + width] - factor[:, :width] * p[:, s:s + width]


def update(entries, step_size, sums, p_kv, p_up, w_kv, w_up):
    vmem, smem = pl.BlockSpec(memory_space=pltpu.VMEM), pl.BlockSpec(memory_space=pltpu.SMEM)
    return pl.pallas_call(
        functools.partial(update_kernel, entries),
        out_shape=(jax.ShapeDtypeStruct(w_kv.shape, F32), jax.ShapeDtypeStruct(w_up.shape, F32)),
        in_specs=[smem] + [vmem] * 5,
        out_specs=(vmem, vmem),
        name="update",
    )(step_size.reshape(1), sums, p_kv, p_up, w_kv, w_up)


def mm(a, b, dims=((1,), (0,))):
    return lax.dot_general(a, b, (dims, ((), ())), preferred_element_type=F32)


def damp(previous, stat, fresh, lam):
    n = previous.shape[0]
    eye = lax.broadcasted_iota(jnp.int32, (n, n), 0) == lax.broadcasted_iota(jnp.int32, (n, n), 1)
    mixed = jnp.where(fresh == 1, 0.5 * previous + 0.5 * stat, previous)
    return mixed + jnp.where(eye, lam, 0.0)


def normalised(damped, scale):
    coef = scale / jnp.sqrt(jnp.sum(damped * damped))
    return coef, coef * damped


def inverse_columns(damped, scale, start, width):
    n = damped.shape[0]
    coef, y_full = normalised(damped, scale)
    y_low = y_full.astype(BF)
    y_cols = lax.dynamic_slice_in_dim(y_full, start, width, 1)
    square = mm(y_low, y_cols.astype(BF))
    cubic = mm(y_low, (4.0 * y_cols - square).astype(BF))
    rows = lax.broadcasted_iota(jnp.int32, (n, width), 0)
    cols = lax.broadcasted_iota(jnp.int32, (n, width), 1) + start
    out = coef * (jnp.where(rows == cols, 4.0, 0.0) - 6.0 * y_cols + cubic)
    return out.astype(BF)


def apply_inverse(damped, scale, right):
    coef, y_full = normalised(damped, scale)
    y_low = y_full.astype(BF)
    wide = right.astype(F32)
    inner = 4.0 * wide - mm(y_low, right)
    inner = 6.0 * wide - mm(y_low, inner.astype(BF))
    return coef * (4.0 * wide - mm(y_low, inner.astype(BF)))


def tile_any(acts_all, block, prevs, prev_a, owners, damping, init_scale, block_index, cols):
    own, total = lax.axis_index("own"), acts_all.shape[0]
    in_width = prev_a[0].shape[0]
    slot = lax.axis_index("dp") % (lax.axis_size("dp") // lax.axis_size("own"))
    tokens = ((0,), (0,))
    outs, terms, begin = [], [], 0
    for linear in range(2):
        fa, fg, width, c = 2 * linear, 2 * linear + 1, prevs[linear].shape[0], cols[linear]
        a_l = acts_all[:, linear * in_width:(linear + 1) * in_width]
        g_l = block[:, begin:begin + width]
        g_damped = damp(prevs[linear].astype(F32), mm(g_l, g_l, tokens) / total, owners[1, fg], damping[fg])
        g_inv = inverse_columns(g_damped, init_scale[fg, block_index], slot * c, c)
        low = (mm(a_l, g_l, tokens) / total).astype(BF)
        right = mm(low, g_inv).astype(BF)
        a_damped = damp(prev_a[linear], mm(a_l, a_l, tokens) / total, owners[1, fa], damping[fa])
        precond = apply_inverse(a_damped, init_scale[fa, own], right)
        terms.append(jnp.sum(precond * lax.dynamic_slice_in_dim(low, slot * c, c, 1).astype(F32)))
        outs.append(precond)
        begin += width
    return outs[0], outs[1], jnp.broadcast_to(jnp.stack(terms)[:, None], (2, 128))


def gather_fast(acts, grads, prev_low):
    dp, own = lax.axis_index("dp"), lax.axis_index("own")
    z, x = dp // 2, own // 2
    rows, cols = grads.shape
    piece = rows // 4
    both = ("dp", "own")
    at = lambda d, o: d * 4 + o
    dp_swap = lambda m: [(d, d ^ m) for d in range(8)]
    own_swap = lambda m: [(o, o ^ m) for o in range(4)]

    split = lax.all_to_all(grads.reshape(4, piece, cols), "own", 0, 0, tiled=True)
    order = [jnp.bitwise_xor(own, q) for q in (0, 2, 1, 3)]
    mine = jnp.concatenate([lax.dynamic_slice_in_dim(acts, piece * q, piece, 0) for q in order], 0).T
    chunks = {0: mine}
    for m in (2, 4, 6):
        chunks[m] = lax.ppermute(mine, "dp", dp_swap(m))
    for m in (0, 2, 4, 6):
        chunks[m + 1] = lax.ppermute(chunks[m], "dp", dp_swap(1))

    wanted = jnp.broadcast_to(split[:, None], (4, 2, piece, cols)).reshape(8, piece, cols)
    first = lax.all_to_all(wanted, "dp", 0, 0, tiled=True).reshape(8 * piece, cols)
    second = lax.ppermute(first, "own", own_swap(2))
    blocks = [first, second, lax.ppermute(first, "own", own_swap(1)), lax.ppermute(second, "own", own_swap(1))]

    low_bit = (own & 1) == (z & 1)
    prevs = []
    for p in prev_low:
        q = lax.ppermute(p, both, [(at(d, d // 2), at(d, (d // 2) ^ 2)) for d in range(8)])
        p = jnp.where(x == z // 2, p, q)
        q = lax.ppermute(
            p, both, [(at(d, o), at(d, o ^ 1)) for d in range(8) for o in range(4) if (o & 1) == ((d // 2) & 1)]
        )
        prevs.append(jnp.where(low_bit, p, q))
    return [chunks[m] for m in range(8)], blocks, prevs


def gather_any(acts, grads, prev_low, block_index):
    dp_count, own_count = lax.axis_size("dp"), lax.axis_size("own")
    rows, cols = grads.shape
    acts_all = lax.all_gather(acts, "dp", axis=0, tiled=True)
    split = lax.all_to_all(grads.reshape(own_count, rows // own_count, cols), "own", 0, 0, tiled=True)
    wanted = jnp.repeat(split, dp_count // own_count, axis=0)
    pieces = lax.all_to_all(wanted, "dp", 0, 0, tiled=True)
    block = lax.all_gather(pieces, "own", axis=1, tiled=True).reshape(rows * dp_count, cols)
    prevs = [
        lax.dynamic_index_in_dim(lax.all_gather(p[None], "own", axis=0, tiled=True), block_index, 0, keepdims=False)
        for p in prev_low
    ]
    return acts_all, block, prevs


def shards(acts_kv, grads_kv, acts_up, grads_up, prev_a_kv, prev_g_kv, prev_a_up, prev_g_up, owners, damping,
           init_scale, weights_kv, weights_up, step_size):
    dp_count, own_count = lax.axis_size("dp"), lax.axis_size("own")
    dp, own = lax.axis_index("dp"), lax.axis_index("own")
    block_index = dp * own_count // dp_count
    slot = dp % (dp_count // own_count)
    total = acts_kv.shape[0] * dp_count
    cols = (weights_kv.shape[1], weights_up.shape[1])
    entries = tuple(float(w.shape[0] * w.shape[1] * dp_count * own_count) for w in (weights_kv, weights_up))

    acts = jnp.concatenate([acts_kv, acts_up], 1)
    grads = jnp.concatenate([grads_kv, grads_up], 1)
    prev_low = [prev_g_kv[0].astype(BF), prev_g_up[0].astype(BF)]
    prev_a = (prev_a_kv[0], prev_a_up[0])
    if (dp_count, own_count) == (8, 4):
        parts, blocks, prevs = gather_fast(acts, grads, prev_low)
        fresh = owners[1] == 1
        scale = jnp.where(
            lax.broadcasted_iota(jnp.int32, (4,), 0) % 2 == 1,
            lax.dynamic_index_in_dim(init_scale, block_index, 1, keepdims=False),
            lax.dynamic_index_in_dim(init_scale, own, 1, keepdims=False),
        )
        sc = jnp.stack(
            [jnp.where(fresh, 0.5, 1.0), jnp.where(fresh, 0.5 / total, 0.0), damping, scale, jnp.full((4,), 1.0 / total)]
        )
        p_kv, p_up, terms = tile(
            sc, jnp.stack([dp, slot]).astype(jnp.int32), parts, blocks, *prev_a, *prevs, cols
        )
    else:
        acts_all, block, prevs = gather_any(acts, grads, prev_low, block_index)
        p_kv, p_up, terms = tile_any(acts_all, block, prevs, prev_a, owners, damping, init_scale, block_index, cols)
    sent = jnp.broadcast_to(terms.reshape(1, 256), (dp_count * own_count, 256))
    sums = lax.all_to_all(sent, ("dp", "own"), 0, 0, tiled=True)
    return update(entries, step_size, sums, p_kv, p_up, weights_kv, weights_up)


def solution(mesh):
    tok, fac, rep = P("dp", "own"), P("own", None, None), P()
    return jax.shard_map(
        shards,
        mesh=mesh,
        in_specs=(tok, tok, tok, tok, fac, fac, fac, fac, rep, rep, rep, P("own", "dp"), P("own", "dp"), rep),
        out_specs=(P("own", "dp"), P("own", "dp")),
        check_vma=False,
    )
```

time: 179 us -> 122 us (0.68)
  matrix products: 39.1 us -> 0 us
  Pallas kernels: 0 us -> 17.8 us
  local copies, waits for them, and re-layouts: 17 us -> 5.45 us
  other arithmetic: 19.1 us -> 7.94 us
  between operations: 11 us -> 1.49 us
  waiting for transfers between devices: 51.1 us -> 48.2 us
    dot_general x14 -> x0, matrix products: 39.1 us -> none  [mm(): return lax.dot_general(a, b, (dims, ((), ())), preferred_element_type=F32)]
    pallas_call x0 -> x2, Pallas kernels: none -> 17.8 us  [the longest x1 15 us: tile(): pl.pallas_call(functools.partial(tile_kernel, count, quarters, in_width,...]
    ppermute x14 -> x10, starting transfers between devices: 26.3 us -> 11.2 us  [the longest x4 5.53 us: gather_fast(): chunks[m + 1] = lax.ppermute(chunks[m], 'dp', dp_swap(1))]
    ppermute x14 -> x10, waiting for transfers between devices: 44.7 us -> 33.5 us  [the longest x3 17.7 us: gather_fast(): chunks[m] = lax.ppermute(mine, 'dp', dp_swap(m))]
    all_to_all x1 -> x3, starting transfers between devices: 3.42 us -> 13.1 us  [the longest x1 5.71 us: gather_fast(): lax.all_to_all(wanted, 'dp', 0, 0, tiled=True).reshape(8 * piece, cols)]
    all_to_all x1 -> x3, waiting for transfers between devices: 6.43 us -> 14.6 us  [the longest x1 6.6 us: shards(): sums = lax.all_to_all(sent, ('dp', 'own'), 0, 0, tiled=True)]
    unnamed x51 -> x25, local copies, waits for them, and re-layouts: 9.87 us -> 3.72 us
    select_n x6, other arithmetic: 8.25 us -> 2.77 us  [the longest x2 1.54 us: gather_fast(): prevs.append(jnp.where(low_bit, p, q))]
  transfers between devices with their start and end apart: 19 -> 17, of which waited for: 7 -> 8; matrix products, arithmetic and copies ran while one was open for 25% -> 6% of each run, Pallas kernels for 0% -> 0%
where the time goes in v2:
time: 122 us
  waiting for transfers between devices  48.2 us (40%)
  starting transfers between devices  40.9 us (34%)
  Pallas kernels  17.8 us (15%)
  other arithmetic  7.94 us (7%)
  local copies, waits for them, and re-layouts  5.45 us (4%)
  between operations  1.49 us (1%)
    ppermute x3, waiting for transfers between devices, gather_fast(): chunks[m] = lax.ppermute(mine, 'dp', dp_swap(m))  17.7 us
    ppermute x4, waiting for transfers between devices, gather_fast(): chunks[m + 1] = lax.ppermute(chunks[m], 'dp', dp_swap(1))  15.8 us
    pallas_call x1, Pallas kernels, tile(): pl.pallas_call(functools.partial(tile_kernel, count, quarters, in_width,...  15 us
    ppermute x2, starting transfers between devices, gather_fast(): lax.ppermute(p, both, [(at(d, d // 2), at(d, d // 2 ^ 2)) for d in range(...  10.5 us
    all_to_all x1, waiting for transfers between devices, shards(): sums = lax.all_to_all(sent, ('dp', 'own'), 0, 0, tiled=True)  6.6 us
    ppermute x2, starting transfers between devices, gather_fast(): lax.ppermute(p, both, [(at(d, o), at(d, o ^ 1)) for d in range(8) for o i...  6.02 us
    all_to_all x1, starting transfers between devices, gather_fast(): lax.all_to_all(wanted, 'dp', 0, 0, tiled=True).reshape(8 * piece, cols)  5.71 us
    ppermute x4, starting transfers between devices, gather_fast(): chunks[m + 1] = lax.ppermute(chunks[m], 'dp', dp_swap(1))  5.53 us
  transfers between devices with their start and end apart: 17, of which 8 were waited for; matrix products, arithmetic and copies ran while one was open for 6% of the time, Pallas kernels for 0%

profile of v2, /device:TPU:0, one launch (start us, length us, event | category | flops | bytes accessed | tf_op | source)
XLA Modules:
  0.0 121.7 jit_solution(10610794788243111792)
XLA Ops:
  0.6 2.8 %convert_bitcast_fusion = bf16[768,768]{1,0:T(8,128)(2,1)} fusion(f32[1,768,768]{2,1,0:T(8,128)} %param.21), kind=kLoop, calls=%fused_computation | loop fusion | flops 589824 | bytes 3538944 | tf_op jit(solution)/shard_map/convert_element_type | solution.py:270
  3.5 6.0 %collective-permute-start.12 = (bf16[768,768]{1,0:T(8,128)(2,1)}, bf16[768,768]{1,0:T(8,128)(2,1)}, u32[]{:S(2)}, u32[]{:S(2)}) collective-permute-start(bf16[768,768]{1,0:T(8,128)(2,1)} %convert_bitcast_fusion), channel_id=1, source_target_pairs={{0,2},{4,6},{9,11},{13,15},{18,16},{22,20},{27,25},{31,29}} | collective-permute-start | bytes 3538952 | tf_op jit(solution)/shard_map/ppermute | solution.py:234
  9.5 0.7 pad_maximum_fusion
  10.2 3.4 %all-to-all-start = ((bf16[4,32,1024]{2,1,0:T(8,128)(2,1)}), bf16[4,32,1024]{2,1,0:T(8,128)(2,1)S(1)}, u32[]{:S(2)}, u32[]{:S(2)}) async-start(bf16[4,32,1024]{2,1,0:T(8,128)(2,1)} %bitcast.5), calls=%async_computation | async-start | bytes 524288 | tf_op jit(solution)/shard_map/all_to_all | solution.py:217
  13.7 0.7 convert_bitcast_fusion.1
  14.3 4.5 %collective-permute-start.10 = (bf16[256,256]{1,0:T(8,128)(2,1)}, bf16[256,256]{1,0:T(8,128)(2,1)}, u32[]{:S(2)}, u32[]{:S(2)}) collective-permute-start(bf16[256,256]{1,0:T(8,128)(2,1)} %convert_bitcast_fusion.1), channel_id=1, source_target_pairs={{0,2},{4,6},{9,11},{13,15},{18,16},{22,20},{27,25},{31,29}} | collective-permute-start | bytes 393224 | tf_op jit(solution)/shard_map/ppermute | solution.py:234
  19.0 1.2 copy.19
  20.3 5.0 %all-to-all-done = bf16[4,32,1024]{2,1,0:T(8,128)(2,1)S(1)} async-done(((bf16[4,32,1024]{2,1,0:T(8,128)(2,1)}), bf16[4,32,1024]{2,1,0:T(8,128)(2,1)S(1)}, u32[]{:S(2)}, u32[]{:S(2)}) %all-to-all-start) | async-done | bytes 262176 | tf_op jit(solution)/shard_map/all_to_all | solution.py:217
  25.3 0.9 broadcast_in_dim.31
  26.2 5.7 %all-to-all-start.1 = ((bf16[8,32,1024]{2,1,0:T(8,128)(2,1)}), bf16[8,32,1024]{2,1,0:T(8,128)(2,1)S(1)}, u32[]{:S(2)}, u32[]{:S(2)}) async-start(bf16[8,32,1024]{2,1,0:T(8,128)(2,1)} %bitcast.6), calls=%async_computation.1 | async-start | bytes 1048576 | tf_op jit(solution)/shard_map/all_to_all | solution.py:227
  31.9 1.2 broadcast_select_fusion
  33.1 2.3 %collective-permute-start.13 = (bf16[768,768]{1,0:T(8,128)(2,1)}, bf16[768,768]{1,0:T(8,128)(2,1)}, u32[]{:S(2)}, u32[]{:S(2)}) collective-permute-start(bf16[768,768]{1,0:T(8,128)(2,1)} %broadcast_select_fusion), channel_id=1, source_target_pairs={{0,1},{2,3},{4,5},{6,7},{9,8},{11,10},{13,12},{15,14},{16,17},{18,... | collective-permute-start | bytes 3538952 | tf_op jit(solution)/shard_map/ppermute | solution.py:236
  36.3 1.0 collective-permute-start.1
  37.3 3.6 %collective-permute-start.3 = (bf16[1280,128]{1,0:T(8,128)(2,1)S(1)}, bf16[1280,128]{1,0:T(8,128)(2,1)S(1)}, u32[]{:S(2)}, u32[]{:S(2)}) collective-permute-start(bf16[1280,128]{1,0:T(8,128)(2,1)S(1)} %maximum_bitcast_fusion.refs_0_), channel_id=1, source_target_pairs={{0,16},{4,20},{8,24},{12,28},{16,0},{20,4},{24,8},{28,12},{1,17},{... | collective-permute-start | bytes 983048 | tf_op jit(solution)/shard_map/ppermute | solution.py:222
  41.2 3.7 %collective-permute-start.11 = (bf16[256,256]{1,0:T(8,128)(2,1)S(1)}, bf16[256,256]{1,0:T(8,128)(2,1)S(1)}, u32[]{:S(2)}, u32[]{:S(2)}) collective-permute-start(bf16[256,256]{1,0:T(8,128)(2,1)S(1)} %broadcast_select_fusion.2), channel_id=1, source_target_pairs={{0,1},{2,3},{4,5},{6,7},{9,8},{11,10},{13,12},{15,14},{16,17},{18,... | collective-permute-start | bytes 393224 | tf_op jit(solution)/shard_map/ppermute | solution.py:236
  44.9 3.0 %all-to-all-done.1 = bf16[8,32,1024]{2,1,0:T(8,128)(2,1)S(1)} async-done(((bf16[8,32,1024]{2,1,0:T(8,128)(2,1)}), bf16[8,32,1024]{2,1,0:T(8,128)(2,1)S(1)}, u32[]{:S(2)}, u32[]{:S(2)}) %all-to-all-start.1) | async-done | bytes 524320 | tf_op jit(solution)/shard_map/all_to_all | solution.py:227
  48.4 6.4 %collective-permute-done.1.refs_2_ = bf16[1280,128]{1,0:T(8,128)(2,1)S(1)} collective-permute-done((bf16[1280,128]{1,0:T(8,128)(2,1)S(1)}, bf16[1280,128]{1,0:T(8,128)(2,1)S(1)}, u32[]{:S(2)}, u32[]{:S(2)}) %collective-permute-start.1) | collective-permute-done | bytes 327712 | tf_op jit(solution)/shard_map/ppermute | solution.py:222
  54.8 2.6 %collective-permute-start = (bf16[1280,128]{1,0:T(8,128)(2,1)S(1)}, bf16[1280,128]{1,0:T(8,128)(2,1)S(1)}, u32[]{:S(2)}, u32[]{:S(2)}) collective-permute-start(bf16[1280,128]{1,0:T(8,128)(2,1)S(1)} %maximum_bitcast_fusion.refs_0_), channel_id=1, source_target_pairs={{0,4},{4,0},{8,12},{12,8},{16,20},{20,16},{24,28},{28,24},{1,5},{5... | collective-permute-start | bytes 983048 | tf_op jit(solution)/shard_map/ppermute | solution.py:224
  57.5 11.4 %collective-permute-done.3.refs_4_ = bf16[1280,128]{1,0:T(8,128)(2,1)S(1)} collective-permute-done((bf16[1280,128]{1,0:T(8,128)(2,1)S(1)}, bf16[1280,128]{1,0:T(8,128)(2,1)S(1)}, u32[]{:S(2)}, u32[]{:S(2)}) %collective-permute-start.3) | collective-permute-done | bytes 327712 | tf_op jit(solution)/shard_map/ppermute | solution.py:222
  68.9 0.9 collective-permute-start.2
  69.8 1.2 collective-permute-start.4
  71.0 0.9 collective-permute-start.6
  72.4 1.5 %broadcast_select_fusion.1.refs_15_ = bf16[768,768]{1,0:T(8,128)(2,1)S(1)} fusion(bf16[768,768]{1,0:T(8,128)(2,1)} %broadcast_select_fusion, bf16[768,768]{1,0:T(8,128)(2,1)} %collective-permute-done.13, pred[]{:T(512)S(6)} %eq.28), kind=kLoop, calls=%fused_computation.2 | loop fusion | flops 589824 | bytes 3538945 | tf_op jit(solution)/shard_map/jit(_where)/select_n | solution.py:239
  73.9 5.7 %collective-permute-done.2.refs_3_ = bf16[1280,128]{1,0:T(8,128)(2,1)S(1)} collective-permute-done((bf16[1280,128]{1,0:T(8,128)(2,1)S(1)}, bf16[1280,128]{1,0:T(8,128)(2,1)S(1)}, u32[]{:S(2)}, u32[]{:S(2)}) %collective-permute-start.2) | collective-permute-done | bytes 327712 | tf_op jit(solution)/shard_map/ppermute | solution.py:224
  79.6 6.6 %collective-permute-done.4.refs_5_ = bf16[1280,128]{1,0:T(8,128)(2,1)S(1)} collective-permute-done((bf16[1280,128]{1,0:T(8,128)(2,1)S(1)}, bf16[1280,128]{1,0:T(8,128)(2,1)S(1)}, u32[]{:S(2)}, u32[]{:S(2)}) %collective-permute-start.4) | collective-permute-done | bytes 327712 | tf_op jit(solution)/shard_map/ppermute | solution.py:224
  86.2 3.5 %collective-permute-done.6.refs_7_ = bf16[1280,128]{1,0:T(8,128)(2,1)S(1)} collective-permute-done((bf16[1280,128]{1,0:T(8,128)(2,1)S(1)}, bf16[1280,128]{1,0:T(8,128)(2,1)S(1)}, u32[]{:S(2)}, u32[]{:S(2)}) %collective-permute-start.6) | collective-permute-done | bytes 327712 | tf_op jit(solution)/shard_map/ppermute | solution.py:224
  89.7 15.0 %tile.1 = (f32[640,128]{1,0:T(8,128)S(1)}, f32[640,384]{1,0:T(8,128)S(1)}, f32[2,128]{1,0:T(2,128)S(1)}) custom-call(f32[5,4]{1,0:T(8,128)S(1)} %stack.19.sc, s32[2]{0:T(128)S(1)} %pad_add_fusion.where_ref, bf16[1280,128]{1,0:T(8,128)(2,1)S(1)} %maximum_bitcast_fusion.refs_0_, bf16[1280,128]{1,0:T(8,128)(2,1)S(1)} %collective-permute-done.refs_1_, ...), custom_call_target="tpu_custom_call" | custom-call | tf_op jit(solution)/shard_map/tile/pallas_call | solution.py:104
  104.7 1.0 copy-done.1
  105.7 0.7 copy-done.2
  107.1 4.0 %all-to-all-start.2 = ((f32[32,1,256]{2,1,0:T(1,128)}), f32[32,1,256]{2,1,0:T(1,128)S(1)}, u32[]{:S(2)}, u32[]{:S(2)}) async-start(f32[32,1,256]{2,1,0:T(1,128)} %broadcast_in_dim.33), calls=%async_computation.2 | async-start | bytes 65536 | tf_op jit(solution)/shard_map/all_to_all | solution.py:290
  111.7 6.6 %all-to-all-done.2 = f32[32,1,256]{2,1,0:T(1,128)S(1)} async-done(((f32[32,1,256]{2,1,0:T(1,128)}), f32[32,1,256]{2,1,0:T(1,128)S(1)}, u32[]{:S(2)}, u32[]{:S(2)}) %all-to-all-start.2) | async-done | bytes 32800 | tf_op jit(solution)/shard_map/all_to_all | solution.py:290
  118.9 2.8 %update.1 = (f32[640,128]{1,0:T(8,128)}, f32[640,384]{1,0:T(8,128)}) custom-call(f32[1]{0:T(128)} %bitcast.27.step_ref, f32[32,256]{1,0:T(8,128)} %bitcast.34, f32[640,128]{1,0:T(8,128)} %copy-done.2, f32[640,384]{1,0:T(8,128)} %copy-done.1, f32[640,128]{1,0:T(8,128)} %w_kv.1, f32[640,384]{1,0:T(8,128)} %w_up.1), custom_call_target="tpu_custom_call" | custom-call | tf_op jit(solution)/shard_map/update/pallas_call | solution.py:138
  (46 shorter events, 3.7 us)
Async XLA Ops:
  0.6 8.9 %copy-start.7 = (bf16[128,256]{1,0:T(8,128)(2,1)S(1)}, bf16[128,256]{1,0:T(8,128)(2,1)}, u32[]{:S(2)}) copy-start(bf16[128,256]{1,0:T(8,128)(2,1)} %param.15) | copy-start | bytes 196612
  0.6 8.9 %copy-start.5 = (bf16[128,768]{1,0:T(8,128)(2,1)S(1)}, bf16[128,768]{1,0:T(8,128)(2,1)}, u32[]{:S(2)}) copy-start(bf16[128,768]{1,0:T(8,128)(2,1)} %param.17) | copy-start | bytes 589828
  3.5 10.2 %copy-start.4 = (f32[1,256,256]{2,1,0:T(8,128)S(1)}, f32[1,256,256]{2,1,0:T(8,128)}, u32[]{:S(2)}) copy-start(f32[1,256,256]{2,1,0:T(8,128)} %param.19) | copy-start | bytes 786436
  3.5 15.4 %copy-start.6 = (bf16[128,640]{1,0:T(8,128)(2,1)S(1)}, bf16[128,640]{1,0:T(8,128)(2,1)}, u32[]{:S(2)}) copy-start(bf16[128,640]{1,0:T(8,128)(2,1)} %param.14) | copy-start | bytes 491524
  3.5 28.4 %collective-permute-start.12 = (bf16[768,768]{1,0:T(8,128)(2,1)}, bf16[768,768]{1,0:T(8,128)(2,1)}, u32[]{:S(2)}, u32[]{:S(2)}) collective-permute-start(bf16[768,768]{1,0:T(8,128)(2,1)} %convert_bitcast_fusion), channel_id=1, source_target_pairs={{0,2},{4,6},{9,11},{13,15},{18,16},{22,20},{27,25},{31,29}} | collective-permute-start | bytes 3538952 | tf_op jit(solution)/shard_map/ppermute | solution.py:234
  10.2 15.1 %all-to-all-start = ((bf16[4,32,1024]{2,1,0:T(8,128)(2,1)}), bf16[4,32,1024]{2,1,0:T(8,128)(2,1)S(1)}, u32[]{:S(2)}, u32[]{:S(2)}) async-start(bf16[4,32,1024]{2,1,0:T(8,128)(2,1)} %bitcast.5), calls=%async_computation | async-start | bytes 524288 | tf_op jit(solution)/shard_map/all_to_all | solution.py:217
  14.3 26.9 %collective-permute-start.10 = (bf16[256,256]{1,0:T(8,128)(2,1)}, bf16[256,256]{1,0:T(8,128)(2,1)}, u32[]{:S(2)}, u32[]{:S(2)}) collective-permute-start(bf16[256,256]{1,0:T(8,128)(2,1)} %convert_bitcast_fusion.1), channel_id=1, source_target_pairs={{0,2},{4,6},{9,11},{13,15},{18,16},{22,20},{27,25},{31,29}} | collective-permute-start | bytes 393224 | tf_op jit(solution)/shard_map/ppermute | solution.py:234
  18.8 13.0 %copy-start.3 = (f32[1,768,768]{2,1,0:T(8,128)S(1)}, f32[1,768,768]{2,1,0:T(8,128)}, u32[]{:S(2)}) copy-start(f32[1,768,768]{2,1,0:T(8,128)} %param.21) | copy-start | bytes 7077892
  26.2 21.8 %all-to-all-start.1 = ((bf16[8,32,1024]{2,1,0:T(8,128)(2,1)}), bf16[8,32,1024]{2,1,0:T(8,128)(2,1)S(1)}, u32[]{:S(2)}, u32[]{:S(2)}) async-start(bf16[8,32,1024]{2,1,0:T(8,128)(2,1)} %bitcast.6), calls=%async_computation.1 | async-start | bytes 1048576 | tf_op jit(solution)/shard_map/all_to_all | solution.py:227
  33.1 38.8 %collective-permute-start.13 = (bf16[768,768]{1,0:T(8,128)(2,1)}, bf16[768,768]{1,0:T(8,128)(2,1)}, u32[]{:S(2)}, u32[]{:S(2)}) collective-permute-start(bf16[768,768]{1,0:T(8,128)(2,1)} %broadcast_select_fusion), channel_id=1, source_target_pairs={{0,1},{2,3},{4,5},{6,7},{9,8},{11,10},{13,12},{15,14},{16,17},{18,... | collective-permute-start | bytes 3538952 | tf_op jit(solution)/shard_map/ppermute | solution.py:236
  35.8 5.1 %copy-start.8 = (f32[4,4]{1,0:T(4,128)S(1)}, f32[4,4]{1,0:T(4,128)}, u32[]{:S(2)}) copy-start(f32[4,4]{1,0:T(4,128)} %param.24) | copy-start | bytes 196
  35.9 12.1 %copy-start.10 = (s32[2,4]{1,0:T(2,128)S(1)}, s32[2,4]{1,0:T(2,128)}, u32[]{:S(2)}) copy-start(s32[2,4]{1,0:T(2,128)} %param.22) | copy-start | bytes 100
  35.9 21.6 %copy-start.9 = (f32[4]{0:T(128)S(1)}, f32[4]{0:T(128)}, u32[]{:S(2)}) copy-start(f32[4]{0:T(128)} %param.23) | copy-start | bytes 52
  36.3 18.5 %collective-permute-start.1 = (bf16[1280,128]{1,0:T(8,128)(2,1)S(1)}, bf16[1280,128]{1,0:T(8,128)(2,1)S(1)}, u32[]{:S(2)}, u32[]{:S(2)}) collective-permute-start(bf16[1280,128]{1,0:T(8,128)(2,1)S(1)} %maximum_bitcast_fusion.refs_0_), channel_id=1, source_target_pairs={{0,8},{4,12},{8,0},{12,4},{16,24},{20,28},{24,16},{28,20},{1,9},{5... | collective-permute-start | bytes 983048 | tf_op jit(solution)/shard_map/ppermute | solution.py:222
  37.3 31.6 %collective-permute-start.3 = (bf16[1280,128]{1,0:T(8,128)(2,1)S(1)}, bf16[1280,128]{1,0:T(8,128)(2,1)S(1)}, u32[]{:S(2)}, u32[]{:S(2)}) collective-permute-start(bf16[1280,128]{1,0:T(8,128)(2,1)S(1)} %maximum_bitcast_fusion.refs_0_), channel_id=1, source_target_pairs={{0,16},{4,20},{8,24},{12,28},{16,0},{20,4},{24,8},{28,12},{1,17},{... | collective-permute-start | bytes 983048 | tf_op jit(solution)/shard_map/ppermute | solution.py:222
  41.2 6.7 %collective-permute-start.11 = (bf16[256,256]{1,0:T(8,128)(2,1)S(1)}, bf16[256,256]{1,0:T(8,128)(2,1)S(1)}, u32[]{:S(2)}, u32[]{:S(2)}) collective-permute-start(bf16[256,256]{1,0:T(8,128)(2,1)S(1)} %broadcast_select_fusion.2), channel_id=1, source_target_pairs={{0,1},{2,3},{4,5},{6,7},{9,8},{11,10},{13,12},{15,14},{16,17},{18,... | collective-permute-start | bytes 393224 | tf_op jit(solution)/shard_map/ppermute | solution.py:236
  47.9 23.9 %collective-permute-start.7 = (bf16[256,1024]{1,0:T(8,128)(2,1)S(1)}, bf16[256,1024]{1,0:T(8,128)(2,1)S(1)}, u32[]{:S(2)}, u32[]{:S(2)}) collective-permute-start(bf16[256,1024]{1,0:T(8,128)(2,1)S(1)} %bitcast.28), channel_id=1, source_target_pairs={{0,2},{1,3},{2,0},{3,1},{4,6},{5,7},{6,4},{7,5},{8,10},{9,11},{10,... | collective-permute-start | bytes 1572872 | tf_op jit(solution)/shard_map/ppermute | solution.py:228
  47.9 21.9 %collective-permute-start.5 = (bf16[1280,128]{1,0:T(8,128)(2,1)S(1)}, bf16[1280,128]{1,0:T(8,128)(2,1)S(1)}, u32[]{:S(2)}, u32[]{:S(2)}) collective-permute-start(bf16[1280,128]{1,0:T(8,128)(2,1)S(1)} %maximum_bitcast_fusion.refs_0_), channel_id=1, source_target_pairs={{0,24},{4,28},{8,16},{12,20},{16,8},{20,12},{24,0},{28,4},{1,25},{... | collective-permute-start | bytes 983048 | tf_op jit(solution)/shard_map/ppermute | solution.py:222
  54.8 16.2 %collective-permute-start = (bf16[1280,128]{1,0:T(8,128)(2,1)S(1)}, bf16[1280,128]{1,0:T(8,128)(2,1)S(1)}, u32[]{:S(2)}, u32[]{:S(2)}) collective-permute-start(bf16[1280,128]{1,0:T(8,128)(2,1)S(1)} %maximum_bitcast_fusion.refs_0_), channel_id=1, source_target_pairs={{0,4},{4,0},{8,12},{12,8},{16,20},{20,16},{24,28},{28,24},{1,5},{5... | collective-permute-start | bytes 983048 | tf_op jit(solution)/shard_map/ppermute | solution.py:224
  68.9 10.6 %collective-permute-start.2 = (bf16[1280,128]{1,0:T(8,128)(2,1)S(1)}, bf16[1280,128]{1,0:T(8,128)(2,1)S(1)}, u32[]{:S(2)}, u32[]{:S(2)}) collective-permute-start(bf16[1280,128]{1,0:T(8,128)(2,1)S(1)} %collective-permute-done.1.refs_2_), channel_id=1, source_target_pairs={{0,4},{4,0},{8,12},{12,8},{16,20},{20,16},{24,28},{28,24},{1,5},{5... | collective-permute-start | bytes 983048 | tf_op jit(solution)/shard_map/ppermute | solution.py:224
  69.8 16.4 %collective-permute-start.4 = (bf16[1280,128]{1,0:T(8,128)(2,1)S(1)}, bf16[1280,128]{1,0:T(8,128)(2,1)S(1)}, u32[]{:S(2)}, u32[]{:S(2)}) collective-permute-start(bf16[1280,128]{1,0:T(8,128)(2,1)S(1)} %collective-permute-done.3.refs_4_), channel_id=1, source_target_pairs={{0,4},{4,0},{8,12},{12,8},{16,20},{20,16},{24,28},{28,24},{1,5},{5... | collective-permute-start | bytes 983048 | tf_op jit(solution)/shard_map/ppermute | solution.py:224
  71.0 18.7 %collective-permute-start.6 = (bf16[1280,128]{1,0:T(8,128)(2,1)S(1)}, bf16[1280,128]{1,0:T(8,128)(2,1)S(1)}, u32[]{:S(2)}, u32[]{:S(2)}) collective-permute-start(bf16[1280,128]{1,0:T(8,128)(2,1)S(1)} %collective-permute-done.5.refs_6_), channel_id=1, source_target_pairs={{0,4},{4,0},{8,12},{12,8},{16,20},{20,16},{24,28},{28,24},{1,5},{5... | collective-permute-start | bytes 983048 | tf_op jit(solution)/shard_map/ppermute | solution.py:224
  71.8 17.9 %collective-permute-start.8 = (bf16[256,1024]{1,0:T(8,128)(2,1)S(1)}, bf16[256,1024]{1,0:T(8,128)(2,1)S(1)}, u32[]{:S(2)}, u32[]{:S(2)}) collective-permute-start(bf16[256,1024]{1,0:T(8,128)(2,1)S(1)} %bitcast.29), channel_id=1, source_target_pairs={{0,1},{1,0},{2,3},{3,2},{4,5},{5,4},{6,7},{7,6},{8,9},{9,8},{10,11... | collective-permute-start | bytes 1572872 | tf_op jit(solution)/shard_map/ppermute | solution.py:229
  71.9 17.9 %collective-permute-start.9 = (bf16[256,1024]{1,0:T(8,128)(2,1)S(1)}, bf16[256,1024]{1,0:T(8,128)(2,1)S(1)}, u32[]{:S(2)}, u32[]{:S(2)}) collective-permute-start(bf16[256,1024]{1,0:T(8,128)(2,1)S(1)} %collective-permute-done.7.refs_9_), channel_id=1, source_target_pairs={{0,1},{1,0},{2,3},{3,2},{4,5},{5,4},{6,7},{7,6},{8,9},{9,8},{10,11... | collective-permute-start | bytes 1572872 | tf_op jit(solution)/shard_map/ppermute | solution.py:229
  72.4 17.3 %copy-start = (f32[1,640,640]{2,1,0:T(8,128)S(1)}, f32[1,640,640]{2,1,0:T(8,128)}, u32[]{:S(2)}) copy-start(f32[1,640,640]{2,1,0:T(8,128)} %param.18) | copy-start | bytes 4915204
  104.7 1.0 copy-start.1
  105.7 0.7 copy-start.2
  107.1 11.2 %all-to-all-start.2 = ((f32[32,1,256]{2,1,0:T(1,128)}), f32[32,1,256]{2,1,0:T(1,128)S(1)}, u32[]{:S(2)}, u32[]{:S(2)}) async-start(f32[32,1,256]{2,1,0:T(1,128)} %broadcast_in_dim.33), calls=%async_computation.2 | async-start | bytes 65536 | tf_op jit(solution)/shard_map/all_to_all | solution.py:290

commit v3 on v2

--- a/solution.py
+++ b/solution.py
@@ -38,18 +38,42 @@
 
 
 def tile_kernel(count, quarters, in_width, widths, sc, where_ref, *refs):
-    parts, blocks = refs[:count], refs[count:count + quarters]
-    pa_kv, pa_up, pg_kv, pg_up, o_kv, o_up, t_ref = refs[count + quarters:count + quarters + 7]
-    at, g, m_a, y_a, low, rt = refs[count + quarters + 7:count + quarters + 13]
-    factor_refs = refs[count + quarters + 13:]
-    dp, slot = where_ref[0], where_ref[1]
+    parts, blocks = refs[:count], refs[count:count + 2 * quarters]
+    refs = refs[count + 2 * quarters:]
+    prev_kv, prev_up, packed, o_kv, o_up, t_ref = refs[:6]
+    at, g, m_a, y_a, low, rt = refs[6:12]
+    factor_refs = refs[12:18]
+    pg_kv, pg_up, pa_kv, pa_up, packed_in, g_sems, p_sems, a_sems = refs[18:]
+    slot = where_ref[0]
     chunk = parts[0].shape[1]
     piece = chunk // quarters
+    loads_g, loads_a = [], []
     for m in range(count):
-        at[:, chunk * m:chunk * (m + 1)] = parts[m][...]
-        source = pl.multiple_of(jnp.bitwise_xor(dp, m) * piece, piece)
         for q in range(quarters):
-            g[chunk * m + piece * q:chunk * m + piece * (q + 1), :] = blocks[q][pl.ds(source, piece), :]
+            k = m % (count // 2)
+            loads_g.append(
+                pltpu.make_async_copy(
+                    blocks[q + quarters * (2 * m // count)].at[piece * k:piece * (k + 1), :],
+                    g.at[chunk * m + piece * q:chunk * m + piece * (q + 1), :],
+                    g_sems.at[quarters * m + q],
+                )
+            )
+        loads_a.append(pltpu.make_async_copy(parts[m], at.at[:, chunk * m:chunk * (m + 1)], a_sems.at[m]))
+    loads_p = [
+        pltpu.make_async_copy(source, target, p_sems.at[i])
+        for i, (source, target) in enumerate(((packed, packed_in), (prev_kv, pa_kv), (prev_up, pa_up)))
+    ]
+    for load in loads_p[:1] + loads_g + loads_a + loads_p[1:]:
+        load.start()
+    small, half = pg_kv.shape[0], pg_up.shape[0] // 2
+    loads_p[0].wait()
+    pg_kv[...] = packed_in[half:half + small, :small]
+    pg_up[:half, :] = packed_in[:half, :]
+    pg_up[half:, half:] = packed_in[half:, half:]
+    pg_up[half:, :half] = packed_in[:half, half:].T
+    for load in loads_g:
+        load.wait()
+
     begin = 0
     for linear, (pa, pg, out) in enumerate(((pa_kv, pg_kv, o_kv), (pa_up, pg_up, o_up))):
         width, cols = widths[linear], out.shape[1]
@@ -69,11 +93,15 @@
             rows = lax.broadcasted_iota(jnp.int32, (width, w), 0)
             lanes = lax.broadcasted_iota(jnp.int32, (width, w), 1) + (first + s)
             i_g[:, s:s + w] = (coef * (jnp.where(rows == lanes, 4.0, 0.0) - 6.0 * yc + cubic)).astype(BF)
+        if linear == 0:
+            for load in loads_a:
+                load.wait()
         al = at.at[in_width * linear:in_width * (linear + 1), :]
         for s, w in tiles(width):
             low[:, s:s + w] = (contract(al[...], part(s, w), 1, 0) * sc[4, 0]).astype(BF)
         for s, w in tiles(cols):
             rt[:, s:s + w] = contract(low[:, :width], i_g[:, s:s + w], 1, 0).astype(BF)
+        loads_p[1 + linear].wait()
         squares = damped_into(
             m_a, lambda s, w: contract(al[...], al[s:s + w, :], 1, 1), pa, sc[0, fa], sc[1, fa], sc[2, fa]
         )
@@ -93,11 +121,12 @@
         begin += width
 
 
-def tile(sc, where, parts, blocks, pa_kv, pa_up, pg_kv, pg_up, cols):
-    count, quarters = len(parts), len(blocks)
-    in_width, widths = pa_kv.shape[0], (pg_kv.shape[0], pg_up.shape[0])
+def tile(sc, where, parts, blocks, pa_kv, pa_up, packed, widths, cols):
+    count, quarters = len(parts), len(blocks) // 2
+    in_width = pa_kv.shape[0]
     tokens = parts[0].shape[1] * count
     vmem, smem = pl.BlockSpec(memory_space=pltpu.VMEM), pl.BlockSpec(memory_space=pltpu.SMEM)
+    anywhere = pl.BlockSpec(memory_space=pl.ANY)
     factors = []
     for w, c in zip(widths, cols):
         factors += [pltpu.VMEM((w, w), F32), pltpu.VMEM((w, w), BF), pltpu.VMEM((w, c), BF)]
@@ -108,7 +137,7 @@
             jax.ShapeDtypeStruct((in_width, cols[1]), F32),
             jax.ShapeDtypeStruct((2, 128), F32),
         ),
-        in_specs=[smem, smem] + [vmem] * (count + quarters + 4),
+        in_specs=[smem, smem] + [anywhere] * (count + 2 * quarters + 3),
         out_specs=(vmem, vmem, vmem),
         scratch_shapes=[
             pltpu.VMEM((2 * in_width, tokens), BF),
@@ -118,10 +147,36 @@
             pltpu.VMEM((in_width, max(widths)), BF),
             pltpu.VMEM((in_width, max(cols)), BF),
         ]
-        + factors,
-        compiler_params=pltpu.CompilerParams(vmem_limit_bytes=44 * 2**20),
+        + factors
+        + [pltpu.VMEM((w, w), BF) for w in widths]
+        + [pltpu.VMEM((in_width, in_width), F32)] * 2
+        + [pltpu.VMEM(packed.shape, BF)]
+        + [pltpu.SemaphoreType.DMA((n,)) for n in (count * quarters, 3, count)],
+        compiler_params=pltpu.CompilerParams(vmem_limit_bytes=32 * 2**20),
         name="tile",
-    )(sc, where, *parts, *blocks, pa_kv, pa_up, pg_kv, pg_up)
+    )(sc, where, *parts, *blocks, pa_kv, pa_up, packed)
+
+
+def stack_kernel(*refs):
+    *sources, out = refs
+    rows = sources[0].shape[0]
+    z = lax.axis_index("dp") // 2
+    inner = (z == 1) | (z == 2)
+    for i in range(2):
+        out[rows * i:rows * (i + 1), :] = sources[i][...]
+        out[rows * (2 + i):rows * (3 + i), :] = jnp.where(inner, sources[3 - i][...], sources[2 + i][...])
+
+
+def stack_rows(parts):
+    rows, cols = parts[0].shape
+    vmem = pl.BlockSpec(memory_space=pltpu.VMEM)
+    return pl.pallas_call(
+        stack_kernel,
+        out_shape=jax.ShapeDtypeStruct((rows * len(parts), cols), parts[0].dtype),
+        in_specs=[vmem] * len(parts),
+        out_specs=vmem,
+        name="stack",
+    )(*parts)
 
 
 def update_kernel(entries, step_ref, sums_ref, p_kv, p_up, w_kv, w_up, n_kv, n_up):
@@ -214,30 +269,53 @@
     dp_swap = lambda m: [(d, d ^ m) for d in range(8)]
     own_swap = lambda m: [(o, o ^ m) for o in range(4)]
 
-    split = lax.all_to_all(grads.reshape(4, piece, cols), "own", 0, 0, tiled=True)
     order = [jnp.bitwise_xor(own, q) for q in (0, 2, 1, 3)]
     mine = jnp.concatenate([lax.dynamic_slice_in_dim(acts, piece * q, piece, 0) for q in order], 0).T
-    chunks = {0: mine}
-    for m in (2, 4, 6):
-        chunks[m] = lax.ppermute(mine, "dp", dp_swap(m))
-    for m in (0, 2, 4, 6):
-        chunks[m + 1] = lax.ppermute(chunks[m], "dp", dp_swap(1))
-
-    wanted = jnp.broadcast_to(split[:, None], (4, 2, piece, cols)).reshape(8, piece, cols)
-    first = lax.all_to_all(wanted, "dp", 0, 0, tiled=True).reshape(8 * piece, cols)
-    second = lax.ppermute(first, "own", own_swap(2))
-    blocks = [first, second, lax.ppermute(first, "own", own_swap(1)), lax.ppermute(second, "own", own_swap(1))]
-
-    low_bit = (own & 1) == (z & 1)
-    prevs = []
-    for p in prev_low:
-        q = lax.ppermute(p, both, [(at(d, d // 2), at(d, (d // 2) ^ 2)) for d in range(8)])
-        p = jnp.where(x == z // 2, p, q)
-        q = lax.ppermute(
-            p, both, [(at(d, o), at(d, o ^ 1)) for d in range(8) for o in range(4) if (o & 1) == ((d // 2) & 1)]
-        )
-        prevs.append(jnp.where(low_bit, p, q))
-    return [chunks[m] for m in range(8)], blocks, prevs
+
+    def along_z(value, pairs):
+        return lax.ppermute(value, "dp", [(2 * s + y, 2 * t + y) for s, t in pairs for y in range(2)])
+
+    def across_y(value):
+        return lax.ppermute(value, "dp", dp_swap(1))
+
+    def repeat_y(value):
+        return jnp.broadcast_to(value[:, None], (4, 2, piece, cols)).reshape(8, piece, cols)
+
+    sends_x = [(at(d, d // 2), at(d, (d // 2) ^ 2)) for d in range(8)]
+    sends_core = [(at(d, o), at(d, o ^ 1)) for d in range(8) for o in range(4) if (o & 1) == ((d // 2) & 1)]
+    inner = (z == 1) | (z == 2)
+    middle, outward = ((1, 2), (2, 1)), ((1, 0), (2, 3))
+    pairs, mirror = ((0, 1), (1, 0), (2, 3), (3, 2)), ((0, 3), (3, 0), (1, 2), (2, 1))
+    skip = ((0, 2), (2, 0), (1, 3), (3, 1))
+    phase = lax.optimization_barrier
+
+    split = lax.all_to_all(grads.reshape(4, piece, cols), "own", 0, 0, tiled=True)
+    near, cross_a, beside = along_z(mine, pairs), along_z(mine, middle), across_y(mine)
+    split, near, cross_a, beside, prev_low = phase((split, near, cross_a, beside, prev_low))
+
+    wanted = [lax.dynamic_index_in_dim(split, jnp.bitwise_xor(z, k), 0, keepdims=False) for k in range(4)]
+    rows_z = [wanted[0]] + [along_z(wanted[k], [(s, s ^ k) for s in range(4)]) for k in (1, 2, 3)]
+    far_a = jnp.where(inner, cross_a, along_z(cross_a, outward))
+    cross_b = along_z(near, middle)
+    near_y = across_y(near)
+    prev_x = lax.ppermute(prev_low, both, sends_x)
+    rows_z, far_a, cross_b, near_y, prev_x = phase((rows_z, far_a, cross_b, near_y, prev_x))
+
+    strip = stack_rows(rows_z)
+    strip_y = across_y(strip)
+    far_b = jnp.where(inner, cross_b, along_z(cross_b, outward))
+    far_a_y = across_y(far_a)
+    prev_low = jnp.where(x == z // 2, prev_low, prev_x)
+    strip_y, far_b = phase((strip_y, far_b))
+
+    prev_core = lax.ppermute(prev_low, both, sends_core)
+    prev_low = jnp.where((own & 1) == (z & 1), prev_low, prev_core)
+    far_b_y = across_y(far_b)
+    blocks = []
+    for v in (strip, strip_y):
+        w = lax.ppermute(v, "own", own_swap(2))
+        blocks += [v, w, lax.ppermute(v, "own", own_swap(1)), lax.ppermute(w, "own", own_swap(1))]
+    return [mine, near, far_a, far_b, beside, near_y, far_a_y, far_b_y], blocks, prev_low
 
 
 def gather_any(acts, grads, prev_low, block_index):
@@ -267,10 +345,11 @@
 
     acts = jnp.concatenate([acts_kv, acts_up], 1)
     grads = jnp.concatenate([grads_kv, grads_up], 1)
-    prev_low = [prev_g_kv[0].astype(BF), prev_g_up[0].astype(BF)]
+    prev_g = [prev_g_kv[0].astype(BF), prev_g_up[0].astype(BF)]
     prev_a = (prev_a_kv[0], prev_a_up[0])
     if (dp_count, own_count) == (8, 4):
-        parts, blocks, prevs = gather_fast(acts, grads, prev_low)
+        packed = lax.dynamic_update_slice(prev_g[1], prev_g[0], (prev_g[1].shape[0] // 2, 0))
+        parts, blocks, packed = gather_fast(acts, grads, packed)
         fresh = owners[1] == 1
         scale = jnp.where(
             lax.broadcasted_iota(jnp.int32, (4,), 0) % 2 == 1,
@@ -281,10 +360,11 @@
             [jnp.where(fresh, 0.5, 1.0), jnp.where(fresh, 0.5 / total, 0.0), damping, scale, jnp.full((4,), 1.0 / total)]
         )
         p_kv, p_up, terms = tile(
-            sc, jnp.stack([dp, slot]).astype(jnp.int32), parts, blocks, *prev_a, *prevs, cols
+            sc, slot[None].astype(jnp.int32), parts, blocks, *prev_a, packed,
+            tuple(p.shape[0] for p in prev_g), cols
         )
     else:
-        acts_all, block, prevs = gather_any(acts, grads, prev_low, block_index)
+        acts_all, block, prevs = gather_any(acts, grads, prev_g, block_index)
         p_kv, p_up, terms = tile_any(acts_all, block, prevs, prev_a, owners, damping, init_scale, block_index, cols)
     sent = jnp.broadcast_to(terms.reshape(1, 256), (dp_count * own_count, 256))
     sums = lax.all_to_all(sent, ("dp", "own"), 0, 0, tiled=True)

time: 122 us -> 114 us (0.934)
  waiting for transfers between devices: 48.2 us -> 38.4 us
  Pallas kernels: 17.8 us -> 24.5 us
  starting transfers between devices: 40.9 us -> 36.2 us
  other arithmetic: 7.94 us -> 6.11 us
    ppermute x14 -> x21, waiting for transfers between devices: 33.5 us -> 27.6 us  [the longest x8 16 us: along_z(): lax.ppermute(value, 'dp', [(2 * s + y, 2 * t + y) for s, t in pairs for y...]
    all_to_all x1 -> x0, starting transfers between devices: 5.71 us -> none  [gather_fast(): lax.all_to_all(wanted, 'dp', 0, 0, tiled=True).reshape(8 * piece, cols)]
    pallas_call x1, Pallas kernels: 15 us -> 20.1 us  [tile(): pl.pallas_call(functools.partial(tile_kernel, count, quarters, in_width,...]
    all_to_all x1, starting transfers between devices: 3.98 us -> 7.61 us  [shards(): sums = lax.all_to_all(sent, ('dp', 'own'), 0, 0, tiled=True)]
    all_to_all x1 -> x0, waiting for transfers between devices: 3 us -> none  [gather_fast(): lax.all_to_all(wanted, 'dp', 0, 0, tiled=True).reshape(8 * piece, cols)]
    ppermute x14 -> x21, starting transfers between devices: 27.8 us -> 25.1 us  [the longest x8 12.4 us: along_z(): lax.ppermute(value, 'dp', [(2 * s + y, 2 * t + y) for s, t in pairs for y...]
    convert_element_type x2 -> x1, other arithmetic: 3.5 us -> 1.83 us  [shards(): prev_g = [prev_g_kv[0].astype(BF), prev_g_up[0].astype(BF)]]
    pallas_call x0 -> x1, Pallas kernels: none -> 1.66 us  [stack_rows(): pl.pallas_call(stack_kernel, out_shape=jax.ShapeDtypeStruct((rows * len(p...]
  transfers between devices with their start and end apart: 17 -> 23, of which waited for: 8 -> 9; matrix products, arithmetic and copies ran while one was open for 6% -> 5% of each run, Pallas kernels for 0% -> 1%
where the time goes in v3:
time: 114 us; the launch traced here: 113 us
  waiting for transfers between devices  38.4 us (34%)
  starting transfers between devices  36.2 us (32%)
  Pallas kernels  24.5 us (21%)
  local copies, waits for them, and re-layouts  6.67 us (6%)
  other arithmetic  6.11 us (5%)
  between operations  1.58 us (1%)
    pallas_call x1, Pallas kernels, tile(): pl.pallas_call(functools.partial(tile_kernel, count, quarters, in_width,...  20.1 us
    ppermute x8, waiting for transfers between devices, along_z(): lax.ppermute(value, 'dp', [(2 * s + y, 2 * t + y) for s, t in pairs for y...  16 us
    ppermute x8, starting transfers between devices, along_z(): lax.ppermute(value, 'dp', [(2 * s + y, 2 * t + y) for s, t in pairs for y...  12.4 us
    ppermute x5, waiting for transfers between devices, across_y(): return lax.ppermute(value, 'dp', dp_swap(1))  8.28 us
    all_to_all x1, starting transfers between devices, shards(): sums = lax.all_to_all(sent, ('dp', 'own'), 0, 0, tiled=True)  7.61 us
    all_to_all x1, waiting for transfers between devices, shards(): sums = lax.all_to_all(sent, ('dp', 'own'), 0, 0, tiled=True)  6.6 us
    ppermute x5, starting transfers between devices, across_y(): return lax.ppermute(value, 'dp', dp_swap(1))  5.18 us
    unnamed x31, local copies, waits for them, and re-layouts  5.12 us
  transfers between devices with their start and end apart: 23, of which 9 were waited for; matrix products, arithmetic and copies ran while one was open for 5% of the time, Pallas kernels for 1%

profile of v3, /device:TPU:0, one launch (start us, length us, event | category | flops | bytes accessed | tf_op | source)
XLA Modules:
  0.0 113.4 jit_solution(6183484273856974553)
XLA Ops:
  0.6 1.1 copy.18
  1.7 1.1 copy.19
  3.7 3.1 %collective-permute-start = (bf16[1280,128]{1,0:T(8,128)(2,1)S(1)}, bf16[1280,128]{1,0:T(8,128)(2,1)S(1)}, u32[]{:S(2)}, u32[]{:S(2)}) collective-permute-start(bf16[1280,128]{1,0:T(8,128)(2,1)S(1)} %maximum_bitcast_fusion.refs_0_), channel_id=1, source_target_pairs={{0,8},{4,12},{8,0},{12,4},{16,24},{20,28},{24,16},{28,20},{1,9},{5... | collective-permute-start | bytes 983048 | tf_op jit(solution)/shard_map/ppermute | solution.py:276
  7.5 1.6 %collective-permute-start.2 = (bf16[1280,128]{1,0:T(8,128)(2,1)S(1)}, bf16[1280,128]{1,0:T(8,128)(2,1)S(1)}, u32[]{:S(2)}, u32[]{:S(2)}) collective-permute-start(bf16[1280,128]{1,0:T(8,128)(2,1)S(1)} %maximum_bitcast_fusion.refs_0_), channel_id=1, source_target_pairs={{0,4},{4,0},{8,12},{12,8},{16,20},{20,16},{24,28},{28,24},{1,5},{5... | collective-permute-start | bytes 983048 | tf_op jit(solution)/shard_map/ppermute | solution.py:279
  9.1 0.7 pad_maximum_fusion
  9.8 3.4 %all-to-all-start = ((bf16[4,32,1024]{2,1,0:T(8,128)(2,1)}), bf16[4,32,1024]{2,1,0:T(8,128)(2,1)S(1)}, u32[]{:S(2)}, u32[]{:S(2)}) async-start(bf16[4,32,1024]{2,1,0:T(8,128)(2,1)} %bitcast.4), calls=%async_computation | async-start | bytes 524288 | tf_op jit(solution)/shard_map/all_to_all | solution.py:292
  13.2 1.8 %convert_bitcast_fusion = bf16[768,768]{1,0:T(8,128)(2,1)S(1)} fusion(f32[1,768,768]{2,1,0:T(8,128)} %param.21), kind=kLoop, calls=%fused_computation | loop fusion | flops 589824 | bytes 3538944 | tf_op jit(solution)/shard_map/convert_element_type | solution.py:348
  15.1 4.1 %all-to-all-done = bf16[4,32,1024]{2,1,0:T(8,128)(2,1)S(1)} async-done(((bf16[4,32,1024]{2,1,0:T(8,128)(2,1)}), bf16[4,32,1024]{2,1,0:T(8,128)(2,1)S(1)}, u32[]{:S(2)}, u32[]{:S(2)}) %all-to-all-start) | async-done | bytes 262176 | tf_op jit(solution)/shard_map/all_to_all | solution.py:292
  19.2 3.3 %collective-permute-start.9 = (bf16[768,768]{1,0:T(8,128)(2,1)S(1)}, bf16[768,768]{1,0:T(8,128)(2,1)}, u32[]{:S(2)}, u32[]{:S(2)}) collective-permute-start(bf16[768,768]{1,0:T(8,128)(2,1)S(1)} %bitcast_dynamic-update-slice_fusion), channel_id=1, source_target_pairs={{0,2},{4,6},{9,11},{13,15},{18,16},{22,20},{27,25},{31,29}} | collective-permute-start | bytes 3538952 | tf_op jit(solution)/shard_map/ppermute | solution.py:301
  22.5 1.3 %collective-permute-start.6 = (bf16[1280,128]{1,0:T(8,128)(2,1)S(1)}, bf16[1280,128]{1,0:T(8,128)(2,1)S(1)}, u32[]{:S(2)}, u32[]{:S(2)}) collective-permute-start(bf16[1280,128]{1,0:T(8,128)(2,1)S(1)} %collective-permute-done.1), channel_id=1, source_target_pairs={{8,0},{12,4},{16,24},{20,28},{9,1},{13,5},{17,25},{21,29},{10,2},{... | collective-permute-start | bytes 983048 | tf_op jit(solution)/shard_map/ppermute | solution.py:276
  24.5 2.8 %collective-permute-start.3 = (bf16[32,1024]{1,0:T(8,128)(2,1)S(1)}, bf16[32,1024]{1,0:T(8,128)(2,1)S(1)}, u32[]{:S(2)}, u32[]{:S(2)}) collective-permute-start(bf16[32,1024]{1,0:T(8,128)(2,1)S(1)} %get-tuple-element.46), channel_id=1, source_target_pairs={{0,8},{4,12},{8,0},{12,4},{16,24},{20,28},{24,16},{28,20},{1,9},{5... | collective-permute-start | bytes 196616 | tf_op jit(solution)/shard_map/ppermute | solution.py:276
  27.3 1.4 %collective-permute-start.7 = (bf16[1280,128]{1,0:T(8,128)(2,1)S(1)}, bf16[1280,128]{1,0:T(8,128)(2,1)}, u32[]{:S(2)}, u32[]{:S(2)}) collective-permute-start(bf16[1280,128]{1,0:T(8,128)(2,1)S(1)} %collective-permute-done.refs_1_), channel_id=1, source_target_pairs={{8,16},{12,20},{16,8},{20,12},{9,17},{13,21},{17,9},{21,13},{10,18... | collective-permute-start | bytes 983048 | tf_op jit(solution)/shard_map/ppermute | solution.py:276
  29.2 6.8 %collective-permute-done.3.refs_1_ = bf16[32,1024]{1,0:T(8,128)(2,1)S(1)} collective-permute-done((bf16[32,1024]{1,0:T(8,128)(2,1)S(1)}, bf16[32,1024]{1,0:T(8,128)(2,1)S(1)}, u32[]{:S(2)}, u32[]{:S(2)}) %collective-permute-start.3) | collective-permute-done | bytes 65568 | tf_op jit(solution)/shard_map/ppermute | solution.py:276
  36.1 1.9 %collective-permute-start.5 = (bf16[32,1024]{1,0:T(8,128)(2,1)}, bf16[32,1024]{1,0:T(8,128)(2,1)S(1)}, u32[]{:S(2)}, u32[]{:S(2)}) collective-permute-start(bf16[32,1024]{1,0:T(8,128)(2,1)} %get-tuple-element.44), channel_id=1, source_target_pairs={{0,24},{4,28},{8,16},{12,20},{16,8},{20,12},{24,0},{28,4},{1,25},{... | collective-permute-start | bytes 196616 | tf_op jit(solution)/shard_map/ppermute | solution.py:276
  38.0 5.6 %collective-permute-done.4.refs_2_ = bf16[32,1024]{1,0:T(8,128)(2,1)S(1)} collective-permute-done((bf16[32,1024]{1,0:T(8,128)(2,1)}, bf16[32,1024]{1,0:T(8,128)(2,1)S(1)}, u32[]{:S(2)}, u32[]{:S(2)}) %collective-permute-start.4) | collective-permute-done | bytes 65568 | tf_op jit(solution)/shard_map/ppermute | solution.py:276
  44.2 1.3 %collective-permute-start.11 = (bf16[1280,128]{1,0:T(8,128)(2,1)}, bf16[1280,128]{1,0:T(8,128)(2,1)S(1)}, u32[]{:S(2)}, u32[]{:S(2)}) collective-permute-start(bf16[1280,128]{1,0:T(8,128)(2,1)} %collective-permute-done.7), channel_id=1, source_target_pairs={{8,0},{12,4},{16,24},{20,28},{9,1},{13,5},{17,25},{21,29},{10,2},{... | collective-permute-start | bytes 983048 | tf_op jit(solution)/shard_map/ppermute | solution.py:276
  45.5 1.2 %broadcast_select_fusion = bf16[768,768]{1,0:T(8,128)(2,1)} fusion(bf16[768,768]{1,0:T(8,128)(2,1)S(1)} %bitcast_dynamic-update-slice_fusion, bf16[768,768]{1,0:T(8,128)(2,1)} %collective-permute-done.9, pred[]{:T(512)S(6)} %eq.36), kind=kLoop, calls=%fused_computation.1 | loop fusion | flops 589824 | bytes 3538945 | tf_op jit(solution)/shard_map/jit(_where)/select_n | solution.py:308
  46.7 3.1 %collective-permute-start.20 = (bf16[768,768]{1,0:T(8,128)(2,1)}, bf16[768,768]{1,0:T(8,128)(2,1)}, u32[]{:S(2)}, u32[]{:S(2)}) collective-permute-start(bf16[768,768]{1,0:T(8,128)(2,1)} %broadcast_select_fusion), channel_id=1, source_target_pairs={{0,1},{2,3},{4,5},{6,7},{9,8},{11,10},{13,12},{15,14},{16,17},{18,... | collective-permute-start | bytes 3538952 | tf_op jit(solution)/shard_map/ppermute | solution.py:311
  49.8 1.7 %stack.12.refs_8_ = bf16[128,1024]{1,0:T(8,128)(2,1)} custom-call(bf16[32,1024]{1,0:T(8,128)(2,1)} %get-tuple-element.25.refs_0_, bf16[32,1024]{1,0:T(8,128)(2,1)} %copy-done.8, bf16[32,1024]{1,0:T(8,128)(2,1)} %copy-done.9, bf16[32,1024]{1,0:T(8,128)(2,1)} %copy-done.10), custom_call_target="tpu_custom_call" | custom-call | tf_op jit(solution)/shard_map/stack/pallas_call | solution.py:173
  52.4 3.6 %collective-permute-done.11 = bf16[1280,128]{1,0:T(8,128)(2,1)S(1)} collective-permute-done((bf16[1280,128]{1,0:T(8,128)(2,1)}, bf16[1280,128]{1,0:T(8,128)(2,1)S(1)}, u32[]{:S(2)}, u32[]{:S(2)}) %collective-permute-start.11) | collective-permute-done | bytes 327712 | tf_op jit(solution)/shard_map/ppermute | solution.py:276
  56.0 2.3 %collective-permute-done.10.refs_12_ = bf16[128,1024]{1,0:T(8,128)(2,1)S(1)} collective-permute-done((bf16[128,1024]{1,0:T(8,128)(2,1)}, bf16[128,1024]{1,0:T(8,128)(2,1)S(1)}, u32[]{:S(2)}, u32[]{:S(2)}) %collective-permute-start.10) | collective-permute-done | bytes 262176 | tf_op jit(solution)/shard_map/ppermute | solution.py:279
  59.3 2.0 %collective-permute-start.13 = (bf16[1280,128]{1,0:T(8,128)(2,1)S(1)}, bf16[1280,128]{1,0:T(8,128)(2,1)S(1)}, u32[]{:S(2)}, u32[]{:S(2)}) collective-permute-start(bf16[1280,128]{1,0:T(8,128)(2,1)S(1)} %broadcast_select_fusion.2.refs_3_), channel_id=1, source_target_pairs={{0,4},{4,0},{8,12},{12,8},{16,20},{20,16},{24,28},{28,24},{1,5},{5... | collective-permute-start | bytes 983048 | tf_op jit(solution)/shard_map/ppermute | solution.py:279
  61.5 3.3 %collective-permute-done.17.refs_13_ = bf16[128,1024]{1,0:T(8,128)(2,1)} collective-permute-done((bf16[128,1024]{1,0:T(8,128)(2,1)S(1)}, bf16[128,1024]{1,0:T(8,128)(2,1)}, u32[]{:S(2)}, u32[]{:S(2)}) %collective-permute-start.17) | collective-permute-done | bytes 262176 | tf_op jit(solution)/shard_map/ppermute | solution.py:316
  65.3 1.4 %broadcast_select_fusion.1.refs_18_ = bf16[768,768]{1,0:T(8,128)(2,1)S(1)} fusion(bf16[768,768]{1,0:T(8,128)(2,1)} %broadcast_select_fusion, bf16[768,768]{1,0:T(8,128)(2,1)} %collective-permute-done.20, pred[]{:T(512)S(6)} %eq.35), kind=kLoop, calls=%fused_computation.2 | loop fusion | flops 589824 | bytes 3538945 | tf_op jit(solution)/shard_map/jit(_where)/select_n | solution.py:312
  66.7 2.5 %collective-permute-done.12.refs_6_ = bf16[1280,128]{1,0:T(8,128)(2,1)S(1)} collective-permute-done((bf16[1280,128]{1,0:T(8,128)(2,1)S(1)}, bf16[1280,128]{1,0:T(8,128)(2,1)S(1)}, u32[]{:S(2)}, u32[]{:S(2)}) %collective-permute-start.12) | collective-permute-done | bytes 327712 | tf_op jit(solution)/shard_map/ppermute | solution.py:279
  69.2 3.5 %collective-permute-done.13.refs_7_ = bf16[1280,128]{1,0:T(8,128)(2,1)S(1)} collective-permute-done((bf16[1280,128]{1,0:T(8,128)(2,1)S(1)}, bf16[1280,128]{1,0:T(8,128)(2,1)S(1)}, u32[]{:S(2)}, u32[]{:S(2)}) %collective-permute-start.13) | collective-permute-done | bytes 327712 | tf_op jit(solution)/shard_map/ppermute | solution.py:279
  72.7 20.1 %tile.1 = (f32[640,128]{1,0:T(8,128)S(1)}, f32[640,384]{1,0:T(8,128)S(1)}, f32[2,128]{1,0:T(2,128)S(1)}) custom-call(f32[5,4]{1,0:T(8,128)S(1)} %stack.11.sc, s32[1]{0:T(128)} %bitcast.2.where_ref, bf16[1280,128]{1,0:T(8,128)(2,1)S(1)} %maximum_bitcast_fusion.refs_0_, bf16[1280,128]{1,0:T(8,128)(2,1)S(1)} %collective-permute-done.refs_1_, ...), custom_call_target="tpu_custom_call" | custom-call | tf_op jit(solution)/shard_map/tile/pallas_call | solution.py:133
  92.8 1.0 copy-done.3
  93.8 0.7 copy-done.4
  95.1 7.6 %all-to-all-start.1 = ((f32[32,1,256]{2,1,0:T(1,128)}), f32[32,1,256]{2,1,0:T(1,128)S(1)}, u32[]{:S(2)}, u32[]{:S(2)}) async-start(f32[32,1,256]{2,1,0:T(1,128)} %broadcast_in_dim.30), calls=%async_computation.1 | async-start | bytes 65536 | tf_op jit(solution)/shard_map/all_to_all | solution.py:370
  103.4 6.6 %all-to-all-done.1 = f32[32,1,256]{2,1,0:T(1,128)S(1)} async-done(((f32[32,1,256]{2,1,0:T(1,128)}), f32[32,1,256]{2,1,0:T(1,128)S(1)}, u32[]{:S(2)}, u32[]{:S(2)}) %all-to-all-start.1) | async-done | bytes 32800 | tf_op jit(solution)/shard_map/all_to_all | solution.py:370
  110.6 2.8 %update.1 = (f32[640,128]{1,0:T(8,128)}, f32[640,384]{1,0:T(8,128)}) custom-call(f32[1]{0:T(128)} %bitcast.28.step_ref, f32[32,256]{1,0:T(8,128)} %bitcast.32, f32[640,128]{1,0:T(8,128)} %copy-done.4, f32[640,384]{1,0:T(8,128)} %copy-done.3, f32[640,128]{1,0:T(8,128)} %w_kv.1, f32[640,384]{1,0:T(8,128)} %w_up.1), custom_call_target="tpu_custom_call" | custom-call | tf_op jit(solution)/shard_map/update/pallas_call | solution.py:193
  (64 shorter events, 7.3 us)
Async XLA Ops:
  3.3 5.8 %copy-start.6 = (bf16[128,768]{1,0:T(8,128)(2,1)S(1)}, bf16[128,768]{1,0:T(8,128)(2,1)}, u32[]{:S(2)}) copy-start(bf16[128,768]{1,0:T(8,128)(2,1)} %param.17) | copy-start | bytes 589828
  3.3 5.8 %copy-start.7 = (bf16[128,256]{1,0:T(8,128)(2,1)S(1)}, bf16[128,256]{1,0:T(8,128)(2,1)}, u32[]{:S(2)}) copy-start(bf16[128,256]{1,0:T(8,128)(2,1)} %param.15) | copy-start | bytes 196612
  3.7 15.5 %collective-permute-start = (bf16[1280,128]{1,0:T(8,128)(2,1)S(1)}, bf16[1280,128]{1,0:T(8,128)(2,1)S(1)}, u32[]{:S(2)}, u32[]{:S(2)}) collective-permute-start(bf16[1280,128]{1,0:T(8,128)(2,1)S(1)} %maximum_bitcast_fusion.refs_0_), channel_id=1, source_target_pairs={{0,8},{4,12},{8,0},{12,4},{16,24},{20,28},{24,16},{28,20},{1,9},{5... | collective-permute-start | bytes 983048 | tf_op jit(solution)/shard_map/ppermute | solution.py:276
  6.8 12.4 %collective-permute-start.1 = (bf16[1280,128]{1,0:T(8,128)(2,1)S(1)}, bf16[1280,128]{1,0:T(8,128)(2,1)S(1)}, u32[]{:S(2)}, u32[]{:S(2)}) collective-permute-start(bf16[1280,128]{1,0:T(8,128)(2,1)S(1)} %maximum_bitcast_fusion.refs_0_), channel_id=1, source_target_pairs={{8,16},{12,20},{16,8},{20,12},{9,17},{13,21},{17,9},{21,13},{10,18... | collective-permute-start | bytes 983048 | tf_op jit(solution)/shard_map/ppermute | solution.py:276
  7.5 11.7 %collective-permute-start.2 = (bf16[1280,128]{1,0:T(8,128)(2,1)S(1)}, bf16[1280,128]{1,0:T(8,128)(2,1)S(1)}, u32[]{:S(2)}, u32[]{:S(2)}) collective-permute-start(bf16[1280,128]{1,0:T(8,128)(2,1)S(1)} %maximum_bitcast_fusion.refs_0_), channel_id=1, source_target_pairs={{0,4},{4,0},{8,12},{12,8},{16,20},{20,16},{24,28},{28,24},{1,5},{5... | collective-permute-start | bytes 983048 | tf_op jit(solution)/shard_map/ppermute | solution.py:279
  9.8 9.4 %all-to-all-start = ((bf16[4,32,1024]{2,1,0:T(8,128)(2,1)}), bf16[4,32,1024]{2,1,0:T(8,128)(2,1)S(1)}, u32[]{:S(2)}, u32[]{:S(2)}) async-start(bf16[4,32,1024]{2,1,0:T(8,128)(2,1)} %bitcast.4), calls=%async_computation | async-start | bytes 524288 | tf_op jit(solution)/shard_map/all_to_all | solution.py:292
  19.2 24.4 %collective-permute-start.9 = (bf16[768,768]{1,0:T(8,128)(2,1)S(1)}, bf16[768,768]{1,0:T(8,128)(2,1)}, u32[]{:S(2)}, u32[]{:S(2)}) collective-permute-start(bf16[768,768]{1,0:T(8,128)(2,1)S(1)} %bitcast_dynamic-update-slice_fusion), channel_id=1, source_target_pairs={{0,2},{4,6},{9,11},{13,15},{18,16},{22,20},{27,25},{31,29}} | collective-permute-start | bytes 3538952 | tf_op jit(solution)/shard_map/ppermute | solution.py:301
  22.5 13.5 %collective-permute-start.6 = (bf16[1280,128]{1,0:T(8,128)(2,1)S(1)}, bf16[1280,128]{1,0:T(8,128)(2,1)S(1)}, u32[]{:S(2)}, u32[]{:S(2)}) collective-permute-start(bf16[1280,128]{1,0:T(8,128)(2,1)S(1)} %collective-permute-done.1), channel_id=1, source_target_pairs={{8,0},{12,4},{16,24},{20,28},{9,1},{13,5},{17,25},{21,29},{10,2},{... | collective-permute-start | bytes 983048 | tf_op jit(solution)/shard_map/ppermute | solution.py:276
  24.5 11.5 %collective-permute-start.3 = (bf16[32,1024]{1,0:T(8,128)(2,1)S(1)}, bf16[32,1024]{1,0:T(8,128)(2,1)S(1)}, u32[]{:S(2)}, u32[]{:S(2)}) collective-permute-start(bf16[32,1024]{1,0:T(8,128)(2,1)S(1)} %get-tuple-element.46), channel_id=1, source_target_pairs={{0,8},{4,12},{8,0},{12,4},{16,24},{20,28},{24,16},{28,20},{1,9},{5... | collective-permute-start | bytes 196616 | tf_op jit(solution)/shard_map/ppermute | solution.py:276
  27.3 16.3 %collective-permute-start.7 = (bf16[1280,128]{1,0:T(8,128)(2,1)S(1)}, bf16[1280,128]{1,0:T(8,128)(2,1)}, u32[]{:S(2)}, u32[]{:S(2)}) collective-permute-start(bf16[1280,128]{1,0:T(8,128)(2,1)S(1)} %collective-permute-done.refs_1_), channel_id=1, source_target_pairs={{8,16},{12,20},{16,8},{20,12},{9,17},{13,21},{17,9},{21,13},{10,18... | collective-permute-start | bytes 983048 | tf_op jit(solution)/shard_map/ppermute | solution.py:276
  28.7 14.9 %collective-permute-start.8 = (bf16[1280,128]{1,0:T(8,128)(2,1)S(1)}, bf16[1280,128]{1,0:T(8,128)(2,1)S(1)}, u32[]{:S(2)}, u32[]{:S(2)}) collective-permute-start(bf16[1280,128]{1,0:T(8,128)(2,1)S(1)} %collective-permute-done.refs_1_), channel_id=1, source_target_pairs={{0,4},{4,0},{8,12},{12,8},{16,20},{20,16},{24,28},{28,24},{1,5},{5... | collective-permute-start | bytes 983048 | tf_op jit(solution)/shard_map/ppermute | solution.py:279
  36.1 10.7 %copy-start.8 = (bf16[32,1024]{1,0:T(8,128)(2,1)}, bf16[32,1024]{1,0:T(8,128)(2,1)S(1)}, u32[]{:S(2)}) copy-start(bf16[32,1024]{1,0:T(8,128)(2,1)S(1)} %collective-permute-done.3.refs_1_) | copy-start | bytes 196612
  36.1 7.5 %collective-permute-start.4 = (bf16[32,1024]{1,0:T(8,128)(2,1)}, bf16[32,1024]{1,0:T(8,128)(2,1)S(1)}, u32[]{:S(2)}, u32[]{:S(2)}) collective-permute-start(bf16[32,1024]{1,0:T(8,128)(2,1)} %get-tuple-element.45), channel_id=1, source_target_pairs={{0,16},{4,20},{8,24},{12,28},{16,0},{20,4},{24,8},{28,12},{1,17},{... | collective-permute-start | bytes 196616 | tf_op jit(solution)/shard_map/ppermute | solution.py:276
  36.1 7.5 %collective-permute-start.5 = (bf16[32,1024]{1,0:T(8,128)(2,1)}, bf16[32,1024]{1,0:T(8,128)(2,1)S(1)}, u32[]{:S(2)}, u32[]{:S(2)}) collective-permute-start(bf16[32,1024]{1,0:T(8,128)(2,1)} %get-tuple-element.44), channel_id=1, source_target_pairs={{0,24},{4,28},{8,16},{12,20},{16,8},{20,12},{24,0},{28,4},{1,25},{... | collective-permute-start | bytes 196616 | tf_op jit(solution)/shard_map/ppermute | solution.py:276
  44.2 11.8 %collective-permute-start.11 = (bf16[1280,128]{1,0:T(8,128)(2,1)}, bf16[1280,128]{1,0:T(8,128)(2,1)S(1)}, u32[]{:S(2)}, u32[]{:S(2)}) collective-permute-start(bf16[1280,128]{1,0:T(8,128)(2,1)} %collective-permute-done.7), channel_id=1, source_target_pairs={{8,0},{12,4},{16,24},{20,28},{9,1},{13,5},{17,25},{21,29},{10,2},{... | collective-permute-start | bytes 983048 | tf_op jit(solution)/shard_map/ppermute | solution.py:276
  46.7 11.8 %copy-start.13 = (s32[2,4]{1,0:T(2,128)S(1)}, s32[2,4]{1,0:T(2,128)}, u32[]{:S(2)}) copy-start(s32[2,4]{1,0:T(2,128)} %param.22) | copy-start | bytes 100
  46.7 11.8 %copy-start.11 = (f32[4,4]{1,0:T(4,128)S(1)}, f32[4,4]{1,0:T(4,128)}, u32[]{:S(2)}) copy-start(f32[4,4]{1,0:T(4,128)} %param.24) | copy-start | bytes 196
  46.7 14.6 %copy-start.12 = (f32[4]{0:T(128)S(1)}, f32[4]{0:T(128)}, u32[]{:S(2)}) copy-start(f32[4]{0:T(128)} %param.23) | copy-start | bytes 52
  46.7 18.1 %collective-permute-start.20 = (bf16[768,768]{1,0:T(8,128)(2,1)}, bf16[768,768]{1,0:T(8,128)(2,1)}, u32[]{:S(2)}, u32[]{:S(2)}) collective-permute-start(bf16[768,768]{1,0:T(8,128)(2,1)} %broadcast_select_fusion), channel_id=1, source_target_pairs={{0,1},{2,3},{4,5},{6,7},{9,8},{11,10},{13,12},{15,14},{16,17},{18,... | collective-permute-start | bytes 3538952 | tf_op jit(solution)/shard_map/ppermute | solution.py:311
  51.5 6.8 %collective-permute-start.10 = (bf16[128,1024]{1,0:T(8,128)(2,1)}, bf16[128,1024]{1,0:T(8,128)(2,1)S(1)}, u32[]{:S(2)}, u32[]{:S(2)}) collective-permute-start(bf16[128,1024]{1,0:T(8,128)(2,1)} %stack.12.refs_8_), channel_id=1, source_target_pairs={{0,4},{4,0},{8,12},{12,8},{16,20},{20,16},{24,28},{28,24},{1,5},{5... | collective-permute-start | bytes 786440 | tf_op jit(solution)/shard_map/ppermute | solution.py:279
  52.0 7.3 %collective-permute-start.14 = (bf16[128,1024]{1,0:T(8,128)(2,1)}, bf16[128,1024]{1,0:T(8,128)(2,1)S(1)}, u32[]{:S(2)}, u32[]{:S(2)}) collective-permute-start(bf16[128,1024]{1,0:T(8,128)(2,1)} %stack.12.refs_8_), channel_id=1, source_target_pairs={{0,2},{1,3},{2,0},{3,1},{4,6},{5,7},{6,4},{7,5},{8,10},{9,11},{10,... | collective-permute-start | bytes 786440 | tf_op jit(solution)/shard_map/ppermute | solution.py:316
  52.4 9.0 %collective-permute-start.15 = (bf16[128,1024]{1,0:T(8,128)(2,1)}, bf16[128,1024]{1,0:T(8,128)(2,1)S(1)}, u32[]{:S(2)}, u32[]{:S(2)}) collective-permute-start(bf16[128,1024]{1,0:T(8,128)(2,1)} %stack.12.refs_8_), channel_id=1, source_target_pairs={{0,1},{1,0},{2,3},{3,2},{4,5},{5,4},{6,7},{7,6},{8,9},{9,8},{10,11... | collective-permute-start | bytes 786440 | tf_op jit(solution)/shard_map/ppermute | solution.py:317
  58.3 6.5 %collective-permute-start.17 = (bf16[128,1024]{1,0:T(8,128)(2,1)S(1)}, bf16[128,1024]{1,0:T(8,128)(2,1)}, u32[]{:S(2)}, u32[]{:S(2)}) collective-permute-start(bf16[128,1024]{1,0:T(8,128)(2,1)S(1)} %collective-permute-done.10.refs_12_), channel_id=1, source_target_pairs={{0,2},{1,3},{2,0},{3,1},{4,6},{5,7},{6,4},{7,5},{8,10},{9,11},{10,... | collective-permute-start | bytes 786440 | tf_op jit(solution)/shard_map/ppermute | solution.py:316
  58.7 10.5 %collective-permute-start.12 = (bf16[1280,128]{1,0:T(8,128)(2,1)S(1)}, bf16[1280,128]{1,0:T(8,128)(2,1)S(1)}, u32[]{:S(2)}, u32[]{:S(2)}) collective-permute-start(bf16[1280,128]{1,0:T(8,128)(2,1)S(1)} %broadcast_select_fusion.3.refs_2_), channel_id=1, source_target_pairs={{0,4},{4,0},{8,12},{12,8},{16,20},{20,16},{24,28},{28,24},{1,5},{5... | collective-permute-start | bytes 983048 | tf_op jit(solution)/shard_map/ppermute | solution.py:279
  59.3 13.4 %collective-permute-start.13 = (bf16[1280,128]{1,0:T(8,128)(2,1)S(1)}, bf16[1280,128]{1,0:T(8,128)(2,1)S(1)}, u32[]{:S(2)}, u32[]{:S(2)}) collective-permute-start(bf16[1280,128]{1,0:T(8,128)(2,1)S(1)} %broadcast_select_fusion.2.refs_3_), channel_id=1, source_target_pairs={{0,4},{4,0},{8,12},{12,8},{16,20},{20,16},{24,28},{28,24},{1,5},{5... | collective-permute-start | bytes 983048 | tf_op jit(solution)/shard_map/ppermute | solution.py:279
  61.3 11.4 %copy-start = (f32[1,640,640]{2,1,0:T(8,128)S(1)}, f32[1,640,640]{2,1,0:T(8,128)}, u32[]{:S(2)}) copy-start(f32[1,640,640]{2,1,0:T(8,128)} %param.18) | copy-start | bytes 4915204
  61.3 11.4 %copy-start.1 = (f32[1,640,640]{2,1,0:T(8,128)S(1)}, f32[1,640,640]{2,1,0:T(8,128)}, u32[]{:S(2)}) copy-start(f32[1,640,640]{2,1,0:T(8,128)} %param.20) | copy-start | bytes 4915204
  61.4 11.4 %copy-start.2 = (bf16[128,1024]{1,0:T(8,128)(2,1)S(1)}, bf16[128,1024]{1,0:T(8,128)(2,1)}, u32[]{:S(2)}) copy-start(bf16[128,1024]{1,0:T(8,128)(2,1)} %stack.12.refs_8_) | copy-start | bytes 786436
  61.4 7.8 %collective-permute-start.16 = (bf16[128,1024]{1,0:T(8,128)(2,1)S(1)}, bf16[128,1024]{1,0:T(8,128)(2,1)S(1)}, u32[]{:S(2)}, u32[]{:S(2)}) collective-permute-start(bf16[128,1024]{1,0:T(8,128)(2,1)S(1)} %collective-permute-done.14.refs_9_), channel_id=1, source_target_pairs={{0,1},{1,0},{2,3},{3,2},{4,5},{5,4},{6,7},{7,6},{8,9},{9,8},{10,11... | collective-permute-start | bytes 786440 | tf_op jit(solution)/shard_map/ppermute | solution.py:317
  64.8 4.4 %collective-permute-start.18 = (bf16[128,1024]{1,0:T(8,128)(2,1)S(1)}, bf16[128,1024]{1,0:T(8,128)(2,1)S(1)}, u32[]{:S(2)}, u32[]{:S(2)}) collective-permute-start(bf16[128,1024]{1,0:T(8,128)(2,1)S(1)} %collective-permute-done.10.refs_12_), channel_id=1, source_target_pairs={{0,1},{1,0},{2,3},{3,2},{4,5},{5,4},{6,7},{7,6},{8,9},{9,8},{10,11... | collective-permute-start | bytes 786440 | tf_op jit(solution)/shard_map/ppermute | solution.py:317
  64.8 7.9 %collective-permute-start.19 = (bf16[128,1024]{1,0:T(8,128)(2,1)}, bf16[128,1024]{1,0:T(8,128)(2,1)S(1)}, u32[]{:S(2)}, u32[]{:S(2)}) collective-permute-start(bf16[128,1024]{1,0:T(8,128)(2,1)} %collective-permute-done.17.refs_13_), channel_id=1, source_target_pairs={{0,1},{1,0},{2,3},{3,2},{4,5},{5,4},{6,7},{7,6},{8,9},{9,8},{10,11... | collective-permute-start | bytes 786440 | tf_op jit(solution)/shard_map/ppermute | solution.py:317
  95.1 14.9 %all-to-all-start.1 = ((f32[32,1,256]{2,1,0:T(1,128)}), f32[32,1,256]{2,1,0:T(1,128)S(1)}, u32[]{:S(2)}, u32[]{:S(2)}) async-start(f32[32,1,256]{2,1,0:T(1,128)} %broadcast_in_dim.30), calls=%async_computation.1 | async-start | bytes 65536 | tf_op jit(solution)/shard_map/all_to_all | solution.py:370
  (5 other events, 4.8 us)

commit v4 on v3

--- a/solution.py
+++ b/solution.py
@@ -40,25 +40,24 @@
 def tile_kernel(count, quarters, in_width, widths, sc, where_ref, *refs):
     parts, blocks = refs[:count], refs[count:count + 2 * quarters]
     refs = refs[count + 2 * quarters:]
-    prev_kv, prev_up, packed, o_kv, o_up, t_ref = refs[:6]
+    prev_kv, prev_up, packed, to_kv, to_up, t_ref = refs[:6]
     at, g, m_a, y_a, low, rt = refs[6:12]
     factor_refs = refs[12:18]
-    pg_kv, pg_up, pa_kv, pa_up, packed_in, g_sems, p_sems, a_sems = refs[18:]
+    pg_kv, pg_up, pa_kv, pa_up, packed_in, o_kv, o_up, g_sems, p_sems, a_sems, o_sems = refs[18:]
     slot = where_ref[0]
     chunk = parts[0].shape[1]
-    piece = chunk // quarters
-    loads_g, loads_a = [], []
+    z = lax.axis_index("dp") // 2
+    inner = ((z == 1) | (z == 2)).astype(jnp.int32)
+    origins = [jnp.bitwise_xor(z, k) for k in (0, 1, 2 + inner, 3 - inner)]
+    loads_g = [
+        pltpu.make_async_copy(blocks[quarters * row + q], g.at[row, :, q], g_sems.at[quarters * row + q])
+        for row in range(2)
+        for q in range(quarters)
+    ]
+    loads_a = []
     for m in range(count):
-        for q in range(quarters):
-            k = m % (count // 2)
-            loads_g.append(
-                pltpu.make_async_copy(
-                    blocks[q + quarters * (2 * m // count)].at[piece * k:piece * (k + 1), :],
-                    g.at[chunk * m + piece * q:chunk * m + piece * (q + 1), :],
-                    g_sems.at[quarters * m + q],
-                )
-            )
-        loads_a.append(pltpu.make_async_copy(parts[m], at.at[:, chunk * m:chunk * (m + 1)], a_sems.at[m]))
+        lane = pl.multiple_of((count // 2 * (m // (count // 2)) + origins[m % (count // 2)]) * chunk, chunk)
+        loads_a.append(pltpu.make_async_copy(parts[m], at.at[:, pl.ds(lane, chunk)], a_sems.at[m]))
     loads_p = [
         pltpu.make_async_copy(source, target, p_sems.at[i])
         for i, (source, target) in enumerate(((packed, packed_in), (prev_kv, pa_kv), (prev_up, pa_up)))
@@ -74,12 +73,12 @@
     for load in loads_g:
         load.wait()
 
-    begin = 0
+    begin, stores = 0, []
     for linear, (pa, pg, out) in enumerate(((pa_kv, pg_kv, o_kv), (pa_up, pg_up, o_up))):
         width, cols = widths[linear], out.shape[1]
         m_g, y_g, i_g = factor_refs[3 * linear:3 * linear + 3]
         fa, fg = 2 * linear, 2 * linear + 1
-        part = lambda s, w, begin=begin: g[:, begin + s:begin + s + w]
+        part = lambda s, w, begin=begin: g[:, :, :, :, begin + s:begin + s + w].reshape(-1, w)
         squares = damped_into(
             m_g, lambda s, w: contract(part(0, width), part(s, w), 0, 0), pg, sc[0, fg], sc[1, fg], sc[2, fg]
         )
@@ -117,11 +116,15 @@
             out[:, s:s + w] = pre
             own_low = low[:, pl.ds(pl.multiple_of(first + s, 128), w)].astype(F32)
             total = total + jnp.sum(pre * own_low, keepdims=True)
-        t_ref[linear:linear + 1, :] = jnp.broadcast_to(total, (1, 128))
+        t_ref[:, :, 128 * linear:128 * (linear + 1)] = jnp.broadcast_to(total[None], (t_ref.shape[0], 1, 128))
+        stores.append(pltpu.make_async_copy(out, (to_kv, to_up)[linear], o_sems.at[linear]))
+        stores[-1].start()
         begin += width
-
-
-def tile(sc, where, parts, blocks, pa_kv, pa_up, packed, widths, cols):
+    for store in stores:
+        store.wait()
+
+
+def tile(devices, sc, where, parts, blocks, pa_kv, pa_up, packed, widths, cols):
     count, quarters = len(parts), len(blocks) // 2
     in_width = pa_kv.shape[0]
     tokens = parts[0].shape[1] * count
@@ -135,13 +138,13 @@
         out_shape=(
             jax.ShapeDtypeStruct((in_width, cols[0]), F32),
             jax.ShapeDtypeStruct((in_width, cols[1]), F32),
-            jax.ShapeDtypeStruct((2, 128), F32),
+            jax.ShapeDtypeStruct((devices, 1, 256), F32),
         ),
         in_specs=[smem, smem] + [anywhere] * (count + 2 * quarters + 3),
-        out_specs=(vmem, vmem, vmem),
+        out_specs=(pl.BlockSpec(memory_space=pltpu.HBM),) * 2 + (vmem,),
         scratch_shapes=[
             pltpu.VMEM((2 * in_width, tokens), BF),
-            pltpu.VMEM((tokens, sum(widths)), BF),
+            pltpu.VMEM((2, count // 2, quarters, tokens // (count * quarters), sum(widths)), BF),
             pltpu.VMEM((in_width, in_width), F32),
             pltpu.VMEM((in_width, in_width), BF),
             pltpu.VMEM((in_width, max(widths)), BF),
@@ -151,50 +154,83 @@
         + [pltpu.VMEM((w, w), BF) for w in widths]
         + [pltpu.VMEM((in_width, in_width), F32)] * 2
         + [pltpu.VMEM(packed.shape, BF)]
-        + [pltpu.SemaphoreType.DMA((n,)) for n in (count * quarters, 3, count)],
+        + [pltpu.VMEM((in_width, c), F32) for c in cols]
+        + [pltpu.SemaphoreType.DMA((n,)) for n in (2 * quarters, 3, count, 2)],
         compiler_params=pltpu.CompilerParams(vmem_limit_bytes=32 * 2**20),
         name="tile",
     )(sc, where, *parts, *blocks, pa_kv, pa_up, packed)
 
 
-def stack_kernel(*refs):
-    *sources, out = refs
-    rows = sources[0].shape[0]
-    z = lax.axis_index("dp") // 2
-    inner = (z == 1) | (z == 2)
-    for i in range(2):
-        out[rows * i:rows * (i + 1), :] = sources[i][...]
-        out[rows * (2 + i):rows * (3 + i), :] = jnp.where(inner, sources[3 - i][...], sources[2 + i][...])
-
-
-def stack_rows(parts):
-    rows, cols = parts[0].shape
+def turn_kernel(kv_ref, up_ref, g_kv, g_up, out_ref, g_ref):
+    own = lax.axis_index("own")
+    rows, width = kv_ref.shape
+    piece = rows // 4
+    edge = g_kv.shape[1]
+    g_ref[:, :edge] = g_kv[...]
+    g_ref[:, edge:] = g_up[...]
+    for i, ref in enumerate((kv_ref, up_ref)):
+        for s, w in tiles(width):
+            quarters = [
+                ref[pl.ds(pl.multiple_of(jnp.bitwise_xor(own, q) * piece, piece), piece), s:s + w] for q in (0, 2, 1, 3)
+            ]
+            out_ref[width * i + s:width * i + s + w, :] = jnp.concatenate(quarters, 0).T
+
+
+def turned(acts, grads):
+    rows, width = acts[0].shape
     vmem = pl.BlockSpec(memory_space=pltpu.VMEM)
     return pl.pallas_call(
-        stack_kernel,
-        out_shape=jax.ShapeDtypeStruct((rows * len(parts), cols), parts[0].dtype),
-        in_specs=[vmem] * len(parts),
-        out_specs=vmem,
-        name="stack",
-    )(*parts)
-
-
-def update_kernel(entries, step_ref, sums_ref, p_kv, p_up, w_kv, w_up, n_kv, n_up):
-    totals = jnp.sum(sums_ref[...], axis=0, keepdims=True)
+        turn_kernel,
+        out_shape=(
+            jax.ShapeDtypeStruct((2 * width, rows), BF),
+            jax.ShapeDtypeStruct((rows, sum(v.shape[1] for v in grads)), BF),
+        ),
+        in_specs=[vmem] * 4,
+        out_specs=(vmem, vmem),
+        name="turn",
+    )(*acts, *grads)
+
+
+def update_kernel(entries, step_ref, sums_any, p_kv, p_up, w_kv, w_up, n_kv, n_up, sums, *refs):
+    values, (sums_sem, load_sems, store_sems) = refs[:6], refs[6:]
+    sums_load = pltpu.make_async_copy(sums_any, sums, sums_sem)
+    sums_load.start()
+    jobs = []
     for linear, (p, w, n) in enumerate(((p_kv, w_kv, n_kv), (p_up, w_up, n_up))):
-        total = totals[:, 128 * linear:128 * (linear + 1)]
-        factor = step_ref[0] * jnp.sqrt(entries[linear] / total)
         for s, width in tiles(p.shape[1], 128):
-            n[:, s:s + width] = w[:, s:s + width] - factor[:, :width] * p[:, s:s + width]
+            part, at = len(jobs), (slice(None), slice(s, s + width))
+            p_in, w_in, out = (v.at[at] for v in values[3 * linear:3 * linear + 3])
+            loads = [
+                pltpu.make_async_copy(p.at[at], p_in, load_sems.at[2 * part]),
+                pltpu.make_async_copy(w.at[at], w_in, load_sems.at[2 * part + 1]),
+            ]
+            for load in loads:
+                load.start()
+            jobs.append((linear, loads, p_in, w_in, out, pltpu.make_async_copy(out, n.at[at], store_sems.at[part])))
+    sums_load.wait()
+    totals = jnp.sum(sums[...], axis=0)
+    factors = [step_ref[0] * jnp.sqrt(entries[i] / totals[:, 128 * i:128 * (i + 1)]) for i in range(2)]
+    for linear, loads, p_in, w_in, out, store in jobs:
+        for load in loads:
+            load.wait()
+        out[...] = w_in[...] - factors[linear][:, :out.shape[1]] * p_in[...]
+        store.start()
+    for job in jobs:
+        job[-1].wait()
 
 
 def update(entries, step_size, sums, p_kv, p_up, w_kv, w_up):
-    vmem, smem = pl.BlockSpec(memory_space=pltpu.VMEM), pl.BlockSpec(memory_space=pltpu.SMEM)
+    smem, anywhere = pl.BlockSpec(memory_space=pltpu.SMEM), pl.BlockSpec(memory_space=pl.ANY)
+    hbm = pl.BlockSpec(memory_space=pltpu.HBM)
+    parts = sum(len(tiles(w.shape[1], 128)) for w in (w_kv, w_up))
     return pl.pallas_call(
         functools.partial(update_kernel, entries),
         out_shape=(jax.ShapeDtypeStruct(w_kv.shape, F32), jax.ShapeDtypeStruct(w_up.shape, F32)),
-        in_specs=[smem] + [vmem] * 5,
-        out_specs=(vmem, vmem),
+        in_specs=[smem, anywhere, hbm, hbm, hbm, hbm],
+        out_specs=(hbm, hbm),
+        scratch_shapes=[pltpu.VMEM(sums.shape, F32)]
+        + [pltpu.VMEM(w.shape, F32) for w in (w_kv, w_up) for _ in range(3)]
+        + [pltpu.SemaphoreType.DMA, pltpu.SemaphoreType.DMA((2 * parts,)), pltpu.SemaphoreType.DMA((parts,))],
         name="update",
     )(step_size.reshape(1), sums, p_kv, p_up, w_kv, w_up)
 
@@ -262,6 +298,7 @@
 def gather_fast(acts, grads, prev_low):
     dp, own = lax.axis_index("dp"), lax.axis_index("own")
     z, x = dp // 2, own // 2
+    mine, grads = turned(acts, grads)
     rows, cols = grads.shape
     piece = rows // 4
     both = ("dp", "own")
@@ -269,8 +306,6 @@
     dp_swap = lambda m: [(d, d ^ m) for d in range(8)]
     own_swap = lambda m: [(o, o ^ m) for o in range(4)]
 
-    order = [jnp.bitwise_xor(own, q) for q in (0, 2, 1, 3)]
-    mine = jnp.concatenate([lax.dynamic_slice_in_dim(acts, piece * q, piece, 0) for q in order], 0).T
 
     def along_z(value, pairs):
         return lax.ppermute(value, "dp", [(2 * s + y, 2 * t + y) for s, t in pairs for y in range(2)])
@@ -293,35 +328,36 @@
     near, cross_a, beside = along_z(mine, pairs), along_z(mine, middle), across_y(mine)
     split, near, cross_a, beside, prev_low = phase((split, near, cross_a, beside, prev_low))
 
-    wanted = [lax.dynamic_index_in_dim(split, jnp.bitwise_xor(z, k), 0, keepdims=False) for k in range(4)]
-    rows_z = [wanted[0]] + [along_z(wanted[k], [(s, s ^ k) for s in range(4)]) for k in (1, 2, 3)]
+    z_lines = [[2 * s + y for s in range(4)] for y in range(2)]
+    strip = lax.all_to_all(split, "dp", 0, 0, tiled=True, axis_index_groups=z_lines)
     far_a = jnp.where(inner, cross_a, along_z(cross_a, outward))
     cross_b = along_z(near, middle)
     near_y = across_y(near)
     prev_x = lax.ppermute(prev_low, both, sends_x)
-    rows_z, far_a, cross_b, near_y, prev_x = phase((rows_z, far_a, cross_b, near_y, prev_x))
-
-    strip = stack_rows(rows_z)
+    strip, far_a, cross_b, near_y, prev_x = phase((strip, far_a, cross_b, near_y, prev_x))
+
     strip_y = across_y(strip)
+    far_a_y = across_y(far_a)
     far_b = jnp.where(inner, cross_b, along_z(cross_b, outward))
-    far_a_y = across_y(far_a)
+    strip_x = lax.ppermute(strip, "own", own_swap(2))
     prev_low = jnp.where(x == z // 2, prev_low, prev_x)
-    strip_y, far_b = phase((strip_y, far_b))
-
     prev_core = lax.ppermute(prev_low, both, sends_core)
+    strip, strip_y, far_b = phase((strip, strip_y, far_b))
+
+    far_b_y = across_y(far_b)
+    strip_xy = lax.ppermute(strip_y, "own", own_swap(2))
     prev_low = jnp.where((own & 1) == (z & 1), prev_low, prev_core)
-    far_b_y = across_y(far_b)
     blocks = []
-    for v in (strip, strip_y):
-        w = lax.ppermute(v, "own", own_swap(2))
+    for v, w in ((strip, strip_x), (strip_y, strip_xy)):
         blocks += [v, w, lax.ppermute(v, "own", own_swap(1)), lax.ppermute(w, "own", own_swap(1))]
     return [mine, near, far_a, far_b, beside, near_y, far_a_y, far_b_y], blocks, prev_low
 
 
 def gather_any(acts, grads, prev_low, block_index):
     dp_count, own_count = lax.axis_size("dp"), lax.axis_size("own")
+    grads = jnp.concatenate(grads, 1)
     rows, cols = grads.shape
-    acts_all = lax.all_gather(acts, "dp", axis=0, tiled=True)
+    acts_all = lax.all_gather(jnp.concatenate(acts, 1), "dp", axis=0, tiled=True)
     split = lax.all_to_all(grads.reshape(own_count, rows // own_count, cols), "own", 0, 0, tiled=True)
     wanted = jnp.repeat(split, dp_count // own_count, axis=0)
     pieces = lax.all_to_all(wanted, "dp", 0, 0, tiled=True)
@@ -343,8 +379,8 @@
     cols = (weights_kv.shape[1], weights_up.shape[1])
     entries = tuple(float(w.shape[0] * w.shape[1] * dp_count * own_count) for w in (weights_kv, weights_up))
 
-    acts = jnp.concatenate([acts_kv, acts_up], 1)
-    grads = jnp.concatenate([grads_kv, grads_up], 1)
+    acts = (acts_kv, acts_up)
+    grads = (grads_kv, grads_up)
     prev_g = [prev_g_kv[0].astype(BF), prev_g_up[0].astype(BF)]
     prev_a = (prev_a_kv[0], prev_a_up[0])
     if (dp_count, own_count) == (8, 4):
@@ -359,14 +395,14 @@
         sc = jnp.stack(
             [jnp.where(fresh, 0.5, 1.0), jnp.where(fresh, 0.5 / total, 0.0), damping, scale, jnp.full((4,), 1.0 / total)]
         )
-        p_kv, p_up, terms = tile(
-            sc, slot[None].astype(jnp.int32), parts, blocks, *prev_a, packed,
+        p_kv, p_up, sent = tile(
+            dp_count * own_count, sc, slot[None].astype(jnp.int32), parts, blocks, *prev_a, packed,
             tuple(p.shape[0] for p in prev_g), cols
         )
     else:
         acts_all, block, prevs = gather_any(acts, grads, prev_g, block_index)
         p_kv, p_up, terms = tile_any(acts_all, block, prevs, prev_a, owners, damping, init_scale, block_index, cols)
-    sent = jnp.broadcast_to(terms.reshape(1, 256), (dp_count * own_count, 256))
+        sent = jnp.broadcast_to(terms.reshape(1, 1, 256), (dp_count * own_count, 1, 256))
     sums = lax.all_to_all(sent, ("dp", "own"), 0, 0, tiled=True)
     return update(entries, step_size, sums, p_kv, p_up, weights_kv, weights_up)
 

time: 114 us -> 105 us (0.921)
  local copies, waits for them, and re-layouts: 6.67 us -> 2.58 us
  starting transfers between devices: 36.2 us -> 33.6 us
  other arithmetic: 6.11 us -> 4.47 us
    ppermute x8 -> x5, waiting for transfers between devices: 16 us -> 6.8 us  [along_z(): lax.ppermute(value, 'dp', [(2 * s + y, 2 * t + y) for s, t in pairs for y...]
    all_to_all x0 -> x1, waiting for transfers between devices: none -> 9.18 us  [gather_fast(): lax.all_to_all(split, 'dp', 0, 0, tiled=True, axis_index_groups=z_lines)]
    all_to_all x0 -> x1, starting transfers between devices: none -> 6.09 us  [gather_fast(): lax.all_to_all(split, 'dp', 0, 0, tiled=True, axis_index_groups=z_lines)]
    ppermute x8 -> x5, starting transfers between devices: 12.4 us -> 7.67 us  [along_z(): lax.ppermute(value, 'dp', [(2 * s + y, 2 * t + y) for s, t in pairs for y...]
    all_to_all x1, starting transfers between devices: 7.61 us -> 3.75 us  [shards(): sums = lax.all_to_all(sent, ('dp', 'own'), 0, 0, tiled=True)]
    ppermute x2, waiting for transfers between devices: 3.32 us -> 0.01 us  [the longest x1 0.01 us: gather_fast(): strip_xy = lax.ppermute(strip_y, 'own', own_swap(2))]
    ppermute x5, waiting for transfers between devices: 8.28 us -> 11.3 us  [across_y(): return lax.ppermute(value, 'dp', dp_swap(1))]
    unnamed x31 -> x20, local copies, waits for them, and re-layouts: 5.12 us -> 2.34 us
  transfers between devices with their start and end apart: 23 -> 21, of which waited for: 9 -> 8; matrix products, arithmetic and copies ran while one was open for 5% -> 5% of each run, Pallas kernels for 1% -> 0%
where the time goes in v4:
time: 105 us; the launch traced here: 104 us
  waiting for transfers between devices  38.1 us (36%)
  starting transfers between devices  33.6 us (32%)
  Pallas kernels  23.6 us (22%)
  other arithmetic  4.47 us (4%)
  local copies, waits for them, and re-layouts  2.58 us (2%)
  between operations  1.72 us (2%)
    pallas_call x1, Pallas kernels, tile(): pl.pallas_call(functools.partial(tile_kernel, count, quarters, in_width,...  18.9 us
    ppermute x5, waiting for transfers between devices, across_y(): return lax.ppermute(value, 'dp', dp_swap(1))  11.3 us
    all_to_all x1, waiting for transfers between devices, gather_fast(): lax.all_to_all(split, 'dp', 0, 0, tiled=True, axis_index_groups=z_lines)  9.18 us
    ppermute x5, starting transfers between devices, along_z(): lax.ppermute(value, 'dp', [(2 * s + y, 2 * t + y) for s, t in pairs for y...  7.67 us
    ppermute x5, waiting for transfers between devices, along_z(): lax.ppermute(value, 'dp', [(2 * s + y, 2 * t + y) for s, t in pairs for y...  6.8 us
    all_to_all x1, waiting for transfers between devices, shards(): sums = lax.all_to_all(sent, ('dp', 'own'), 0, 0, tiled=True)  6.6 us
    all_to_all x1, starting transfers between devices, gather_fast(): lax.all_to_all(split, 'dp', 0, 0, tiled=True, axis_index_groups=z_lines)  6.09 us
    ppermute x5, starting transfers between devices, across_y(): return lax.ppermute(value, 'dp', dp_swap(1))  4.7 us
  transfers between devices with their start and end apart: 21, of which 8 were waited for; matrix products, arithmetic and copies ran while one was open for 5% of the time, Pallas kernels for 0%

profile of v4, /device:TPU:0, one launch (start us, length us, event | category | flops | bytes accessed | tf_op | source)
XLA Modules:
  0.0 104.1 jit_solution(1369361527904715204)
XLA Ops:
  0.6 2.0 %turn.1 = (bf16[1280,128]{1,0:T(8,128)(2,1)}, bf16[128,1024]{1,0:T(8,128)(2,1)}) custom-call(bf16[128,640]{1,0:T(8,128)(2,1)} %kv_ref.1, bf16[128,640]{1,0:T(8,128)(2,1)} %up_ref.1, bf16[128,256]{1,0:T(8,128)(2,1)} %g_kv.1, bf16[128,768]{1,0:T(8,128)(2,1)} %g_up.1), custom_call_target="tpu_custom_call" | custom-call | tf_op jit(solution)/shard_map/turn/pallas_call | solution.py:182
  2.7 3.0 %collective-permute-start = (bf16[1280,128]{1,0:T(8,128)(2,1)}, bf16[1280,128]{1,0:T(8,128)(2,1)S(1)}, u32[]{:S(2)}, u32[]{:S(2)}) collective-permute-start(bf16[1280,128]{1,0:T(8,128)(2,1)} %get-tuple-element.20.refs_0_), channel_id=1, source_target_pairs={{0,8},{4,12},{8,0},{12,4},{16,24},{20,28},{24,16},{28,20},{1,9},{5... | collective-permute-start | bytes 983048 | tf_op jit(solution)/shard_map/ppermute | solution.py:311
  5.7 0.7 collective-permute-start.1
  6.4 1.6 %collective-permute-start.2 = (bf16[1280,128]{1,0:T(8,128)(2,1)}, bf16[1280,128]{1,0:T(8,128)(2,1)S(1)}, u32[]{:S(2)}, u32[]{:S(2)}) collective-permute-start(bf16[1280,128]{1,0:T(8,128)(2,1)} %get-tuple-element.20.refs_0_), channel_id=1, source_target_pairs={{0,4},{4,0},{8,12},{12,8},{16,20},{20,16},{24,28},{28,24},{1,5},{5... | collective-permute-start | bytes 983048 | tf_op jit(solution)/shard_map/ppermute | solution.py:314
  7.9 4.1 %all-to-all-start = ((bf16[4,32,1024]{2,1,0:T(8,128)(2,1)}), bf16[4,32,1024]{2,1,0:T(8,128)(2,1)}, u32[]{:S(2)}, u32[]{:S(2)}) async-start(bf16[4,32,1024]{2,1,0:T(8,128)(2,1)} %bitcast.17), calls=%async_computation | async-start | bytes 524288 | tf_op jit(solution)/shard_map/all_to_all | solution.py:327
  12.0 1.8 %convert_bitcast_fusion = bf16[768,768]{1,0:T(8,128)(2,1)S(1)} fusion(f32[1,768,768]{2,1,0:T(8,128)} %param.21), kind=kLoop, calls=%fused_computation | loop fusion | flops 589824 | bytes 3538944 | tf_op jit(solution)/shard_map/convert_element_type | solution.py:384
  13.9 4.2 %all-to-all-done = bf16[4,32,1024]{2,1,0:T(8,128)(2,1)} async-done(((bf16[4,32,1024]{2,1,0:T(8,128)(2,1)}), bf16[4,32,1024]{2,1,0:T(8,128)(2,1)}, u32[]{:S(2)}, u32[]{:S(2)}) %all-to-all-start) | async-done | bytes 262176 | tf_op jit(solution)/shard_map/all_to_all | solution.py:327
  18.1 3.3 %collective-permute-start.6 = (bf16[768,768]{1,0:T(8,128)(2,1)S(1)}, bf16[768,768]{1,0:T(8,128)(2,1)}, u32[]{:S(2)}, u32[]{:S(2)}) collective-permute-start(bf16[768,768]{1,0:T(8,128)(2,1)S(1)} %bitcast_dynamic-update-slice_fusion), channel_id=1, source_target_pairs={{0,2},{4,6},{9,11},{13,15},{18,16},{22,20},{27,25},{31,29}} | collective-permute-start | bytes 3538952 | tf_op jit(solution)/shard_map/ppermute | solution.py:336
  21.4 1.3 %collective-permute-start.3 = (bf16[1280,128]{1,0:T(8,128)(2,1)S(1)}, bf16[1280,128]{1,0:T(8,128)(2,1)S(1)}, u32[]{:S(2)}, u32[]{:S(2)}) collective-permute-start(bf16[1280,128]{1,0:T(8,128)(2,1)S(1)} %collective-permute-done.1), channel_id=1, source_target_pairs={{8,0},{12,4},{16,24},{20,28},{9,1},{13,5},{17,25},{21,29},{10,2},{... | collective-permute-start | bytes 983048 | tf_op jit(solution)/shard_map/ppermute | solution.py:311
  22.8 1.4 %collective-permute-start.4 = (bf16[1280,128]{1,0:T(8,128)(2,1)S(1)}, bf16[1280,128]{1,0:T(8,128)(2,1)}, u32[]{:S(2)}, u32[]{:S(2)}) collective-permute-start(bf16[1280,128]{1,0:T(8,128)(2,1)S(1)} %collective-permute-done.refs_1_), channel_id=1, source_target_pairs={{8,16},{12,20},{16,8},{20,12},{9,17},{13,21},{17,9},{21,13},{10,18... | collective-permute-start | bytes 983048 | tf_op jit(solution)/shard_map/ppermute | solution.py:311
  24.2 0.5 collective-permute-start.5
  24.7 6.1 %all-to-all-start.1 = ((bf16[4,32,1024]{2,1,0:T(8,128)(2,1)}), bf16[4,32,1024]{2,1,0:T(8,128)(2,1)S(1)}, u32[]{:S(2)}, u32[]{:S(2)}) async-start(bf16[4,32,1024]{2,1,0:T(8,128)(2,1)} %all-to-all-done), calls=%async_computation.1 | async-start | bytes 524288 | tf_op jit(solution)/shard_map/all_to_all | solution.py:332
  30.8 2.8 %collective-permute-done.3 = bf16[1280,128]{1,0:T(8,128)(2,1)S(1)} collective-permute-done((bf16[1280,128]{1,0:T(8,128)(2,1)S(1)}, bf16[1280,128]{1,0:T(8,128)(2,1)S(1)}, u32[]{:S(2)}, u32[]{:S(2)}) %collective-permute-start.3) | collective-permute-done | bytes 327712 | tf_op jit(solution)/shard_map/ppermute | solution.py:311
  33.7 9.2 %all-to-all-done.1.refs_8_ = bf16[4,32,1024]{2,1,0:T(8,128)(2,1)S(1)} async-done(((bf16[4,32,1024]{2,1,0:T(8,128)(2,1)}), bf16[4,32,1024]{2,1,0:T(8,128)(2,1)S(1)}, u32[]{:S(2)}, u32[]{:S(2)}) %all-to-all-start.1) | async-done | bytes 262176 | tf_op jit(solution)/shard_map/all_to_all | solution.py:332
  42.8 1.3 %collective-permute-start.8 = (bf16[1280,128]{1,0:T(8,128)(2,1)}, bf16[1280,128]{1,0:T(8,128)(2,1)S(1)}, u32[]{:S(2)}, u32[]{:S(2)}) collective-permute-start(bf16[1280,128]{1,0:T(8,128)(2,1)} %collective-permute-done.4), channel_id=1, source_target_pairs={{8,0},{12,4},{16,24},{20,28},{9,1},{13,5},{17,25},{21,29},{10,2},{... | collective-permute-start | bytes 983048 | tf_op jit(solution)/shard_map/ppermute | solution.py:311
  44.1 1.2 %broadcast_select_fusion = bf16[768,768]{1,0:T(8,128)(2,1)} fusion(bf16[768,768]{1,0:T(8,128)(2,1)S(1)} %bitcast_dynamic-update-slice_fusion, bf16[768,768]{1,0:T(8,128)(2,1)} %collective-permute-done.6, pred[]{:T(512)S(6)} %eq.36), kind=kLoop, calls=%fused_computation.1 | loop fusion | flops 589824 | bytes 3538945 | tf_op jit(solution)/shard_map/jit(_where)/select_n | solution.py:343
  45.3 3.1 %collective-permute-start.17 = (bf16[768,768]{1,0:T(8,128)(2,1)}, bf16[768,768]{1,0:T(8,128)(2,1)}, u32[]{:S(2)}, u32[]{:S(2)}) collective-permute-start(bf16[768,768]{1,0:T(8,128)(2,1)} %broadcast_select_fusion), channel_id=1, source_target_pairs={{0,1},{2,3},{4,5},{6,7},{9,8},{11,10},{13,12},{15,14},{16,17},{18,... | collective-permute-start | bytes 3538952 | tf_op jit(solution)/shard_map/ppermute | solution.py:344
  49.1 1.5 %collective-permute-start.9 = (bf16[1280,128]{1,0:T(8,128)(2,1)S(1)}, bf16[1280,128]{1,0:T(8,128)(2,1)S(1)}, u32[]{:S(2)}, u32[]{:S(2)}) collective-permute-start(bf16[1280,128]{1,0:T(8,128)(2,1)S(1)} %broadcast_select_fusion.3.refs_2_), channel_id=1, source_target_pairs={{0,4},{4,0},{8,12},{12,8},{16,20},{20,16},{24,28},{28,24},{1,5},{5... | collective-permute-start | bytes 983048 | tf_op jit(solution)/shard_map/ppermute | solution.py:314
  50.6 4.0 %collective-permute-done.8 = bf16[1280,128]{1,0:T(8,128)(2,1)S(1)} collective-permute-done((bf16[1280,128]{1,0:T(8,128)(2,1)}, bf16[1280,128]{1,0:T(8,128)(2,1)S(1)}, u32[]{:S(2)}, u32[]{:S(2)}) %collective-permute-start.8) | collective-permute-done | bytes 327712 | tf_op jit(solution)/shard_map/ppermute | solution.py:311
  54.7 2.9 %collective-permute-done.7.refs_12_ = bf16[4,32,1024]{2,1,0:T(8,128)(2,1)S(1)} collective-permute-done((bf16[4,32,1024]{2,1,0:T(8,128)(2,1)S(1)}, bf16[4,32,1024]{2,1,0:T(8,128)(2,1)S(1)}, u32[]{:S(2)}, u32[]{:S(2)}) %collective-permute-start.7) | collective-permute-done | bytes 262176 | tf_op jit(solution)/shard_map/ppermute | solution.py:314
  57.9 0.6 collective-permute-start.10
  58.6 6.0 %collective-permute-done.9.refs_6_ = bf16[1280,128]{1,0:T(8,128)(2,1)S(1)} collective-permute-done((bf16[1280,128]{1,0:T(8,128)(2,1)S(1)}, bf16[1280,128]{1,0:T(8,128)(2,1)S(1)}, u32[]{:S(2)}, u32[]{:S(2)}) %collective-permute-start.9) | collective-permute-done | bytes 327712 | tf_op jit(solution)/shard_map/ppermute | solution.py:314
  64.6 0.5 collective-permute-start.12
  65.2 1.4 %broadcast_select_fusion.1.refs_18_ = bf16[768,768]{1,0:T(8,128)(2,1)S(1)} fusion(bf16[768,768]{1,0:T(8,128)(2,1)} %broadcast_select_fusion, bf16[768,768]{1,0:T(8,128)(2,1)} %collective-permute-done.17, pred[]{:T(512)S(6)} %eq.35), kind=kLoop, calls=%fused_computation.2 | loop fusion | flops 589824 | bytes 3538945 | tf_op jit(solution)/shard_map/jit(_where)/select_n | solution.py:349
  66.6 2.4 %collective-permute-done.10.refs_7_ = bf16[1280,128]{1,0:T(8,128)(2,1)S(1)} collective-permute-done((bf16[1280,128]{1,0:T(8,128)(2,1)S(1)}, bf16[1280,128]{1,0:T(8,128)(2,1)S(1)}, u32[]{:S(2)}, u32[]{:S(2)}) %collective-permute-start.10) | collective-permute-done | bytes 327712 | tf_op jit(solution)/shard_map/ppermute | solution.py:314
  69.0 18.9 %tile.1 = (f32[640,128]{1,0:T(8,128)S(1)}, f32[640,384]{1,0:T(8,128)S(1)}, f32[32,1,256]{2,1,0:T(1,128)}) custom-call(f32[5,4]{1,0:T(8,128)S(1)} %stack.10.sc, s32[1]{0:T(128)} %bitcast.2.where_ref, bf16[1280,128]{1,0:T(8,128)(2,1)S(1)} %copy-done.3, bf16[1280,128]{1,0:T(8,128)(2,1)S(1)} %collective-permute-done.refs_1_, ...), custom_call_target="tpu_custom_call" | custom-call | tf_op jit(solution)/shard_map/tile/pallas_call | solution.py:136
  87.9 1.0 copy-done.2
  88.9 0.7 copy-done.4
  89.6 3.7 %all-to-all-start.2 = ((f32[32,1,256]{2,1,0:T(1,128)}), f32[32,1,256]{2,1,0:T(1,128)S(1)}, u32[]{:S(2)}, u32[]{:S(2)}) async-start(f32[32,1,256]{2,1,0:T(1,128)} %get-tuple-element.35), calls=%async_computation.2 | async-start | bytes 65536 | tf_op jit(solution)/shard_map/all_to_all | solution.py:406
  94.0 6.6 %all-to-all-done.2.sums_any = f32[32,1,256]{2,1,0:T(1,128)S(1)} async-done(((f32[32,1,256]{2,1,0:T(1,128)}), f32[32,1,256]{2,1,0:T(1,128)S(1)}, u32[]{:S(2)}, u32[]{:S(2)}) %all-to-all-start.2) | async-done | bytes 32800 | tf_op jit(solution)/shard_map/all_to_all | solution.py:406
  100.6 0.6 copy-done.6
  101.2 2.7 %update.1 = (f32[640,128]{1,0:T(8,128)}, f32[640,384]{1,0:T(8,128)}) custom-call(f32[1]{0:T(128)} %bitcast.14.step_ref, f32[32,1,256]{2,1,0:T(1,128)} %copy-done.6, f32[640,128]{1,0:T(8,128)} %copy-done.4, f32[640,384]{1,0:T(8,128)} %copy-done.2, f32[640,128]{1,0:T(8,128)} %w_kv.1, f32[640,384]{1,0:T(8,128)} %w_up.1), custom_call_target="tpu_custom_call" | custom-call | tf_op jit(solution)/shard_map/update/pallas_call | solution.py:226
  (44 shorter events, 1.4 us)
Async XLA Ops:
  2.7 15.5 %collective-permute-start = (bf16[1280,128]{1,0:T(8,128)(2,1)}, bf16[1280,128]{1,0:T(8,128)(2,1)S(1)}, u32[]{:S(2)}, u32[]{:S(2)}) collective-permute-start(bf16[1280,128]{1,0:T(8,128)(2,1)} %get-tuple-element.20.refs_0_), channel_id=1, source_target_pairs={{0,8},{4,12},{8,0},{12,4},{16,24},{20,28},{24,16},{28,20},{1,9},{5... | collective-permute-start | bytes 983048 | tf_op jit(solution)/shard_map/ppermute | solution.py:311
  5.7 12.4 %collective-permute-start.1 = (bf16[1280,128]{1,0:T(8,128)(2,1)}, bf16[1280,128]{1,0:T(8,128)(2,1)S(1)}, u32[]{:S(2)}, u32[]{:S(2)}) collective-permute-start(bf16[1280,128]{1,0:T(8,128)(2,1)} %get-tuple-element.20.refs_0_), channel_id=1, source_target_pairs={{8,16},{12,20},{16,8},{20,12},{9,17},{13,21},{17,9},{21,13},{10,18... | collective-permute-start | bytes 983048 | tf_op jit(solution)/shard_map/ppermute | solution.py:311
  6.4 11.8 %collective-permute-start.2 = (bf16[1280,128]{1,0:T(8,128)(2,1)}, bf16[1280,128]{1,0:T(8,128)(2,1)S(1)}, u32[]{:S(2)}, u32[]{:S(2)}) collective-permute-start(bf16[1280,128]{1,0:T(8,128)(2,1)} %get-tuple-element.20.refs_0_), channel_id=1, source_target_pairs={{0,4},{4,0},{8,12},{12,8},{16,20},{20,16},{24,28},{28,24},{1,5},{5... | collective-permute-start | bytes 983048 | tf_op jit(solution)/shard_map/ppermute | solution.py:314
  7.9 10.2 %all-to-all-start = ((bf16[4,32,1024]{2,1,0:T(8,128)(2,1)}), bf16[4,32,1024]{2,1,0:T(8,128)(2,1)}, u32[]{:S(2)}, u32[]{:S(2)}) async-start(bf16[4,32,1024]{2,1,0:T(8,128)(2,1)} %bitcast.17), calls=%async_computation | async-start | bytes 524288 | tf_op jit(solution)/shard_map/all_to_all | solution.py:327
  12.0 1.8 %copy-start.5 = (f32[1,256,256]{2,1,0:T(8,128)S(1)}, f32[1,256,256]{2,1,0:T(8,128)}, u32[]{:S(2)}) copy-start(f32[1,256,256]{2,1,0:T(8,128)} %param.19) | copy-start | bytes 786436
  18.1 24.7 %collective-permute-start.6 = (bf16[768,768]{1,0:T(8,128)(2,1)S(1)}, bf16[768,768]{1,0:T(8,128)(2,1)}, u32[]{:S(2)}, u32[]{:S(2)}) collective-permute-start(bf16[768,768]{1,0:T(8,128)(2,1)S(1)} %bitcast_dynamic-update-slice_fusion), channel_id=1, source_target_pairs={{0,2},{4,6},{9,11},{13,15},{18,16},{22,20},{27,25},{31,29}} | collective-permute-start | bytes 3538952 | tf_op jit(solution)/shard_map/ppermute | solution.py:336
  21.4 12.1 %collective-permute-start.3 = (bf16[1280,128]{1,0:T(8,128)(2,1)S(1)}, bf16[1280,128]{1,0:T(8,128)(2,1)S(1)}, u32[]{:S(2)}, u32[]{:S(2)}) collective-permute-start(bf16[1280,128]{1,0:T(8,128)(2,1)S(1)} %collective-permute-done.1), channel_id=1, source_target_pairs={{8,0},{12,4},{16,24},{20,28},{9,1},{13,5},{17,25},{21,29},{10,2},{... | collective-permute-start | bytes 983048 | tf_op jit(solution)/shard_map/ppermute | solution.py:311
  22.8 10.9 %collective-permute-start.4 = (bf16[1280,128]{1,0:T(8,128)(2,1)S(1)}, bf16[1280,128]{1,0:T(8,128)(2,1)}, u32[]{:S(2)}, u32[]{:S(2)}) collective-permute-start(bf16[1280,128]{1,0:T(8,128)(2,1)S(1)} %collective-permute-done.refs_1_), channel_id=1, source_target_pairs={{8,16},{12,20},{16,8},{20,12},{9,17},{13,21},{17,9},{21,13},{10,18... | collective-permute-start | bytes 983048 | tf_op jit(solution)/shard_map/ppermute | solution.py:311
  24.2 9.5 %collective-permute-start.5 = (bf16[1280,128]{1,0:T(8,128)(2,1)S(1)}, bf16[1280,128]{1,0:T(8,128)(2,1)S(1)}, u32[]{:S(2)}, u32[]{:S(2)}) collective-permute-start(bf16[1280,128]{1,0:T(8,128)(2,1)S(1)} %collective-permute-done.refs_1_), channel_id=1, source_target_pairs={{0,4},{4,0},{8,12},{12,8},{16,20},{20,16},{24,28},{28,24},{1,5},{5... | collective-permute-start | bytes 983048 | tf_op jit(solution)/shard_map/ppermute | solution.py:314
  24.7 18.1 %all-to-all-start.1 = ((bf16[4,32,1024]{2,1,0:T(8,128)(2,1)}), bf16[4,32,1024]{2,1,0:T(8,128)(2,1)S(1)}, u32[]{:S(2)}, u32[]{:S(2)}) async-start(bf16[4,32,1024]{2,1,0:T(8,128)(2,1)} %all-to-all-done), calls=%async_computation.1 | async-start | bytes 524288 | tf_op jit(solution)/shard_map/all_to_all | solution.py:332
  33.6 24.0 %copy-start.9 = (s32[2,4]{1,0:T(2,128)S(1)}, s32[2,4]{1,0:T(2,128)}, u32[]{:S(2)}) copy-start(s32[2,4]{1,0:T(2,128)} %param.22) | copy-start | bytes 100
  33.6 24.0 %copy-start.7 = (f32[4,4]{1,0:T(4,128)S(1)}, f32[4,4]{1,0:T(4,128)}, u32[]{:S(2)}) copy-start(f32[4,4]{1,0:T(4,128)} %param.24) | copy-start | bytes 196
  33.6 24.8 %copy-start.8 = (f32[4]{0:T(128)S(1)}, f32[4]{0:T(128)}, u32[]{:S(2)}) copy-start(f32[4]{0:T(128)} %param.23) | copy-start | bytes 52
  42.8 11.8 %collective-permute-start.8 = (bf16[1280,128]{1,0:T(8,128)(2,1)}, bf16[1280,128]{1,0:T(8,128)(2,1)S(1)}, u32[]{:S(2)}, u32[]{:S(2)}) collective-permute-start(bf16[1280,128]{1,0:T(8,128)(2,1)} %collective-permute-done.4), channel_id=1, source_target_pairs={{8,0},{12,4},{16,24},{20,28},{9,1},{13,5},{17,25},{21,29},{10,2},{... | collective-permute-start | bytes 983048 | tf_op jit(solution)/shard_map/ppermute | solution.py:311
  45.3 19.8 %collective-permute-start.17 = (bf16[768,768]{1,0:T(8,128)(2,1)}, bf16[768,768]{1,0:T(8,128)(2,1)}, u32[]{:S(2)}, u32[]{:S(2)}) collective-permute-start(bf16[768,768]{1,0:T(8,128)(2,1)} %broadcast_select_fusion), channel_id=1, source_target_pairs={{0,1},{2,3},{4,5},{6,7},{9,8},{11,10},{13,12},{15,14},{16,17},{18,... | collective-permute-start | bytes 3538952 | tf_op jit(solution)/shard_map/ppermute | solution.py:344
  48.3 9.2 %collective-permute-start.7 = (bf16[4,32,1024]{2,1,0:T(8,128)(2,1)S(1)}, bf16[4,32,1024]{2,1,0:T(8,128)(2,1)S(1)}, u32[]{:S(2)}, u32[]{:S(2)}) collective-permute-start(bf16[4,32,1024]{2,1,0:T(8,128)(2,1)S(1)} %all-to-all-done.1.refs_8_), channel_id=1, source_target_pairs={{0,4},{4,0},{8,12},{12,8},{16,20},{20,16},{24,28},{28,24},{1,5},{5... | collective-permute-start | bytes 786440 | tf_op jit(solution)/shard_map/ppermute | solution.py:314
  48.9 9.7 %collective-permute-start.11 = (bf16[4,32,1024]{2,1,0:T(8,128)(2,1)S(1)}, bf16[4,32,1024]{2,1,0:T(8,128)(2,1)S(1)}, u32[]{:S(2)}, u32[]{:S(2)}) collective-permute-start(bf16[4,32,1024]{2,1,0:T(8,128)(2,1)S(1)} %all-to-all-done.1.refs_8_), channel_id=1, source_target_pairs={{0,2},{1,3},{2,0},{3,1},{4,6},{5,7},{6,4},{7,5},{8,10},{9,11},{10,... | collective-permute-start | bytes 786440 | tf_op jit(solution)/shard_map/ppermute | solution.py:342
  49.1 15.5 %collective-permute-start.9 = (bf16[1280,128]{1,0:T(8,128)(2,1)S(1)}, bf16[1280,128]{1,0:T(8,128)(2,1)S(1)}, u32[]{:S(2)}, u32[]{:S(2)}) collective-permute-start(bf16[1280,128]{1,0:T(8,128)(2,1)S(1)} %broadcast_select_fusion.3.refs_2_), channel_id=1, source_target_pairs={{0,4},{4,0},{8,12},{12,8},{16,20},{20,16},{24,28},{28,24},{1,5},{5... | collective-permute-start | bytes 983048 | tf_op jit(solution)/shard_map/ppermute | solution.py:314
  54.7 14.3 %copy-start.3 = (bf16[1280,128]{1,0:T(8,128)(2,1)S(1)}, bf16[1280,128]{1,0:T(8,128)(2,1)}, u32[]{:S(2)}) copy-start(bf16[1280,128]{1,0:T(8,128)(2,1)} %get-tuple-element.20.refs_0_) | copy-start | bytes 983044
  57.6 7.0 %collective-permute-start.14 = (bf16[4,32,1024]{2,1,0:T(8,128)(2,1)S(1)}, bf16[4,32,1024]{2,1,0:T(8,128)(2,1)}, u32[]{:S(2)}, u32[]{:S(2)}) collective-permute-start(bf16[4,32,1024]{2,1,0:T(8,128)(2,1)S(1)} %collective-permute-done.7.refs_12_), channel_id=1, source_target_pairs={{0,2},{1,3},{2,0},{3,1},{4,6},{5,7},{6,4},{7,5},{8,10},{9,11},{10,... | collective-permute-start | bytes 786440 | tf_op jit(solution)/shard_map/ppermute | solution.py:348
  57.9 11.1 %collective-permute-start.10 = (bf16[1280,128]{1,0:T(8,128)(2,1)S(1)}, bf16[1280,128]{1,0:T(8,128)(2,1)S(1)}, u32[]{:S(2)}, u32[]{:S(2)}) collective-permute-start(bf16[1280,128]{1,0:T(8,128)(2,1)S(1)} %broadcast_select_fusion.2.refs_3_), channel_id=1, source_target_pairs={{0,4},{4,0},{8,12},{12,8},{16,20},{20,16},{24,28},{28,24},{1,5},{5... | collective-permute-start | bytes 983048 | tf_op jit(solution)/shard_map/ppermute | solution.py:314
  58.5 10.5 %copy-start = (f32[1,640,640]{2,1,0:T(8,128)S(1)}, f32[1,640,640]{2,1,0:T(8,128)}, u32[]{:S(2)}) copy-start(f32[1,640,640]{2,1,0:T(8,128)} %param.18) | copy-start | bytes 4915204
  58.5 10.5 %copy-start.1 = (f32[1,640,640]{2,1,0:T(8,128)S(1)}, f32[1,640,640]{2,1,0:T(8,128)}, u32[]{:S(2)}) copy-start(f32[1,640,640]{2,1,0:T(8,128)} %param.20) | copy-start | bytes 4915204
  58.5 8.1 %collective-permute-start.13 = (bf16[4,32,1024]{2,1,0:T(8,128)(2,1)S(1)}, bf16[4,32,1024]{2,1,0:T(8,128)(2,1)S(1)}, u32[]{:S(2)}, u32[]{:S(2)}) collective-permute-start(bf16[4,32,1024]{2,1,0:T(8,128)(2,1)S(1)} %collective-permute-done.11.refs_9_), channel_id=1, source_target_pairs={{0,1},{1,0},{2,3},{3,2},{4,5},{5,4},{6,7},{7,6},{8,9},{9,8},{10,11... | collective-permute-start | bytes 786440 | tf_op jit(solution)/shard_map/ppermute | solution.py:352
  64.6 2.0 %collective-permute-start.15 = (bf16[4,32,1024]{2,1,0:T(8,128)(2,1)S(1)}, bf16[4,32,1024]{2,1,0:T(8,128)(2,1)S(1)}, u32[]{:S(2)}, u32[]{:S(2)}) collective-permute-start(bf16[4,32,1024]{2,1,0:T(8,128)(2,1)S(1)} %collective-permute-done.7.refs_12_), channel_id=1, source_target_pairs={{0,1},{1,0},{2,3},{3,2},{4,5},{5,4},{6,7},{7,6},{8,9},{9,8},{10,11... | collective-permute-start | bytes 786440 | tf_op jit(solution)/shard_map/ppermute | solution.py:352
  64.6 2.0 %collective-permute-start.12 = (bf16[4,32,1024]{2,1,0:T(8,128)(2,1)S(1)}, bf16[4,32,1024]{2,1,0:T(8,128)(2,1)S(1)}, u32[]{:S(2)}, u32[]{:S(2)}) collective-permute-start(bf16[4,32,1024]{2,1,0:T(8,128)(2,1)S(1)} %all-to-all-done.1.refs_8_), channel_id=1, source_target_pairs={{0,1},{1,0},{2,3},{3,2},{4,5},{5,4},{6,7},{7,6},{8,9},{9,8},{10,11... | collective-permute-start | bytes 786440 | tf_op jit(solution)/shard_map/ppermute | solution.py:352
  65.1 3.9 %collective-permute-start.16 = (bf16[4,32,1024]{2,1,0:T(8,128)(2,1)}, bf16[4,32,1024]{2,1,0:T(8,128)(2,1)S(1)}, u32[]{:S(2)}, u32[]{:S(2)}) collective-permute-start(bf16[4,32,1024]{2,1,0:T(8,128)(2,1)} %collective-permute-done.14.refs_13_), channel_id=1, source_target_pairs={{0,1},{1,0},{2,3},{3,2},{4,5},{5,4},{6,7},{7,6},{8,9},{9,8},{10,11... | collective-permute-start | bytes 786440 | tf_op jit(solution)/shard_map/ppermute | solution.py:352
  87.9 1.0 copy-start.2
  88.9 0.7 copy-start.4
  89.6 11.0 %all-to-all-start.2 = ((f32[32,1,256]{2,1,0:T(1,128)}), f32[32,1,256]{2,1,0:T(1,128)S(1)}, u32[]{:S(2)}, u32[]{:S(2)}) async-start(f32[32,1,256]{2,1,0:T(1,128)} %get-tuple-element.35), calls=%async_computation.2 | async-start | bytes 65536 | tf_op jit(solution)/shard_map/all_to_all | solution.py:406
  100.6 0.6 copy-start.6

commit v5 on v4

--- a/solution.py
+++ b/solution.py
@@ -85,7 +85,7 @@
         coef = sc[3, fg] * lax.rsqrt(squares)
         scaled_into(y_g, m_g, coef)
         first = pl.multiple_of(slot * cols, 128)
-        for s, w in tiles(cols):
+        for s, w in tiles(cols, 512):
             yc = coef * m_g[:, pl.ds(pl.multiple_of(first + s, 128), w)]
             square = contract(y_g[...], yc.astype(BF), 1, 0)
             cubic = contract(y_g[...], (4.0 * yc - square).astype(BF), 1, 0)
@@ -98,7 +98,7 @@
         al = at.at[in_width * linear:in_width * (linear + 1), :]
         for s, w in tiles(width):
             low[:, s:s + w] = (contract(al[...], part(s, w), 1, 0) * sc[4, 0]).astype(BF)
-        for s, w in tiles(cols):
+        for s, w in tiles(cols, 512):
             rt[:, s:s + w] = contract(low[:, :width], i_g[:, s:s + w], 1, 0).astype(BF)
         loads_p[1 + linear].wait()
         squares = damped_into(
@@ -107,7 +107,7 @@
         coef = sc[3, fa] * lax.rsqrt(squares)
         scaled_into(y_a, m_a, coef)
         total = jnp.zeros((1, 1), F32)
-        for s, w in tiles(cols):
+        for s, w in tiles(cols, 512):
             right = rt[:, s:s + w]
             wide = right.astype(F32)
             inner = 4.0 * wide - contract(y_a[...], right, 1, 0)
@@ -156,7 +156,7 @@
         + [pltpu.VMEM(packed.shape, BF)]
         + [pltpu.VMEM((in_width, c), F32) for c in cols]
         + [pltpu.SemaphoreType.DMA((n,)) for n in (2 * quarters, 3, count, 2)],
-        compiler_params=pltpu.CompilerParams(vmem_limit_bytes=32 * 2**20),
+        compiler_params=pltpu.CompilerParams(vmem_limit_bytes=48 * 2**20),
         name="tile",
     )(sc, where, *parts, *blocks, pa_kv, pa_up, packed)
 

time: 105 us -> 104 us (level)
    unnamed x20 -> x16, local copies, waits for them, and re-layouts: 2.34 us -> 2.37 us
  transfers between devices with their start and end apart: 21 -> 21, of which waited for: 8 -> 8; matrix products, arithmetic and copies ran while one was open for 5% -> 6% of each run, Pallas kernels for 0% -> 0%
where the time goes in v5:
time: 104 us; the launch traced here: 103 us
  waiting for transfers between devices  37.2 us (36%)
  starting transfers between devices  33.5 us (32%)
  Pallas kernels  22.7 us (22%)
  other arithmetic  5.49 us (5%)
  local copies, waits for them, and re-layouts  2.61 us (3%)
  between operations  1.68 us (2%)
    pallas_call x1, Pallas kernels, tile(): pl.pallas_call(functools.partial(tile_kernel, count, quarters, in_width,...  18 us
    ppermute x5, waiting for transfers between devices, across_y(): return lax.ppermute(value, 'dp', dp_swap(1))  10.3 us
    all_to_all x1, waiting for transfers between devices, gather_fast(): lax.all_to_all(split, 'dp', 0, 0, tiled=True, axis_index_groups=z_lines)  9.18 us
    ppermute x5, starting transfers between devices, along_z(): lax.ppermute(value, 'dp', [(2 * s + y, 2 * t + y) for s, t in pairs for y...  7.66 us
    ppermute x5, waiting for transfers between devices, along_z(): lax.ppermute(value, 'dp', [(2 * s + y, 2 * t + y) for s, t in pairs for y...  6.82 us
    all_to_all x1, waiting for transfers between devices, shards(): sums = lax.all_to_all(sent, ('dp', 'own'), 0, 0, tiled=True)  6.6 us
    all_to_all x1, starting transfers between devices, gather_fast(): lax.all_to_all(split, 'dp', 0, 0, tiled=True, axis_index_groups=z_lines)  6.1 us
    ppermute x5, starting transfers between devices, across_y(): return lax.ppermute(value, 'dp', dp_swap(1))  4.66 us
  transfers between devices with their start and end apart: 21, of which 8 were waited for; matrix products, arithmetic and copies ran while one was open for 6% of the time, Pallas kernels for 0%

profile of v5, /device:TPU:0, one launch (start us, length us, event | category | flops | bytes accessed | tf_op | source)
XLA Modules:
  0.0 103.2 jit_solution(15981588075407444109)
XLA Ops:
  0.6 2.0 %turn.1 = (bf16[1280,128]{1,0:T(8,128)(2,1)}, bf16[128,1024]{1,0:T(8,128)(2,1)}) custom-call(bf16[128,640]{1,0:T(8,128)(2,1)} %kv_ref.1, bf16[128,640]{1,0:T(8,128)(2,1)} %up_ref.1, bf16[128,256]{1,0:T(8,128)(2,1)} %g_kv.1, bf16[128,768]{1,0:T(8,128)(2,1)} %g_up.1), custom_call_target="tpu_custom_call" | custom-call | tf_op jit(solution)/shard_map/turn/pallas_call | solution.py:182
  2.7 3.0 %collective-permute-start = (bf16[1280,128]{1,0:T(8,128)(2,1)}, bf16[1280,128]{1,0:T(8,128)(2,1)S(1)}, u32[]{:S(2)}, u32[]{:S(2)}) collective-permute-start(bf16[1280,128]{1,0:T(8,128)(2,1)} %get-tuple-element.20.refs_0_), channel_id=1, source_target_pairs={{0,8},{4,12},{8,0},{12,4},{16,24},{20,28},{24,16},{28,20},{1,9},{5... | collective-permute-start | bytes 983048 | tf_op jit(solution)/shard_map/ppermute | solution.py:311
  5.7 0.7 collective-permute-start.1
  6.4 1.6 %collective-permute-start.2 = (bf16[1280,128]{1,0:T(8,128)(2,1)}, bf16[1280,128]{1,0:T(8,128)(2,1)S(1)}, u32[]{:S(2)}, u32[]{:S(2)}) collective-permute-start(bf16[1280,128]{1,0:T(8,128)(2,1)} %get-tuple-element.20.refs_0_), channel_id=1, source_target_pairs={{0,4},{4,0},{8,12},{12,8},{16,20},{20,16},{24,28},{28,24},{1,5},{5... | collective-permute-start | bytes 983048 | tf_op jit(solution)/shard_map/ppermute | solution.py:314
  7.9 4.0 %all-to-all-start = ((bf16[4,32,1024]{2,1,0:T(8,128)(2,1)}), bf16[4,32,1024]{2,1,0:T(8,128)(2,1)}, u32[]{:S(2)}, u32[]{:S(2)}) async-start(bf16[4,32,1024]{2,1,0:T(8,128)(2,1)} %bitcast.17), calls=%async_computation | async-start | bytes 524288 | tf_op jit(solution)/shard_map/all_to_all | solution.py:327
  12.0 1.8 %convert_bitcast_fusion = bf16[768,768]{1,0:T(8,128)(2,1)S(1)} fusion(f32[1,768,768]{2,1,0:T(8,128)} %param.21), kind=kLoop, calls=%fused_computation | loop fusion | flops 589824 | bytes 3538944 | tf_op jit(solution)/shard_map/convert_element_type | solution.py:384
  13.9 4.2 %all-to-all-done = bf16[4,32,1024]{2,1,0:T(8,128)(2,1)} async-done(((bf16[4,32,1024]{2,1,0:T(8,128)(2,1)}), bf16[4,32,1024]{2,1,0:T(8,128)(2,1)}, u32[]{:S(2)}, u32[]{:S(2)}) %all-to-all-start) | async-done | bytes 262176 | tf_op jit(solution)/shard_map/all_to_all | solution.py:327
  18.1 3.3 %collective-permute-start.6 = (bf16[768,768]{1,0:T(8,128)(2,1)S(1)}, bf16[768,768]{1,0:T(8,128)(2,1)}, u32[]{:S(2)}, u32[]{:S(2)}) collective-permute-start(bf16[768,768]{1,0:T(8,128)(2,1)S(1)} %bitcast_dynamic-update-slice_fusion), channel_id=1, source_target_pairs={{0,2},{4,6},{9,11},{13,15},{18,16},{22,20},{27,25},{31,29}} | collective-permute-start | bytes 3538952 | tf_op jit(solution)/shard_map/ppermute | solution.py:336
  21.4 1.3 %collective-permute-start.3 = (bf16[1280,128]{1,0:T(8,128)(2,1)S(1)}, bf16[1280,128]{1,0:T(8,128)(2,1)S(1)}, u32[]{:S(2)}, u32[]{:S(2)}) collective-permute-start(bf16[1280,128]{1,0:T(8,128)(2,1)S(1)} %collective-permute-done.1), channel_id=1, source_target_pairs={{8,0},{12,4},{16,24},{20,28},{9,1},{13,5},{17,25},{21,29},{10,2},{... | collective-permute-start | bytes 983048 | tf_op jit(solution)/shard_map/ppermute | solution.py:311
  22.7 1.4 %collective-permute-start.4 = (bf16[1280,128]{1,0:T(8,128)(2,1)S(1)}, bf16[1280,128]{1,0:T(8,128)(2,1)}, u32[]{:S(2)}, u32[]{:S(2)}) collective-permute-start(bf16[1280,128]{1,0:T(8,128)(2,1)S(1)} %collective-permute-done.refs_1_), channel_id=1, source_target_pairs={{8,16},{12,20},{16,8},{20,12},{9,17},{13,21},{17,9},{21,13},{10,18... | collective-permute-start | bytes 983048 | tf_op jit(solution)/shard_map/ppermute | solution.py:311
  24.7 6.1 %all-to-all-start.1 = ((bf16[4,32,1024]{2,1,0:T(8,128)(2,1)}), bf16[4,32,1024]{2,1,0:T(8,128)(2,1)S(1)}, u32[]{:S(2)}, u32[]{:S(2)}) async-start(bf16[4,32,1024]{2,1,0:T(8,128)(2,1)} %all-to-all-done), calls=%async_computation.1 | async-start | bytes 524288 | tf_op jit(solution)/shard_map/all_to_all | solution.py:332
  30.8 2.8 %collective-permute-done.3 = bf16[1280,128]{1,0:T(8,128)(2,1)S(1)} collective-permute-done((bf16[1280,128]{1,0:T(8,128)(2,1)S(1)}, bf16[1280,128]{1,0:T(8,128)(2,1)S(1)}, u32[]{:S(2)}, u32[]{:S(2)}) %collective-permute-start.3) | collective-permute-done | bytes 327712 | tf_op jit(solution)/shard_map/ppermute | solution.py:311
  33.6 9.2 %all-to-all-done.1.refs_8_ = bf16[4,32,1024]{2,1,0:T(8,128)(2,1)S(1)} async-done(((bf16[4,32,1024]{2,1,0:T(8,128)(2,1)}), bf16[4,32,1024]{2,1,0:T(8,128)(2,1)S(1)}, u32[]{:S(2)}, u32[]{:S(2)}) %all-to-all-start.1) | async-done | bytes 262176 | tf_op jit(solution)/shard_map/all_to_all | solution.py:332
  42.8 1.3 %collective-permute-start.8 = (bf16[1280,128]{1,0:T(8,128)(2,1)}, bf16[1280,128]{1,0:T(8,128)(2,1)S(1)}, u32[]{:S(2)}, u32[]{:S(2)}) collective-permute-start(bf16[1280,128]{1,0:T(8,128)(2,1)} %collective-permute-done.4), channel_id=1, source_target_pairs={{8,0},{12,4},{16,24},{20,28},{9,1},{13,5},{17,25},{21,29},{10,2},{... | collective-permute-start | bytes 983048 | tf_op jit(solution)/shard_map/ppermute | solution.py:311
  44.1 1.2 %broadcast_select_fusion = bf16[768,768]{1,0:T(8,128)(2,1)} fusion(bf16[768,768]{1,0:T(8,128)(2,1)S(1)} %bitcast_dynamic-update-slice_fusion, bf16[768,768]{1,0:T(8,128)(2,1)} %collective-permute-done.6, pred[]{:T(512)S(6)} %eq.36), kind=kLoop, calls=%fused_computation.1 | loop fusion | flops 589824 | bytes 3538945 | tf_op jit(solution)/shard_map/jit(_where)/select_n | solution.py:343
  45.3 3.0 %collective-permute-start.17 = (bf16[768,768]{1,0:T(8,128)(2,1)}, bf16[768,768]{1,0:T(8,128)(2,1)}, u32[]{:S(2)}, u32[]{:S(2)}) collective-permute-start(bf16[768,768]{1,0:T(8,128)(2,1)} %broadcast_select_fusion), channel_id=1, source_target_pairs={{0,1},{2,3},{4,5},{6,7},{9,8},{11,10},{13,12},{15,14},{16,17},{18,... | collective-permute-start | bytes 3538952 | tf_op jit(solution)/shard_map/ppermute | solution.py:344
  48.3 0.5 collective-permute-start.7
  49.1 1.5 %collective-permute-start.9 = (bf16[1280,128]{1,0:T(8,128)(2,1)S(1)}, bf16[1280,128]{1,0:T(8,128)(2,1)S(1)}, u32[]{:S(2)}, u32[]{:S(2)}) collective-permute-start(bf16[1280,128]{1,0:T(8,128)(2,1)S(1)} %broadcast_select_fusion.3.refs_2_), channel_id=1, source_target_pairs={{0,4},{4,0},{8,12},{12,8},{16,20},{20,16},{24,28},{28,24},{1,5},{5... | collective-permute-start | bytes 983048 | tf_op jit(solution)/shard_map/ppermute | solution.py:314
  50.6 4.0 %collective-permute-done.8 = bf16[1280,128]{1,0:T(8,128)(2,1)S(1)} collective-permute-done((bf16[1280,128]{1,0:T(8,128)(2,1)}, bf16[1280,128]{1,0:T(8,128)(2,1)S(1)}, u32[]{:S(2)}, u32[]{:S(2)}) %collective-permute-start.8) | collective-permute-done | bytes 327712 | tf_op jit(solution)/shard_map/ppermute | solution.py:311
  54.7 2.9 %collective-permute-done.7.refs_12_ = bf16[4,32,1024]{2,1,0:T(8,128)(2,1)S(1)} collective-permute-done((bf16[4,32,1024]{2,1,0:T(8,128)(2,1)S(1)}, bf16[4,32,1024]{2,1,0:T(8,128)(2,1)S(1)}, u32[]{:S(2)}, u32[]{:S(2)}) %collective-permute-start.7) | collective-permute-done | bytes 262176 | tf_op jit(solution)/shard_map/ppermute | solution.py:314
  57.8 0.5 collective-permute-start.10
  58.5 6.0 %collective-permute-done.9.refs_6_ = bf16[1280,128]{1,0:T(8,128)(2,1)S(1)} collective-permute-done((bf16[1280,128]{1,0:T(8,128)(2,1)S(1)}, bf16[1280,128]{1,0:T(8,128)(2,1)S(1)}, u32[]{:S(2)}, u32[]{:S(2)}) %collective-permute-start.9) | collective-permute-done | bytes 327712 | tf_op jit(solution)/shard_map/ppermute | solution.py:314
  64.6 0.5 collective-permute-start.12
  65.1 2.4 %broadcast_select_fusion.1.refs_18_ = bf16[768,768]{1,0:T(8,128)(2,1)} fusion(bf16[768,768]{1,0:T(8,128)(2,1)} %broadcast_select_fusion, bf16[768,768]{1,0:T(8,128)(2,1)} %collective-permute-done.17, pred[]{:T(512)S(6)} %eq.35), kind=kLoop, calls=%fused_computation.2 | loop fusion | flops 589824 | bytes 3538945 | tf_op jit(solution)/shard_map/jit(_where)/select_n | solution.py:349
  67.6 1.4 %collective-permute-done.10.refs_7_ = bf16[1280,128]{1,0:T(8,128)(2,1)S(1)} collective-permute-done((bf16[1280,128]{1,0:T(8,128)(2,1)S(1)}, bf16[1280,128]{1,0:T(8,128)(2,1)S(1)}, u32[]{:S(2)}, u32[]{:S(2)}) %collective-permute-start.10) | collective-permute-done | bytes 327712 | tf_op jit(solution)/shard_map/ppermute | solution.py:314
  69.0 18.0 %tile.1 = (f32[640,128]{1,0:T(8,128)S(1)}, f32[640,384]{1,0:T(8,128)S(1)}, f32[32,1,256]{2,1,0:T(1,128)}) custom-call(f32[5,4]{1,0:T(8,128)S(1)} %stack.10.sc, s32[1]{0:T(128)} %bitcast.2.where_ref, bf16[1280,128]{1,0:T(8,128)(2,1)S(1)} %copy-done.1, bf16[1280,128]{1,0:T(8,128)(2,1)S(1)} %collective-permute-done.refs_1_, ...), custom_call_target="tpu_custom_call" | custom-call | tf_op jit(solution)/shard_map/tile/pallas_call | solution.py:136
  87.0 1.0 copy-done
  88.0 0.7 copy-done.2
  88.7 3.7 %all-to-all-start.2 = ((f32[32,1,256]{2,1,0:T(1,128)}), f32[32,1,256]{2,1,0:T(1,128)S(1)}, u32[]{:S(2)}, u32[]{:S(2)}) async-start(f32[32,1,256]{2,1,0:T(1,128)} %get-tuple-element.35), calls=%async_computation.2 | async-start | bytes 65536 | tf_op jit(solution)/shard_map/all_to_all | solution.py:406
  93.1 6.6 %all-to-all-done.2.sums_any = f32[32,1,256]{2,1,0:T(1,128)S(1)} async-done(((f32[32,1,256]{2,1,0:T(1,128)}), f32[32,1,256]{2,1,0:T(1,128)S(1)}, u32[]{:S(2)}, u32[]{:S(2)}) %all-to-all-start.2) | async-done | bytes 32800 | tf_op jit(solution)/shard_map/all_to_all | solution.py:406
  99.7 0.6 copy-done.4
  100.3 2.7 %update.1 = (f32[640,128]{1,0:T(8,128)}, f32[640,384]{1,0:T(8,128)}) custom-call(f32[1]{0:T(128)} %bitcast.14.step_ref, f32[32,1,256]{2,1,0:T(1,128)} %copy-done.4, f32[640,128]{1,0:T(8,128)} %copy-done.2, f32[640,384]{1,0:T(8,128)} %copy-done, f32[640,128]{1,0:T(8,128)} %w_kv.1, f32[640,384]{1,0:T(8,128)} %w_up.1), custom_call_target="tpu_custom_call" | custom-call | tf_op jit(solution)/shard_map/update/pallas_call | solution.py:226
  (40 shorter events, 1.4 us)
Async XLA Ops:
  2.7 15.4 %collective-permute-start = (bf16[1280,128]{1,0:T(8,128)(2,1)}, bf16[1280,128]{1,0:T(8,128)(2,1)S(1)}, u32[]{:S(2)}, u32[]{:S(2)}) collective-permute-start(bf16[1280,128]{1,0:T(8,128)(2,1)} %get-tuple-element.20.refs_0_), channel_id=1, source_target_pairs={{0,8},{4,12},{8,0},{12,4},{16,24},{20,28},{24,16},{28,20},{1,9},{5... | collective-permute-start | bytes 983048 | tf_op jit(solution)/shard_map/ppermute | solution.py:311
  5.7 12.4 %collective-permute-start.1 = (bf16[1280,128]{1,0:T(8,128)(2,1)}, bf16[1280,128]{1,0:T(8,128)(2,1)S(1)}, u32[]{:S(2)}, u32[]{:S(2)}) collective-permute-start(bf16[1280,128]{1,0:T(8,128)(2,1)} %get-tuple-element.20.refs_0_), channel_id=1, source_target_pairs={{8,16},{12,20},{16,8},{20,12},{9,17},{13,21},{17,9},{21,13},{10,18... | collective-permute-start | bytes 983048 | tf_op jit(solution)/shard_map/ppermute | solution.py:311
  6.4 11.7 %collective-permute-start.2 = (bf16[1280,128]{1,0:T(8,128)(2,1)}, bf16[1280,128]{1,0:T(8,128)(2,1)S(1)}, u32[]{:S(2)}, u32[]{:S(2)}) collective-permute-start(bf16[1280,128]{1,0:T(8,128)(2,1)} %get-tuple-element.20.refs_0_), channel_id=1, source_target_pairs={{0,4},{4,0},{8,12},{12,8},{16,20},{20,16},{24,28},{28,24},{1,5},{5... | collective-permute-start | bytes 983048 | tf_op jit(solution)/shard_map/ppermute | solution.py:314
  7.9 10.1 %all-to-all-start = ((bf16[4,32,1024]{2,1,0:T(8,128)(2,1)}), bf16[4,32,1024]{2,1,0:T(8,128)(2,1)}, u32[]{:S(2)}, u32[]{:S(2)}) async-start(bf16[4,32,1024]{2,1,0:T(8,128)(2,1)} %bitcast.17), calls=%async_computation | async-start | bytes 524288 | tf_op jit(solution)/shard_map/all_to_all | solution.py:327
  12.0 1.8 %copy-start.3 = (f32[1,256,256]{2,1,0:T(8,128)S(1)}, f32[1,256,256]{2,1,0:T(8,128)}, u32[]{:S(2)}) copy-start(f32[1,256,256]{2,1,0:T(8,128)} %param.19) | copy-start | bytes 786436
  18.1 24.7 %collective-permute-start.6 = (bf16[768,768]{1,0:T(8,128)(2,1)S(1)}, bf16[768,768]{1,0:T(8,128)(2,1)}, u32[]{:S(2)}, u32[]{:S(2)}) collective-permute-start(bf16[768,768]{1,0:T(8,128)(2,1)S(1)} %bitcast_dynamic-update-slice_fusion), channel_id=1, source_target_pairs={{0,2},{4,6},{9,11},{13,15},{18,16},{22,20},{27,25},{31,29}} | collective-permute-start | bytes 3538952 | tf_op jit(solution)/shard_map/ppermute | solution.py:336
  21.4 12.1 %collective-permute-start.3 = (bf16[1280,128]{1,0:T(8,128)(2,1)S(1)}, bf16[1280,128]{1,0:T(8,128)(2,1)S(1)}, u32[]{:S(2)}, u32[]{:S(2)}) collective-permute-start(bf16[1280,128]{1,0:T(8,128)(2,1)S(1)} %collective-permute-done.1), channel_id=1, source_target_pairs={{8,0},{12,4},{16,24},{20,28},{9,1},{13,5},{17,25},{21,29},{10,2},{... | collective-permute-start | bytes 983048 | tf_op jit(solution)/shard_map/ppermute | solution.py:311
  22.7 10.9 %collective-permute-start.4 = (bf16[1280,128]{1,0:T(8,128)(2,1)S(1)}, bf16[1280,128]{1,0:T(8,128)(2,1)}, u32[]{:S(2)}, u32[]{:S(2)}) collective-permute-start(bf16[1280,128]{1,0:T(8,128)(2,1)S(1)} %collective-permute-done.refs_1_), channel_id=1, source_target_pairs={{8,16},{12,20},{16,8},{20,12},{9,17},{13,21},{17,9},{21,13},{10,18... | collective-permute-start | bytes 983048 | tf_op jit(solution)/shard_map/ppermute | solution.py:311
  24.1 9.5 %collective-permute-start.5 = (bf16[1280,128]{1,0:T(8,128)(2,1)S(1)}, bf16[1280,128]{1,0:T(8,128)(2,1)S(1)}, u32[]{:S(2)}, u32[]{:S(2)}) collective-permute-start(bf16[1280,128]{1,0:T(8,128)(2,1)S(1)} %collective-permute-done.refs_1_), channel_id=1, source_target_pairs={{0,4},{4,0},{8,12},{12,8},{16,20},{20,16},{24,28},{28,24},{1,5},{5... | collective-permute-start | bytes 983048 | tf_op jit(solution)/shard_map/ppermute | solution.py:314
  24.7 18.2 %all-to-all-start.1 = ((bf16[4,32,1024]{2,1,0:T(8,128)(2,1)}), bf16[4,32,1024]{2,1,0:T(8,128)(2,1)S(1)}, u32[]{:S(2)}, u32[]{:S(2)}) async-start(bf16[4,32,1024]{2,1,0:T(8,128)(2,1)} %all-to-all-done), calls=%async_computation.1 | async-start | bytes 524288 | tf_op jit(solution)/shard_map/all_to_all | solution.py:332
  33.6 24.0 %copy-start.7 = (s32[2,4]{1,0:T(2,128)S(1)}, s32[2,4]{1,0:T(2,128)}, u32[]{:S(2)}) copy-start(s32[2,4]{1,0:T(2,128)} %param.22) | copy-start | bytes 100
  33.6 24.0 %copy-start.5 = (f32[4,4]{1,0:T(4,128)S(1)}, f32[4,4]{1,0:T(4,128)}, u32[]{:S(2)}) copy-start(f32[4,4]{1,0:T(4,128)} %param.24) | copy-start | bytes 196
  33.6 24.8 %copy-start.6 = (f32[4]{0:T(128)S(1)}, f32[4]{0:T(128)}, u32[]{:S(2)}) copy-start(f32[4]{0:T(128)} %param.23) | copy-start | bytes 52
  42.8 11.8 %collective-permute-start.8 = (bf16[1280,128]{1,0:T(8,128)(2,1)}, bf16[1280,128]{1,0:T(8,128)(2,1)S(1)}, u32[]{:S(2)}, u32[]{:S(2)}) collective-permute-start(bf16[1280,128]{1,0:T(8,128)(2,1)} %collective-permute-done.4), channel_id=1, source_target_pairs={{8,0},{12,4},{16,24},{20,28},{9,1},{13,5},{17,25},{21,29},{10,2},{... | collective-permute-start | bytes 983048 | tf_op jit(solution)/shard_map/ppermute | solution.py:311
  45.3 19.8 %collective-permute-start.17 = (bf16[768,768]{1,0:T(8,128)(2,1)}, bf16[768,768]{1,0:T(8,128)(2,1)}, u32[]{:S(2)}, u32[]{:S(2)}) collective-permute-start(bf16[768,768]{1,0:T(8,128)(2,1)} %broadcast_select_fusion), channel_id=1, source_target_pairs={{0,1},{2,3},{4,5},{6,7},{9,8},{11,10},{13,12},{15,14},{16,17},{18,... | collective-permute-start | bytes 3538952 | tf_op jit(solution)/shard_map/ppermute | solution.py:344
  48.3 9.2 %collective-permute-start.7 = (bf16[4,32,1024]{2,1,0:T(8,128)(2,1)S(1)}, bf16[4,32,1024]{2,1,0:T(8,128)(2,1)S(1)}, u32[]{:S(2)}, u32[]{:S(2)}) collective-permute-start(bf16[4,32,1024]{2,1,0:T(8,128)(2,1)S(1)} %all-to-all-done.1.refs_8_), channel_id=1, source_target_pairs={{0,4},{4,0},{8,12},{12,8},{16,20},{20,16},{24,28},{28,24},{1,5},{5... | collective-permute-start | bytes 786440 | tf_op jit(solution)/shard_map/ppermute | solution.py:314
  48.8 9.6 %collective-permute-start.11 = (bf16[4,32,1024]{2,1,0:T(8,128)(2,1)S(1)}, bf16[4,32,1024]{2,1,0:T(8,128)(2,1)S(1)}, u32[]{:S(2)}, u32[]{:S(2)}) collective-permute-start(bf16[4,32,1024]{2,1,0:T(8,128)(2,1)S(1)} %all-to-all-done.1.refs_8_), channel_id=1, source_target_pairs={{0,2},{1,3},{2,0},{3,1},{4,6},{5,7},{6,4},{7,5},{8,10},{9,11},{10,... | collective-permute-start | bytes 786440 | tf_op jit(solution)/shard_map/ppermute | solution.py:342
  49.1 15.5 %collective-permute-start.9 = (bf16[1280,128]{1,0:T(8,128)(2,1)S(1)}, bf16[1280,128]{1,0:T(8,128)(2,1)S(1)}, u32[]{:S(2)}, u32[]{:S(2)}) collective-permute-start(bf16[1280,128]{1,0:T(8,128)(2,1)S(1)} %broadcast_select_fusion.3.refs_2_), channel_id=1, source_target_pairs={{0,4},{4,0},{8,12},{12,8},{16,20},{20,16},{24,28},{28,24},{1,5},{5... | collective-permute-start | bytes 983048 | tf_op jit(solution)/shard_map/ppermute | solution.py:314
  57.5 7.0 %collective-permute-start.14 = (bf16[4,32,1024]{2,1,0:T(8,128)(2,1)S(1)}, bf16[4,32,1024]{2,1,0:T(8,128)(2,1)S(1)}, u32[]{:S(2)}, u32[]{:S(2)}) collective-permute-start(bf16[4,32,1024]{2,1,0:T(8,128)(2,1)S(1)} %collective-permute-done.7.refs_12_), channel_id=1, source_target_pairs={{0,2},{1,3},{2,0},{3,1},{4,6},{5,7},{6,4},{7,5},{8,10},{9,11},{10,... | collective-permute-start | bytes 786440 | tf_op jit(solution)/shard_map/ppermute | solution.py:348
  57.8 11.1 %collective-permute-start.10 = (bf16[1280,128]{1,0:T(8,128)(2,1)S(1)}, bf16[1280,128]{1,0:T(8,128)(2,1)S(1)}, u32[]{:S(2)}, u32[]{:S(2)}) collective-permute-start(bf16[1280,128]{1,0:T(8,128)(2,1)S(1)} %broadcast_select_fusion.2.refs_3_), channel_id=1, source_target_pairs={{0,4},{4,0},{8,12},{12,8},{16,20},{20,16},{24,28},{28,24},{1,5},{5... | collective-permute-start | bytes 983048 | tf_op jit(solution)/shard_map/ppermute | solution.py:314
  58.4 10.6 %copy-start.1 = (bf16[1280,128]{1,0:T(8,128)(2,1)S(1)}, bf16[1280,128]{1,0:T(8,128)(2,1)}, u32[]{:S(2)}) copy-start(bf16[1280,128]{1,0:T(8,128)(2,1)} %get-tuple-element.20.refs_0_) | copy-start | bytes 983044
  58.4 9.1 %collective-permute-start.13 = (bf16[4,32,1024]{2,1,0:T(8,128)(2,1)S(1)}, bf16[4,32,1024]{2,1,0:T(8,128)(2,1)S(1)}, u32[]{:S(2)}, u32[]{:S(2)}) collective-permute-start(bf16[4,32,1024]{2,1,0:T(8,128)(2,1)S(1)} %collective-permute-done.11.refs_9_), channel_id=1, source_target_pairs={{0,1},{1,0},{2,3},{3,2},{4,5},{5,4},{6,7},{7,6},{8,9},{9,8},{10,11... | collective-permute-start | bytes 786440 | tf_op jit(solution)/shard_map/ppermute | solution.py:352
  64.6 3.0 %collective-permute-start.15 = (bf16[4,32,1024]{2,1,0:T(8,128)(2,1)S(1)}, bf16[4,32,1024]{2,1,0:T(8,128)(2,1)S(1)}, u32[]{:S(2)}, u32[]{:S(2)}) collective-permute-start(bf16[4,32,1024]{2,1,0:T(8,128)(2,1)S(1)} %collective-permute-done.7.refs_12_), channel_id=1, source_target_pairs={{0,1},{1,0},{2,3},{3,2},{4,5},{5,4},{6,7},{7,6},{8,9},{9,8},{10,11... | collective-permute-start | bytes 786440 | tf_op jit(solution)/shard_map/ppermute | solution.py:352
  64.6 3.0 %collective-permute-start.12 = (bf16[4,32,1024]{2,1,0:T(8,128)(2,1)S(1)}, bf16[4,32,1024]{2,1,0:T(8,128)(2,1)S(1)}, u32[]{:S(2)}, u32[]{:S(2)}) collective-permute-start(bf16[4,32,1024]{2,1,0:T(8,128)(2,1)S(1)} %all-to-all-done.1.refs_8_), channel_id=1, source_target_pairs={{0,1},{1,0},{2,3},{3,2},{4,5},{5,4},{6,7},{7,6},{8,9},{9,8},{10,11... | collective-permute-start | bytes 786440 | tf_op jit(solution)/shard_map/ppermute | solution.py:352
  65.1 3.9 %collective-permute-start.16 = (bf16[4,32,1024]{2,1,0:T(8,128)(2,1)S(1)}, bf16[4,32,1024]{2,1,0:T(8,128)(2,1)S(1)}, u32[]{:S(2)}, u32[]{:S(2)}) collective-permute-start(bf16[4,32,1024]{2,1,0:T(8,128)(2,1)S(1)} %collective-permute-done.14.refs_13_), channel_id=1, source_target_pairs={{0,1},{1,0},{2,3},{3,2},{4,5},{5,4},{6,7},{7,6},{8,9},{9,8},{10,11... | collective-permute-start | bytes 786440 | tf_op jit(solution)/shard_map/ppermute | solution.py:352
  87.0 1.0 copy-start
  88.0 0.7 copy-start.2
  88.7 11.0 %all-to-all-start.2 = ((f32[32,1,256]{2,1,0:T(1,128)}), f32[32,1,256]{2,1,0:T(1,128)S(1)}, u32[]{:S(2)}, u32[]{:S(2)}) async-start(f32[32,1,256]{2,1,0:T(1,128)} %get-tuple-element.35), calls=%async_computation.2 | async-start | bytes 65536 | tf_op jit(solution)/shard_map/all_to_all | solution.py:406
  99.7 0.6 copy-start.4

commit v6 on v5

--- a/solution.py
+++ b/solution.py
@@ -156,7 +156,7 @@
         + [pltpu.VMEM(packed.shape, BF)]
         + [pltpu.VMEM((in_width, c), F32) for c in cols]
         + [pltpu.SemaphoreType.DMA((n,)) for n in (2 * quarters, 3, count, 2)],
-        compiler_params=pltpu.CompilerParams(vmem_limit_bytes=48 * 2**20),
+        compiler_params=pltpu.CompilerParams(vmem_limit_bytes=54 * 2**20),
         name="tile",
     )(sc, where, *parts, *blocks, pa_kv, pa_up, packed)
 
@@ -334,10 +334,10 @@
     cross_b = along_z(near, middle)
     near_y = across_y(near)
     prev_x = lax.ppermute(prev_low, both, sends_x)
-    strip, far_a, cross_b, near_y, prev_x = phase((strip, far_a, cross_b, near_y, prev_x))
+    far_a_y = across_y(far_a)
+    strip, far_a_y, cross_b, near_y, prev_x = phase((strip, far_a_y, cross_b, near_y, prev_x))
 
     strip_y = across_y(strip)
-    far_a_y = across_y(far_a)
     far_b = jnp.where(inner, cross_b, along_z(cross_b, outward))
     strip_x = lax.ppermute(strip, "own", own_swap(2))
     prev_low = jnp.where(x == z // 2, prev_low, prev_x)

time: 104 us -> 104 us (level)
  waiting for transfers between devices: 37.2 us -> 32.8 us
  starting transfers between devices: 33.5 us -> 36.9 us
  Pallas kernels: 22.7 us -> 24.4 us
  other arithmetic: 5.49 us -> 4.17 us
    ppermute x5, waiting for transfers between devices: 10.3 us -> 1.31 us  [across_y(): return lax.ppermute(value, 'dp', dp_swap(1))]
    ppermute x1, waiting for transfers between devices: 0.01 us -> 4.58 us  [gather_fast(): strip_xy = lax.ppermute(strip_y, 'own', own_swap(2))]
    all_to_all x1, starting transfers between devices: 3.75 us -> 7.21 us  [shards(): sums = lax.all_to_all(sent, ('dp', 'own'), 0, 0, tiled=True)]
    pallas_call x1, Pallas kernels: 18 us -> 19.6 us  [tile(): pl.pallas_call(functools.partial(tile_kernel, count, quarters, in_width,...]
    select_n x1, other arithmetic: 2.41 us -> 1.13 us  [gather_fast(): prev_low = jnp.where(own & 1 == z & 1, prev_low, prev_core)]
    ppermute x1, starting transfers between devices: 0.28 us -> 1.35 us  [gather_fast(): strip_x = lax.ppermute(strip, 'own', own_swap(2))]
    unnamed x16 -> x38, local copies, waits for them, and re-layouts: 2.37 us -> 2.59 us
  transfers between devices with their start and end apart: 21 -> 21, of which waited for: 8 -> 8; matrix products, arithmetic and copies ran while one was open for 6% -> 5% of each run, Pallas kernels for 0% -> 0%
where the time goes in v6:
time: 104 us; the launch traced here: 103 us
  starting transfers between devices  36.9 us (35%)
  waiting for transfers between devices  32.8 us (32%)
  Pallas kernels  24.4 us (23%)
  other arithmetic  4.17 us (4%)
  local copies, waits for them, and re-layouts  3.41 us (3%)
  between operations  1.59 us (2%)
    pallas_call x1, Pallas kernels, tile(): pl.pallas_call(functools.partial(tile_kernel, count, quarters, in_width,...  19.6 us
    all_to_all x1, waiting for transfers between devices, gather_fast(): lax.all_to_all(split, 'dp', 0, 0, tiled=True, axis_index_groups=z_lines)  8.19 us
    ppermute x5, waiting for transfers between devices, along_z(): lax.ppermute(value, 'dp', [(2 * s + y, 2 * t + y) for s, t in pairs for y...  7.73 us
    ppermute x5, starting transfers between devices, along_z(): lax.ppermute(value, 'dp', [(2 * s + y, 2 * t + y) for s, t in pairs for y...  7.65 us
    all_to_all x1, starting transfers between devices, shards(): sums = lax.all_to_all(sent, ('dp', 'own'), 0, 0, tiled=True)  7.21 us
    all_to_all x1, starting transfers between devices, gather_fast(): lax.all_to_all(split, 'dp', 0, 0, tiled=True, axis_index_groups=z_lines)  6.79 us
    all_to_all x1, waiting for transfers between devices, shards(): sums = lax.all_to_all(sent, ('dp', 'own'), 0, 0, tiled=True)  6.6 us
    ppermute x1, waiting for transfers between devices, gather_fast(): strip_xy = lax.ppermute(strip_y, 'own', own_swap(2))  4.58 us
  transfers between devices with their start and end apart: 21, of which 8 were waited for; matrix products, arithmetic and copies ran while one was open for 5% of the time, Pallas kernels for 0%

profile of v6, /device:TPU:0, one launch (start us, length us, event | category | flops | bytes accessed | tf_op | source)
XLA Modules:
  0.0 103.2 jit_solution(2282650747076469209)
XLA Ops:
  0.6 2.0 %turn.1 = (bf16[1280,128]{1,0:T(8,128)(2,1)}, bf16[128,1024]{1,0:T(8,128)(2,1)}) custom-call(bf16[128,640]{1,0:T(8,128)(2,1)} %kv_ref.1, bf16[128,640]{1,0:T(8,128)(2,1)} %up_ref.1, bf16[128,256]{1,0:T(8,128)(2,1)} %g_kv.1, bf16[128,768]{1,0:T(8,128)(2,1)} %g_up.1), custom_call_target="tpu_custom_call" | custom-call | tf_op jit(solution)/shard_map/turn/pallas_call | solution.py:182
  2.7 3.0 %collective-permute-start = (bf16[1280,128]{1,0:T(8,128)(2,1)}, bf16[1280,128]{1,0:T(8,128)(2,1)S(1)}, u32[]{:S(2)}, u32[]{:S(2)}) collective-permute-start(bf16[1280,128]{1,0:T(8,128)(2,1)} %get-tuple-element.20.refs_0_), channel_id=1, source_target_pairs={{0,8},{4,12},{8,0},{12,4},{16,24},{20,28},{24,16},{28,20},{1,9},{5... | collective-permute-start | bytes 983048 | tf_op jit(solution)/shard_map/ppermute | solution.py:311
  5.7 0.7 collective-permute-start.1
  6.4 1.6 %collective-permute-start.2 = (bf16[1280,128]{1,0:T(8,128)(2,1)}, bf16[1280,128]{1,0:T(8,128)(2,1)}, u32[]{:S(2)}, u32[]{:S(2)}) collective-permute-start(bf16[1280,128]{1,0:T(8,128)(2,1)} %get-tuple-element.20.refs_0_), channel_id=1, source_target_pairs={{0,4},{4,0},{8,12},{12,8},{16,20},{20,16},{24,28},{28,24},{1,5},{5... | collective-permute-start | bytes 983048 | tf_op jit(solution)/shard_map/ppermute | solution.py:314
  7.9 4.0 %all-to-all-start = ((bf16[4,32,1024]{2,1,0:T(8,128)(2,1)}), bf16[4,32,1024]{2,1,0:T(8,128)(2,1)}, u32[]{:S(2)}, u32[]{:S(2)}) async-start(bf16[4,32,1024]{2,1,0:T(8,128)(2,1)} %bitcast.17), calls=%async_computation | async-start | bytes 524288 | tf_op jit(solution)/shard_map/all_to_all | solution.py:327
  12.0 1.8 %convert_bitcast_fusion = bf16[768,768]{1,0:T(8,128)(2,1)S(1)} fusion(f32[1,768,768]{2,1,0:T(8,128)} %param.21), kind=kLoop, calls=%fused_computation | loop fusion | flops 589824 | bytes 3538944 | tf_op jit(solution)/shard_map/convert_element_type | solution.py:384
  13.9 4.2 %all-to-all-done = bf16[4,32,1024]{2,1,0:T(8,128)(2,1)} async-done(((bf16[4,32,1024]{2,1,0:T(8,128)(2,1)}), bf16[4,32,1024]{2,1,0:T(8,128)(2,1)}, u32[]{:S(2)}, u32[]{:S(2)}) %all-to-all-start) | async-done | bytes 262176 | tf_op jit(solution)/shard_map/all_to_all | solution.py:327
  18.1 2.3 %collective-permute-start.7 = (bf16[768,768]{1,0:T(8,128)(2,1)S(1)}, bf16[768,768]{1,0:T(8,128)(2,1)S(1)}, u32[]{:S(2)}, u32[]{:S(2)}) collective-permute-start(bf16[768,768]{1,0:T(8,128)(2,1)S(1)} %bitcast_dynamic-update-slice_fusion), channel_id=1, source_target_pairs={{0,2},{4,6},{9,11},{13,15},{18,16},{22,20},{27,25},{31,29}} | collective-permute-start | bytes 3538952 | tf_op jit(solution)/shard_map/ppermute | solution.py:336
  20.5 1.3 %collective-permute-start.3 = (bf16[1280,128]{1,0:T(8,128)(2,1)S(1)}, bf16[1280,128]{1,0:T(8,128)(2,1)}, u32[]{:S(2)}, u32[]{:S(2)}) collective-permute-start(bf16[1280,128]{1,0:T(8,128)(2,1)S(1)} %collective-permute-done.1), channel_id=1, source_target_pairs={{8,0},{12,4},{16,24},{20,28},{9,1},{13,5},{17,25},{21,29},{10,2},{... | collective-permute-start | bytes 983048 | tf_op jit(solution)/shard_map/ppermute | solution.py:311
  21.8 1.4 %collective-permute-start.5 = (bf16[1280,128]{1,0:T(8,128)(2,1)S(1)}, bf16[1280,128]{1,0:T(8,128)(2,1)}, u32[]{:S(2)}, u32[]{:S(2)}) collective-permute-start(bf16[1280,128]{1,0:T(8,128)(2,1)S(1)} %collective-permute-done.refs_1_), channel_id=1, source_target_pairs={{8,16},{12,20},{16,8},{20,12},{9,17},{13,21},{17,9},{21,13},{10,18... | collective-permute-start | bytes 983048 | tf_op jit(solution)/shard_map/ppermute | solution.py:311
  23.2 0.5 collective-permute-start.6
  23.7 6.8 %all-to-all-start.1 = ((bf16[4,32,1024]{2,1,0:T(8,128)(2,1)}), bf16[4,32,1024]{2,1,0:T(8,128)(2,1)S(1)}, u32[]{:S(2)}, u32[]{:S(2)}) async-start(bf16[4,32,1024]{2,1,0:T(8,128)(2,1)} %all-to-all-done), calls=%async_computation.1 | async-start | bytes 524288 | tf_op jit(solution)/shard_map/all_to_all | solution.py:332
  30.5 2.2 %collective-permute-done.3 = bf16[1280,128]{1,0:T(8,128)(2,1)} collective-permute-done((bf16[1280,128]{1,0:T(8,128)(2,1)S(1)}, bf16[1280,128]{1,0:T(8,128)(2,1)}, u32[]{:S(2)}, u32[]{:S(2)}) %collective-permute-start.3) | collective-permute-done | bytes 327712 | tf_op jit(solution)/shard_map/ppermute | solution.py:311
  32.7 1.0 broadcast_select_fusion.3.refs_2_
  33.7 0.6 collective-permute-start.4
  34.3 8.2 %all-to-all-done.1.refs_8_ = bf16[4,32,1024]{2,1,0:T(8,128)(2,1)S(1)} async-done(((bf16[4,32,1024]{2,1,0:T(8,128)(2,1)}), bf16[4,32,1024]{2,1,0:T(8,128)(2,1)S(1)}, u32[]{:S(2)}, u32[]{:S(2)}) %all-to-all-start.1) | async-done | bytes 262176 | tf_op jit(solution)/shard_map/all_to_all | solution.py:332
  42.5 1.3 %collective-permute-done.4.refs_6_ = bf16[1280,128]{1,0:T(8,128)(2,1)} collective-permute-done((bf16[1280,128]{1,0:T(8,128)(2,1)S(1)}, bf16[1280,128]{1,0:T(8,128)(2,1)}, u32[]{:S(2)}, u32[]{:S(2)}) %collective-permute-start.4) | collective-permute-done | bytes 327712 | tf_op jit(solution)/shard_map/ppermute | solution.py:314
  43.8 1.0 %copy-done.2 = bf16[768,768]{1,0:T(8,128)(2,1)} copy-done((bf16[768,768]{1,0:T(8,128)(2,1)}, bf16[768,768]{1,0:T(8,128)(2,1)S(1)}, u32[]{:S(2)}) %copy-start.2) | copy-done | bytes 1179672
  44.9 1.3 %collective-permute-start.9 = (bf16[1280,128]{1,0:T(8,128)(2,1)}, bf16[1280,128]{1,0:T(8,128)(2,1)S(1)}, u32[]{:S(2)}, u32[]{:S(2)}) collective-permute-start(bf16[1280,128]{1,0:T(8,128)(2,1)} %collective-permute-done.5), channel_id=1, source_target_pairs={{8,0},{12,4},{16,24},{20,28},{9,1},{13,5},{17,25},{21,29},{10,2},{... | collective-permute-start | bytes 983048 | tf_op jit(solution)/shard_map/ppermute | solution.py:311
  46.3 2.4 %collective-permute-start.17 = (bf16[768,768]{1,0:T(8,128)(2,1)S(1)}, bf16[768,768]{1,0:T(8,128)(2,1)}, u32[]{:S(2)}, u32[]{:S(2)}) collective-permute-start(bf16[768,768]{1,0:T(8,128)(2,1)S(1)} %broadcast_select_fusion), channel_id=1, source_target_pairs={{0,1},{2,3},{4,5},{6,7},{9,8},{11,10},{13,12},{15,14},{16,17},{18,... | collective-permute-start | bytes 3538952 | tf_op jit(solution)/shard_map/ppermute | solution.py:344
  48.7 0.5 collective-permute-start.8
  49.2 1.3 %collective-permute-start.11 = (bf16[4,32,1024]{2,1,0:T(8,128)(2,1)S(1)}, bf16[4,32,1024]{2,1,0:T(8,128)(2,1)S(1)}, u32[]{:S(2)}, u32[]{:S(2)}) collective-permute-start(bf16[4,32,1024]{2,1,0:T(8,128)(2,1)S(1)} %all-to-all-done.1.refs_8_), channel_id=1, source_target_pairs={{0,2},{1,3},{2,0},{3,1},{4,6},{5,7},{6,4},{7,5},{8,10},{9,11},{10,... | collective-permute-start | bytes 786440 | tf_op jit(solution)/shard_map/ppermute | solution.py:342
  50.6 5.5 %collective-permute-done.9 = bf16[1280,128]{1,0:T(8,128)(2,1)S(1)} collective-permute-done((bf16[1280,128]{1,0:T(8,128)(2,1)}, bf16[1280,128]{1,0:T(8,128)(2,1)S(1)}, u32[]{:S(2)}, u32[]{:S(2)}) %collective-permute-start.9) | collective-permute-done | bytes 327712 | tf_op jit(solution)/shard_map/ppermute | solution.py:311
  56.7 0.6 collective-permute-start.10
  57.3 0.6 stack.10.sc
  58.4 4.6 %collective-permute-done.14.refs_13_ = bf16[4,32,1024]{2,1,0:T(8,128)(2,1)S(1)} collective-permute-done((bf16[4,32,1024]{2,1,0:T(8,128)(2,1)S(1)}, bf16[4,32,1024]{2,1,0:T(8,128)(2,1)S(1)}, u32[]{:S(2)}, u32[]{:S(2)}) %collective-permute-start.14) | collective-permute-done | bytes 262176 | tf_op jit(solution)/shard_map/ppermute | solution.py:348
  63.5 1.1 %broadcast_select_fusion.1.refs_18_ = bf16[768,768]{1,0:T(8,128)(2,1)} fusion(bf16[768,768]{1,0:T(8,128)(2,1)S(1)} %broadcast_select_fusion, bf16[768,768]{1,0:T(8,128)(2,1)} %collective-permute-done.17, pred[]{:T(512)S(6)} %eq.35), kind=kLoop, calls=%fused_computation.2 | loop fusion | flops 589824 | bytes 3538945 | tf_op jit(solution)/shard_map/jit(_where)/select_n | solution.py:349
  65.8 19.6 %tile.1 = (f32[640,128]{1,0:T(8,128)}, f32[640,384]{1,0:T(8,128)}, f32[32,1,256]{2,1,0:T(1,128)}) custom-call(f32[5,4]{1,0:T(8,128)} %stack.10.sc, s32[1]{0:T(128)} %bitcast.2.where_ref, bf16[1280,128]{1,0:T(8,128)(2,1)} %get-tuple-element.20.refs_0_, bf16[1280,128]{1,0:T(8,128)(2,1)} %copy-done.4, bf16[1280,128]{1,0:T(8,128)(2,1)} %copy-done, ...), custom_call_target="tpu_custom_call" | custom-call | tf_op jit(solution)/shard_map/tile/pallas_call | solution.py:136
  85.4 7.2 %all-to-all-start.2 = ((f32[32,1,256]{2,1,0:T(1,128)}), f32[32,1,256]{2,1,0:T(1,128)S(1)}, u32[]{:S(2)}, u32[]{:S(2)}) async-start(f32[32,1,256]{2,1,0:T(1,128)} %get-tuple-element.35), calls=%async_computation.2 | async-start | bytes 65536 | tf_op jit(solution)/shard_map/all_to_all | solution.py:406
  93.2 6.6 %all-to-all-done.2.sums_any = f32[32,1,256]{2,1,0:T(1,128)S(1)} async-done(((f32[32,1,256]{2,1,0:T(1,128)}), f32[32,1,256]{2,1,0:T(1,128)S(1)}, u32[]{:S(2)}, u32[]{:S(2)}) %all-to-all-start.2) | async-done | bytes 32800 | tf_op jit(solution)/shard_map/all_to_all | solution.py:406
  99.8 0.6 copy-done.15
  100.4 2.8 %update.1 = (f32[640,128]{1,0:T(8,128)}, f32[640,384]{1,0:T(8,128)}) custom-call(f32[1]{0:T(128)} %bitcast.14.step_ref, f32[32,1,256]{2,1,0:T(1,128)} %copy-done.15, f32[640,128]{1,0:T(8,128)} %get-tuple-element.36.p_kv, f32[640,384]{1,0:T(8,128)} %get-tuple-element.37.p_up, f32[640,128]{1,0:T(8,128)} %w_kv.1, f32[640,384]{1,0:T(8,128)} %w_up.1), custom_call_target="tpu_custom_call" | custom-call | tf_op jit(solution)/shard_map/update/pallas_call | solution.py:226
  (62 shorter events, 2.9 us)
Async XLA Ops:
  2.7 15.4 %collective-permute-start = (bf16[1280,128]{1,0:T(8,128)(2,1)}, bf16[1280,128]{1,0:T(8,128)(2,1)S(1)}, u32[]{:S(2)}, u32[]{:S(2)}) collective-permute-start(bf16[1280,128]{1,0:T(8,128)(2,1)} %get-tuple-element.20.refs_0_), channel_id=1, source_target_pairs={{0,8},{4,12},{8,0},{12,4},{16,24},{20,28},{24,16},{28,20},{1,9},{5... | collective-permute-start | bytes 983048 | tf_op jit(solution)/shard_map/ppermute | solution.py:311
  5.7 12.4 %collective-permute-start.1 = (bf16[1280,128]{1,0:T(8,128)(2,1)}, bf16[1280,128]{1,0:T(8,128)(2,1)S(1)}, u32[]{:S(2)}, u32[]{:S(2)}) collective-permute-start(bf16[1280,128]{1,0:T(8,128)(2,1)} %get-tuple-element.20.refs_0_), channel_id=1, source_target_pairs={{8,16},{12,20},{16,8},{20,12},{9,17},{13,21},{17,9},{21,13},{10,18... | collective-permute-start | bytes 983048 | tf_op jit(solution)/shard_map/ppermute | solution.py:311
  6.4 11.8 %collective-permute-start.2 = (bf16[1280,128]{1,0:T(8,128)(2,1)}, bf16[1280,128]{1,0:T(8,128)(2,1)}, u32[]{:S(2)}, u32[]{:S(2)}) collective-permute-start(bf16[1280,128]{1,0:T(8,128)(2,1)} %get-tuple-element.20.refs_0_), channel_id=1, source_target_pairs={{0,4},{4,0},{8,12},{12,8},{16,20},{20,16},{24,28},{28,24},{1,5},{5... | collective-permute-start | bytes 983048 | tf_op jit(solution)/shard_map/ppermute | solution.py:314
  7.9 10.1 %all-to-all-start = ((bf16[4,32,1024]{2,1,0:T(8,128)(2,1)}), bf16[4,32,1024]{2,1,0:T(8,128)(2,1)}, u32[]{:S(2)}, u32[]{:S(2)}) async-start(bf16[4,32,1024]{2,1,0:T(8,128)(2,1)} %bitcast.17), calls=%async_computation | async-start | bytes 524288 | tf_op jit(solution)/shard_map/all_to_all | solution.py:327
  12.0 1.8 %copy-start.14 = (f32[1,256,256]{2,1,0:T(8,128)S(1)}, f32[1,256,256]{2,1,0:T(8,128)}, u32[]{:S(2)}) copy-start(f32[1,256,256]{2,1,0:T(8,128)} %param.19) | copy-start | bytes 786436
  18.1 28.2 %copy-start.4 = (bf16[1280,128]{1,0:T(8,128)(2,1)}, bf16[1280,128]{1,0:T(8,128)(2,1)S(1)}, u32[]{:S(2)}) copy-start(bf16[1280,128]{1,0:T(8,128)(2,1)S(1)} %collective-permute-done.refs_1_) | copy-start | bytes 983044
  18.1 12.4 %copy-start.6 = (bf16[1280,128]{1,0:T(8,128)(2,1)}, bf16[1280,128]{1,0:T(8,128)(2,1)S(1)}, u32[]{:S(2)}) copy-start(bf16[1280,128]{1,0:T(8,128)(2,1)S(1)} %collective-permute-done.1) | copy-start | bytes 983044
  18.1 25.7 %collective-permute-start.7 = (bf16[768,768]{1,0:T(8,128)(2,1)S(1)}, bf16[768,768]{1,0:T(8,128)(2,1)S(1)}, u32[]{:S(2)}, u32[]{:S(2)}) collective-permute-start(bf16[768,768]{1,0:T(8,128)(2,1)S(1)} %bitcast_dynamic-update-slice_fusion), channel_id=1, source_target_pairs={{0,2},{4,6},{9,11},{13,15},{18,16},{22,20},{27,25},{31,29}} | collective-permute-start | bytes 3538952 | tf_op jit(solution)/shard_map/ppermute | solution.py:336
  20.5 12.3 %collective-permute-start.3 = (bf16[1280,128]{1,0:T(8,128)(2,1)S(1)}, bf16[1280,128]{1,0:T(8,128)(2,1)}, u32[]{:S(2)}, u32[]{:S(2)}) collective-permute-start(bf16[1280,128]{1,0:T(8,128)(2,1)S(1)} %collective-permute-done.1), channel_id=1, source_target_pairs={{8,0},{12,4},{16,24},{20,28},{9,1},{13,5},{17,25},{21,29},{10,2},{... | collective-permute-start | bytes 983048 | tf_op jit(solution)/shard_map/ppermute | solution.py:311
  21.8 12.5 %collective-permute-start.5 = (bf16[1280,128]{1,0:T(8,128)(2,1)S(1)}, bf16[1280,128]{1,0:T(8,128)(2,1)}, u32[]{:S(2)}, u32[]{:S(2)}) collective-permute-start(bf16[1280,128]{1,0:T(8,128)(2,1)S(1)} %collective-permute-done.refs_1_), channel_id=1, source_target_pairs={{8,16},{12,20},{16,8},{20,12},{9,17},{13,21},{17,9},{21,13},{10,18... | collective-permute-start | bytes 983048 | tf_op jit(solution)/shard_map/ppermute | solution.py:311
  23.2 11.2 %collective-permute-start.6 = (bf16[1280,128]{1,0:T(8,128)(2,1)S(1)}, bf16[1280,128]{1,0:T(8,128)(2,1)}, u32[]{:S(2)}, u32[]{:S(2)}) collective-permute-start(bf16[1280,128]{1,0:T(8,128)(2,1)S(1)} %collective-permute-done.refs_1_), channel_id=1, source_target_pairs={{0,4},{4,0},{8,12},{12,8},{16,20},{20,16},{24,28},{28,24},{1,5},{5... | collective-permute-start | bytes 983048 | tf_op jit(solution)/shard_map/ppermute | solution.py:314
  23.7 18.8 %all-to-all-start.1 = ((bf16[4,32,1024]{2,1,0:T(8,128)(2,1)}), bf16[4,32,1024]{2,1,0:T(8,128)(2,1)S(1)}, u32[]{:S(2)}, u32[]{:S(2)}) async-start(bf16[4,32,1024]{2,1,0:T(8,128)(2,1)} %all-to-all-done), calls=%async_computation.1 | async-start | bytes 524288 | tf_op jit(solution)/shard_map/all_to_all | solution.py:332
  33.7 12.6 %copy-start = (bf16[1280,128]{1,0:T(8,128)(2,1)}, bf16[1280,128]{1,0:T(8,128)(2,1)S(1)}, u32[]{:S(2)}) copy-start(bf16[1280,128]{1,0:T(8,128)(2,1)S(1)} %broadcast_select_fusion.3.refs_2_) | copy-start | bytes 983044
  33.7 10.1 %collective-permute-start.4 = (bf16[1280,128]{1,0:T(8,128)(2,1)S(1)}, bf16[1280,128]{1,0:T(8,128)(2,1)}, u32[]{:S(2)}, u32[]{:S(2)}) collective-permute-start(bf16[1280,128]{1,0:T(8,128)(2,1)S(1)} %broadcast_select_fusion.3.refs_2_), channel_id=1, source_target_pairs={{0,4},{4,0},{8,12},{12,8},{16,20},{20,16},{24,28},{28,24},{1,5},{5... | collective-permute-start | bytes 983048 | tf_op jit(solution)/shard_map/ppermute | solution.py:314
  34.3 22.1 %copy-start.18 = (s32[2,4]{1,0:T(2,128)S(1)}, s32[2,4]{1,0:T(2,128)}, u32[]{:S(2)}) copy-start(s32[2,4]{1,0:T(2,128)} %param.22) | copy-start | bytes 100
  34.3 22.1 %copy-start.16 = (f32[4,4]{1,0:T(4,128)S(1)}, f32[4,4]{1,0:T(4,128)}, u32[]{:S(2)}) copy-start(f32[4,4]{1,0:T(4,128)} %param.24) | copy-start | bytes 196
  34.3 22.9 %copy-start.17 = (f32[4]{0:T(128)S(1)}, f32[4]{0:T(128)}, u32[]{:S(2)}) copy-start(f32[4]{0:T(128)} %param.23) | copy-start | bytes 52
  42.5 22.1 %copy-start.3 = (bf16[4,32,1024]{2,1,0:T(8,128)(2,1)}, bf16[4,32,1024]{2,1,0:T(8,128)(2,1)S(1)}, u32[]{:S(2)}) copy-start(bf16[4,32,1024]{2,1,0:T(8,128)(2,1)S(1)} %all-to-all-done.1.refs_8_) | copy-start | bytes 786436
  44.9 11.2 %collective-permute-start.9 = (bf16[1280,128]{1,0:T(8,128)(2,1)}, bf16[1280,128]{1,0:T(8,128)(2,1)S(1)}, u32[]{:S(2)}, u32[]{:S(2)}) collective-permute-start(bf16[1280,128]{1,0:T(8,128)(2,1)} %collective-permute-done.5), channel_id=1, source_target_pairs={{8,0},{12,4},{16,24},{20,28},{9,1},{13,5},{17,25},{21,29},{10,2},{... | collective-permute-start | bytes 983048 | tf_op jit(solution)/shard_map/ppermute | solution.py:311
  46.3 16.7 %collective-permute-start.17 = (bf16[768,768]{1,0:T(8,128)(2,1)S(1)}, bf16[768,768]{1,0:T(8,128)(2,1)}, u32[]{:S(2)}, u32[]{:S(2)}) collective-permute-start(bf16[768,768]{1,0:T(8,128)(2,1)S(1)} %broadcast_select_fusion), channel_id=1, source_target_pairs={{0,1},{2,3},{4,5},{6,7},{9,8},{11,10},{13,12},{15,14},{16,17},{18,... | collective-permute-start | bytes 3538952 | tf_op jit(solution)/shard_map/ppermute | solution.py:344
  48.7 7.4 %collective-permute-start.8 = (bf16[4,32,1024]{2,1,0:T(8,128)(2,1)S(1)}, bf16[4,32,1024]{2,1,0:T(8,128)(2,1)S(1)}, u32[]{:S(2)}, u32[]{:S(2)}) collective-permute-start(bf16[4,32,1024]{2,1,0:T(8,128)(2,1)S(1)} %all-to-all-done.1.refs_8_), channel_id=1, source_target_pairs={{0,4},{4,0},{8,12},{12,8},{16,20},{20,16},{24,28},{28,24},{1,5},{5... | collective-permute-start | bytes 786440 | tf_op jit(solution)/shard_map/ppermute | solution.py:314
  49.2 8.6 %collective-permute-start.11 = (bf16[4,32,1024]{2,1,0:T(8,128)(2,1)S(1)}, bf16[4,32,1024]{2,1,0:T(8,128)(2,1)S(1)}, u32[]{:S(2)}, u32[]{:S(2)}) collective-permute-start(bf16[4,32,1024]{2,1,0:T(8,128)(2,1)S(1)} %all-to-all-done.1.refs_8_), channel_id=1, source_target_pairs={{0,2},{1,3},{2,0},{3,1},{4,6},{5,7},{6,4},{7,5},{8,10},{9,11},{10,... | collective-permute-start | bytes 786440 | tf_op jit(solution)/shard_map/ppermute | solution.py:342
  56.1 8.5 %copy-start.1 = (bf16[1280,128]{1,0:T(8,128)(2,1)}, bf16[1280,128]{1,0:T(8,128)(2,1)S(1)}, u32[]{:S(2)}) copy-start(bf16[1280,128]{1,0:T(8,128)(2,1)S(1)} %broadcast_select_fusion.2.refs_3_) | copy-start | bytes 983044
  56.1 8.5 %copy-start.7 = (bf16[4,32,1024]{2,1,0:T(8,128)(2,1)}, bf16[4,32,1024]{2,1,0:T(8,128)(2,1)S(1)}, u32[]{:S(2)}) copy-start(bf16[4,32,1024]{2,1,0:T(8,128)(2,1)S(1)} %collective-permute-done.8.refs_12_) | copy-start | bytes 786436
  56.1 6.8 %collective-permute-start.14 = (bf16[4,32,1024]{2,1,0:T(8,128)(2,1)S(1)}, bf16[4,32,1024]{2,1,0:T(8,128)(2,1)S(1)}, u32[]{:S(2)}, u32[]{:S(2)}) collective-permute-start(bf16[4,32,1024]{2,1,0:T(8,128)(2,1)S(1)} %collective-permute-done.8.refs_12_), channel_id=1, source_target_pairs={{0,2},{1,3},{2,0},{3,1},{4,6},{5,7},{6,4},{7,5},{8,10},{9,11},{10,... | collective-permute-start | bytes 786440 | tf_op jit(solution)/shard_map/ppermute | solution.py:348
  56.7 8.0 %collective-permute-start.10 = (bf16[1280,128]{1,0:T(8,128)(2,1)S(1)}, bf16[1280,128]{1,0:T(8,128)(2,1)S(1)}, u32[]{:S(2)}, u32[]{:S(2)}) collective-permute-start(bf16[1280,128]{1,0:T(8,128)(2,1)S(1)} %broadcast_select_fusion.2.refs_3_), channel_id=1, source_target_pairs={{0,4},{4,0},{8,12},{12,8},{16,20},{20,16},{24,28},{28,24},{1,5},{5... | collective-permute-start | bytes 983048 | tf_op jit(solution)/shard_map/ppermute | solution.py:314
  57.9 6.8 %copy-start.8 = (bf16[4,32,1024]{2,1,0:T(8,128)(2,1)}, bf16[4,32,1024]{2,1,0:T(8,128)(2,1)S(1)}, u32[]{:S(2)}) copy-start(bf16[4,32,1024]{2,1,0:T(8,128)(2,1)S(1)} %collective-permute-done.11.refs_9_) | copy-start | bytes 786436
  57.9 6.8 %collective-permute-start.13 = (bf16[4,32,1024]{2,1,0:T(8,128)(2,1)S(1)}, bf16[4,32,1024]{2,1,0:T(8,128)(2,1)S(1)}, u32[]{:S(2)}, u32[]{:S(2)}) collective-permute-start(bf16[4,32,1024]{2,1,0:T(8,128)(2,1)S(1)} %collective-permute-done.11.refs_9_), channel_id=1, source_target_pairs={{0,1},{1,0},{2,3},{3,2},{4,5},{5,4},{6,7},{7,6},{8,9},{9,8},{10,11... | collective-permute-start | bytes 786440 | tf_op jit(solution)/shard_map/ppermute | solution.py:352
  57.9 6.8 %collective-permute-start.15 = (bf16[4,32,1024]{2,1,0:T(8,128)(2,1)S(1)}, bf16[4,32,1024]{2,1,0:T(8,128)(2,1)S(1)}, u32[]{:S(2)}, u32[]{:S(2)}) collective-permute-start(bf16[4,32,1024]{2,1,0:T(8,128)(2,1)S(1)} %collective-permute-done.8.refs_12_), channel_id=1, source_target_pairs={{0,1},{1,0},{2,3},{3,2},{4,5},{5,4},{6,7},{7,6},{8,9},{9,8},{10,11... | collective-permute-start | bytes 786440 | tf_op jit(solution)/shard_map/ppermute | solution.py:352
  63.0 1.7 %collective-permute-start.12 = (bf16[4,32,1024]{2,1,0:T(8,128)(2,1)S(1)}, bf16[4,32,1024]{2,1,0:T(8,128)(2,1)S(1)}, u32[]{:S(2)}, u32[]{:S(2)}) collective-permute-start(bf16[4,32,1024]{2,1,0:T(8,128)(2,1)S(1)} %all-to-all-done.1.refs_8_), channel_id=1, source_target_pairs={{0,1},{1,0},{2,3},{3,2},{4,5},{5,4},{6,7},{7,6},{8,9},{9,8},{10,11... | collective-permute-start | bytes 786440 | tf_op jit(solution)/shard_map/ppermute | solution.py:352
  63.0 1.9 %collective-permute-start.16 = (bf16[4,32,1024]{2,1,0:T(8,128)(2,1)S(1)}, bf16[4,32,1024]{2,1,0:T(8,128)(2,1)S(1)}, u32[]{:S(2)}, u32[]{:S(2)}) collective-permute-start(bf16[4,32,1024]{2,1,0:T(8,128)(2,1)S(1)} %collective-permute-done.14.refs_13_), channel_id=1, source_target_pairs={{0,1},{1,0},{2,3},{3,2},{4,5},{5,4},{6,7},{7,6},{8,9},{9,8},{10,11... | collective-permute-start | bytes 786440 | tf_op jit(solution)/shard_map/ppermute | solution.py:352
  85.4 14.5 %all-to-all-start.2 = ((f32[32,1,256]{2,1,0:T(1,128)}), f32[32,1,256]{2,1,0:T(1,128)S(1)}, u32[]{:S(2)}, u32[]{:S(2)}) async-start(f32[32,1,256]{2,1,0:T(1,128)} %get-tuple-element.35), calls=%async_computation.2 | async-start | bytes 65536 | tf_op jit(solution)/shard_map/all_to_all | solution.py:406
  (8 other events, 7.5 us)
